TPU v7x, 32 devices: a whole 2x2x4 slice. The times are simulated.
32 devices in a mesh: fsdp: 16 (over z, y, x), rep: 2 (over core).
Axes of the slice: x: 2, y: 2, z: 4, core: 2. Of those that a mesh axis runs over, the one named last changes fastest.
Arguments:
- tokens: bfloat16 [32768, 768], P(('fsdp', 'rep')), may hold values from -6 to 6
- cotangent: bfloat16 [32768, 768], P(('fsdp', 'rep')), may hold values from -6 to 6
- segments: int32 [32768], P(('fsdp', 'rep')), may hold values from -1 to 511, as said below
- box_coords: int32 [4, 32768], P(None, ('fsdp', 'rep')), may hold values from 0 to 1023
- w_qkv: float32 [768, 2304], P('fsdp'), may hold values from -0.21875 to 0.21875
- b_qkv: float32 [2304], P('fsdp'), may hold values from -1 to 1
- w_box: float32 [128, 64], P('fsdp'), may hold values from -0.75 to 0.75
- w_out: float32 [768, 768], P('fsdp'), may hold values from -1.25 to 1.25
- b_out: float32 [768], P('fsdp'), may hold values from -1 to 1
- gain_one: float32 [768], P('fsdp'), may hold values from 0.5 to 1.5
- shift_one: float32 [768], P('fsdp'), may hold values from -1 to 1
- w_up: float32 [768, 3072], P('fsdp'), may hold values from -0.21875 to 0.21875
- b_up: float32 [3072], P('fsdp'), may hold values from -1 to 1
- w_down: float32 [3072, 768], P('fsdp'), may hold values from -0.109375 to 0.109375
- b_down: float32 [768], P('fsdp'), may hold values from -1 to 1
- gain_two: float32 [768], P('fsdp'), may hold values from 0.5 to 1.5
- shift_two: float32 [768], P('fsdp'), may hold values from -1 to 1
Outputs:
- layer_out: bfloat16 [32768, 768], P(('fsdp', 'rep'))
- grad_tokens: float32 [32768, 768], P(('fsdp', 'rep'))
- grad_w_qkv: float32 [768, 2304], P('fsdp')
- grad_b_qkv: float32 [2304], P('fsdp')
- grad_w_box: float32 [128, 64], P('fsdp')
- grad_w_out: float32 [768, 768], P('fsdp')
- grad_b_out: float32 [768], P('fsdp')
- grad_gain_one: float32 [768], P('fsdp')
- grad_shift_one: float32 [768], P('fsdp')
- grad_w_up: float32 [768, 3072], P('fsdp')
- grad_b_up: float32 [3072], P('fsdp')
- grad_w_down: float32 [3072, 768], P('fsdp')
- grad_b_down: float32 [768], P('fsdp')
- grad_gain_two: float32 [768], P('fsdp')
- grad_shift_two: float32 [768], P('fsdp')
Inputs may be any that keep to these rules, and one draw needn't show every extreme that they name: `segments`: each slot of 512 consecutive tokens holds whole pages, each page a run of consecutive tokens with the position in the slot of its first token as value, followed by padding at the slot's end valued -1; pages hold up to 512 tokens, heavy-tailed; every fourth slot (slot index divisible by 4) has no padding and ends with a page of one token, the others have 1 to 256 padding tokens.
All inputs are finite; a program needn't handle non-finite values.
Results may differ from a plain program's by a relative error of at most 0.022.
Values may be sent and summed in bfloat16 or wider, within the bound.
A program may use at most 256 MiB of HBM per device.

v0:
```python
import math

import jax
import jax.numpy as jnp
from jax import lax
from jax.sharding import PartitionSpec as P

HEADS = 12
HD = 64
FREQ = 16
SLOT = 512


neg_large = -1e30
eps_norm = 1e-12


def low_cast(value):
    return value.astype(jnp.bfloat16)


def wave_tables(box_coords):
    scaled = box_coords.astype(jnp.float32) * (100.0 / 1024.0)
    frequency = jnp.exp(-math.log(10000.0) * jnp.arange(FREQ, dtype=jnp.float32) / FREQ)
    angles = scaled[:, :, None] * frequency[None, None, :]
    angles = jnp.transpose(angles, (1, 0, 2)).reshape(box_coords.shape[1], 4 * FREQ)
    return (jnp.sin(angles).astype(jnp.bfloat16), jnp.cos(angles).astype(jnp.bfloat16))


def norm_forward(pre_rows, gain, shift):
    center = pre_rows - jnp.mean(pre_rows, axis=-1, keepdims=True)
    invdev = lax.rsqrt(jnp.mean(center * center, axis=-1, keepdims=True) + eps_norm)
    normed = center * invdev
    return (normed * gain + shift, normed, invdev)


def norm_backward(grad_rows, normed, invdev, gain):
    scaled = grad_rows * gain
    first_mean = jnp.mean(scaled, axis=-1, keepdims=True)
    second = jnp.mean(scaled * normed, axis=-1, keepdims=True)
    grad_pre = invdev * (scaled - first_mean - normed * second)
    return (grad_pre, jnp.sum(grad_rows * normed, axis=0), jnp.sum(grad_rows, axis=0))


def gelu_exact(value):
    return jax.nn.gelu(value, approximate=False)


def per_device(
    tokens,
    cotangent,
    segments,
    box_coords,
    w_qkv,
    b_qkv,
    w_box,
    w_out,
    b_out,
    gain_one,
    shift_one,
    w_up,
    b_up,
    w_down,
    b_down,
    gain_two,
    shift_two,
):
    row_count = tokens.shape[0]
    model_width = tokens.shape[1]
    slot_count = row_count // SLOT
    scale_factor = 1.0 / math.sqrt(HD)
    f32 = jnp.float32
    wq_full, bq_full, wb_full, wo_full, bo_full, gone_full, sone_full = (
        lax.all_gather(low_cast(w_qkv), "fsdp", axis=0, tiled=True),
        lax.all_gather(low_cast(b_qkv), "fsdp", axis=0, tiled=True),
        lax.all_gather(low_cast(w_box), "fsdp", axis=0, tiled=True),
        lax.all_gather(low_cast(w_out), "fsdp", axis=0, tiled=True),
        lax.all_gather(low_cast(b_out), "fsdp", axis=0, tiled=True),
        lax.all_gather(low_cast(gain_one), "fsdp", axis=0, tiled=True),
        lax.all_gather(low_cast(shift_one), "fsdp", axis=0, tiled=True),
    )
    sine_table, cosine_table = wave_tables(box_coords)
    wave_half = sine_table.shape[1]
    sine_f = sine_table.astype(f32)[:, None, :]
    cosine_f = cosine_table.astype(f32)[:, None, :]
    mixed_rows = (
        jnp.dot(tokens, wq_full, preferred_element_type=f32) + bq_full.astype(f32)
    ).astype(jnp.bfloat16)
    queries = mixed_rows[:, :model_width].reshape(row_count, HEADS, HD)
    keys_in = mixed_rows[:, model_width : 2 * model_width].reshape(row_count, HEADS, HD)
    values_in = mixed_rows[:, 2 * model_width :].reshape(row_count, HEADS, HD)
    q_box = jnp.einsum("thd,fd->thf", queries, wb_full, preferred_element_type=f32)
    k_box = jnp.einsum("thd,fd->thf", keys_in, wb_full, preferred_element_type=f32)
    q_sin, q_cos = (q_box[..., :wave_half], q_box[..., wave_half:])
    k_sin, k_cos = (k_box[..., :wave_half], k_box[..., wave_half:])
    q_side = jnp.concatenate(
        [q_sin * sine_f + q_cos * cosine_f, q_cos * sine_f - q_sin * cosine_f], axis=-1
    ).astype(jnp.bfloat16)
    k_side = jnp.concatenate(
        [k_sin * cosine_f + k_cos * sine_f, k_cos * cosine_f - k_sin * sine_f], axis=-1
    ).astype(jnp.bfloat16)
    sine_heads = jnp.broadcast_to(sine_table[:, None, :], (row_count, HEADS, wave_half))
    cosine_heads = jnp.broadcast_to(cosine_table[:, None, :], (row_count, HEADS, wave_half))
    q_full = jnp.concatenate([queries, q_side, sine_heads, cosine_heads], axis=-1)
    k_full = jnp.concatenate([keys_in, cosine_heads, sine_heads, k_side], axis=-1)
    q_slots = q_full.reshape(slot_count, SLOT, HEADS, -1)
    k_slots = k_full.reshape(slot_count, SLOT, HEADS, -1)
    v_slots = values_in.reshape(slot_count, SLOT, HEADS, HD)
    segment_rows = segments.reshape(slot_count, SLOT)
    allowed = segment_rows[:, :, None] == segment_rows[:, None, :]

    def head_scores(head_index):
        q_head = lax.dynamic_index_in_dim(q_slots, head_index, 2, keepdims=False)
        k_head = lax.dynamic_index_in_dim(k_slots, head_index, 2, keepdims=False)
        scores = (
            jnp.einsum("nqd,nkd->nqk", q_head, k_head, preferred_element_type=f32) * scale_factor
        )
        return (jnp.where(allowed, scores, neg_large), q_head, k_head)

    def forward_head(head_index):
        scores, q_head, k_head = head_scores(head_index)
        row_max = jnp.max(scores, axis=-1, keepdims=True)
        exp_scores = jnp.exp(scores - row_max)
        row_total = jnp.sum(exp_scores, axis=-1, keepdims=True)
        soft_probs = (exp_scores / row_total).astype(jnp.bfloat16)
        v_head = lax.dynamic_index_in_dim(v_slots, head_index, 2, keepdims=False)
        context_head = jnp.einsum("nqk,nkd->nqd", soft_probs, v_head, preferred_element_type=f32)
        return (context_head, row_max + jnp.log(row_total))

    context_heads, log_totals = lax.map(forward_head, jnp.arange(HEADS))
    context = jnp.moveaxis(context_heads, 0, 2).reshape(row_count, model_width).astype(jnp.bfloat16)
    branch = jnp.dot(context, wo_full, preferred_element_type=f32) + bo_full.astype(f32)
    hidden, normed_one, invdev_one = norm_forward(
        tokens.astype(f32) + branch, gone_full.astype(f32), sone_full.astype(f32)
    )
    hidden_low = hidden.astype(jnp.bfloat16)
    wu_full, bu_full, wd_full, bd_full, gtwo_full, stwo_full = (
        lax.all_gather(low_cast(w_up), "fsdp", axis=0, tiled=True),
        lax.all_gather(low_cast(b_up), "fsdp", axis=0, tiled=True),
        lax.all_gather(low_cast(w_down), "fsdp", axis=0, tiled=True),
        lax.all_gather(low_cast(b_down), "fsdp", axis=0, tiled=True),
        lax.all_gather(low_cast(gain_two), "fsdp", axis=0, tiled=True),
        lax.all_gather(low_cast(shift_two), "fsdp", axis=0, tiled=True),
    )
    up_proj = jnp.dot(hidden_low, wu_full, preferred_element_type=f32) + bu_full.astype(f32)
    act_low = gelu_exact(up_proj).astype(jnp.bfloat16)
    down_proj = jnp.dot(act_low, wd_full, preferred_element_type=f32) + bd_full.astype(f32)
    final, normed_two, invdev_two = norm_forward(
        hidden + down_proj, gtwo_full.astype(f32), stwo_full.astype(f32)
    )
    layer_out = final.astype(jnp.bfloat16)
    wu_back, wd_back, gtwo_back = (
        lax.all_gather(low_cast(w_up), "fsdp", axis=0, tiled=True),
        lax.all_gather(low_cast(w_down), "fsdp", axis=0, tiled=True),
        lax.all_gather(low_cast(gain_two), "fsdp", axis=0, tiled=True),
    )
    grad_pre_two, grad_gain_two, grad_shift_two = norm_backward(
        cotangent.astype(f32), normed_two, invdev_two, gtwo_back.astype(f32)
    )
    grad_down = grad_pre_two.astype(jnp.bfloat16)
    grad_w_down = jnp.einsum("tf,td->fd", act_low, grad_down, preferred_element_type=f32)
    grad_b_down = jnp.sum(grad_down.astype(f32), axis=0)
    grad_act = jnp.einsum("td,fd->tf", grad_down, wd_back, preferred_element_type=f32)
    grad_up = jax.vjp(gelu_exact, up_proj)[1](grad_act)[0].astype(jnp.bfloat16)
    grad_w_up = jnp.einsum("td,tf->df", hidden_low, grad_up, preferred_element_type=f32)
    grad_b_up = jnp.sum(grad_up.astype(f32), axis=0)
    grad_hidden = grad_pre_two + jnp.einsum(
        "tf,df->td", grad_up, wu_back, preferred_element_type=f32
    )
    part_wu, part_bu, part_wd, part_bd, part_gt, part_st = (
        lax.psum_scatter(grad_w_up, "fsdp", scatter_dimension=0, tiled=True),
        lax.psum_scatter(grad_b_up, "fsdp", scatter_dimension=0, tiled=True),
        lax.psum_scatter(grad_w_down, "fsdp", scatter_dimension=0, tiled=True),
        lax.psum_scatter(grad_b_down, "fsdp", scatter_dimension=0, tiled=True),
        lax.psum_scatter(grad_gain_two, "fsdp", scatter_dimension=0, tiled=True),
        lax.psum_scatter(grad_shift_two, "fsdp", scatter_dimension=0, tiled=True),
    )
    part_wu, part_bu, part_wd, part_bd, part_gt, part_st = (
        lax.psum(part_wu.astype(jnp.bfloat16), "rep").astype(jnp.float32),
        lax.psum(part_bu.astype(jnp.bfloat16), "rep").astype(jnp.float32),
        lax.psum(part_wd.astype(jnp.bfloat16), "rep").astype(jnp.float32),
        lax.psum(part_bd.astype(jnp.bfloat16), "rep").astype(jnp.float32),
        lax.psum(part_gt.astype(jnp.bfloat16), "rep").astype(jnp.float32),
        lax.psum(part_st.astype(jnp.bfloat16), "rep").astype(jnp.float32),
    )
    wq_back, wb_back, wo_back, gone_back = (
        lax.all_gather(low_cast(w_qkv), "fsdp", axis=0, tiled=True),
        lax.all_gather(low_cast(w_box), "fsdp", axis=0, tiled=True),
        lax.all_gather(low_cast(w_out), "fsdp", axis=0, tiled=True),
        lax.all_gather(low_cast(gain_one), "fsdp", axis=0, tiled=True),
    )
    grad_pre_one, grad_gain_one, grad_shift_one = norm_backward(
        grad_hidden, normed_one, invdev_one, gone_back.astype(f32)
    )
    grad_branch = grad_pre_one.astype(jnp.bfloat16)
    grad_w_out = jnp.einsum("td,te->de", context, grad_branch, preferred_element_type=f32)
    grad_b_out = jnp.sum(grad_branch.astype(f32), axis=0)
    grad_context = jnp.einsum("te,de->td", grad_branch, wo_back, preferred_element_type=f32)
    grad_context = grad_context.astype(jnp.bfloat16).reshape(slot_count, SLOT, HEADS, HD)

    def backward_head(head_inputs):
        head_index, log_total = head_inputs
        scores, q_head, k_head = head_scores(head_index)
        soft_probs = jnp.exp(scores - log_total)
        grad_ctx_head = lax.dynamic_index_in_dim(grad_context, head_index, 2, keepdims=False)
        v_head = lax.dynamic_index_in_dim(v_slots, head_index, 2, keepdims=False)
        grad_probs = jnp.einsum("nqd,nkd->nqk", grad_ctx_head, v_head, preferred_element_type=f32)
        row_dot = jnp.sum(soft_probs * grad_probs, axis=-1, keepdims=True)
        grad_scores = (soft_probs * (grad_probs - row_dot)).astype(jnp.bfloat16)
        grad_q_head = (
            jnp.einsum("nqk,nkd->nqd", grad_scores, k_head, preferred_element_type=f32)
            * scale_factor
        )
        grad_k_head = (
            jnp.einsum("nqk,nqd->nkd", grad_scores, q_head, preferred_element_type=f32)
            * scale_factor
        )
        grad_v_head = jnp.einsum(
            "nqk,nqd->nkd",
            soft_probs.astype(jnp.bfloat16),
            grad_ctx_head,
            preferred_element_type=f32,
        )
        return (grad_q_head, grad_k_head, grad_v_head)

    gq_heads, gk_heads, gv_heads = lax.map(backward_head, (jnp.arange(HEADS), log_totals))
    grad_qfull = jnp.moveaxis(gq_heads, 0, 2).reshape(row_count, HEADS, -1)
    grad_kfull = jnp.moveaxis(gk_heads, 0, 2).reshape(row_count, HEADS, -1)
    grad_values = jnp.moveaxis(gv_heads, 0, 2).reshape(row_count, model_width)
    side_start = HD
    side_stop = HD + 2 * wave_half
    q_first = grad_qfull[..., side_start : side_start + wave_half]
    q_second = grad_qfull[..., side_start + wave_half : side_stop]
    k_first = grad_kfull[..., side_stop : side_stop + wave_half]
    k_second = grad_kfull[..., side_stop + wave_half : side_stop + 2 * wave_half]
    grad_qbox = jnp.concatenate(
        [q_first * sine_f - q_second * cosine_f, q_first * cosine_f + q_second * sine_f], axis=-1
    ).astype(jnp.bfloat16)
    grad_kbox = jnp.concatenate(
        [k_first * cosine_f - k_second * sine_f, k_first * sine_f + k_second * cosine_f], axis=-1
    ).astype(jnp.bfloat16)
    grad_queries = grad_qfull[..., :HD] + jnp.einsum(
        "thf,fd->thd", grad_qbox, wb_back, preferred_element_type=f32
    )
    grad_keys = grad_kfull[..., :HD] + jnp.einsum(
        "thf,fd->thd", grad_kbox, wb_back, preferred_element_type=f32
    )
    grad_w_box = jnp.einsum(
        "thf,thd->fd", grad_qbox, queries, preferred_element_type=f32
    ) + jnp.einsum("thf,thd->fd", grad_kbox, keys_in, preferred_element_type=f32)
    grad_mixed = jnp.concatenate(
        [
            grad_queries.reshape(row_count, model_width),
            grad_keys.reshape(row_count, model_width),
            grad_values,
        ],
        axis=-1,
    ).astype(jnp.bfloat16)
    grad_w_qkv = jnp.einsum("td,te->de", tokens, grad_mixed, preferred_element_type=f32)
    grad_b_qkv = jnp.sum(grad_mixed.astype(f32), axis=0)
    grad_tokens = grad_pre_one + jnp.einsum(
        "te,de->td", grad_mixed, wq_back, preferred_element_type=f32
    )
    part_wq, part_bq, part_wb, part_wo, part_bo, part_go, part_so = (
        lax.psum_scatter(grad_w_qkv, "fsdp", scatter_dimension=0, tiled=True),
        lax.psum_scatter(grad_b_qkv, "fsdp", scatter_dimension=0, tiled=True),
        lax.psum_scatter(grad_w_box, "fsdp", scatter_dimension=0, tiled=True),
        lax.psum_scatter(grad_w_out, "fsdp", scatter_dimension=0, tiled=True),
        lax.psum_scatter(grad_b_out, "fsdp", scatter_dimension=0, tiled=True),
        lax.psum_scatter(grad_gain_one, "fsdp", scatter_dimension=0, tiled=True),
        lax.psum_scatter(grad_shift_one, "fsdp", scatter_dimension=0, tiled=True),
    )
    part_wq, part_bq, part_wb, part_wo, part_bo, part_go, part_so = (
        lax.psum(part_wq.astype(jnp.bfloat16), "rep").astype(jnp.float32),
        lax.psum(part_bq.astype(jnp.bfloat16), "rep").astype(jnp.float32),
        lax.psum(part_wb.astype(jnp.bfloat16), "rep").astype(jnp.float32),
        lax.psum(part_wo.astype(jnp.bfloat16), "rep").astype(jnp.float32),
        lax.psum(part_bo.astype(jnp.bfloat16), "rep").astype(jnp.float32),
        lax.psum(part_go.astype(jnp.bfloat16), "rep").astype(jnp.float32),
        lax.psum(part_so.astype(jnp.bfloat16), "rep").astype(jnp.float32),
    )
    return (
        layer_out,
        grad_tokens,
        part_wq,
        part_bq,
        part_wb,
        part_wo,
        part_bo,
        part_go,
        part_so,
        part_wu,
        part_bu,
        part_wd,
        part_bd,
        part_gt,
        part_st,
    )


def solution(mesh):
    return jax.shard_map(
        per_device,
        mesh=mesh,
        in_specs=(
            P(("fsdp", "rep"), None),
            P(("fsdp", "rep"), None),
            P(("fsdp", "rep")),
            P(None, ("fsdp", "rep")),
            P("fsdp", None),
            P("fsdp"),
            P("fsdp", None),
            P("fsdp", None),
            P("fsdp"),
            P("fsdp"),
            P("fsdp"),
            P("fsdp", None),
            P("fsdp"),
            P("fsdp", None),
            P("fsdp"),
            P("fsdp"),
            P("fsdp"),
        ),
        out_specs=(
            P(("fsdp", "rep"), None),
            P(("fsdp", "rep"), None),
            P("fsdp", None),
            P("fsdp"),
            P("fsdp", None),
            P("fsdp", None),
            P("fsdp"),
            P("fsdp"),
            P("fsdp"),
            P("fsdp", None),
            P("fsdp"),
            P("fsdp", None),
            P("fsdp"),
            P("fsdp"),
            P("fsdp"),
        ),
        check_vma=False,
    )
```

profile of v0, /device:TPU:0, one launch (start us, length us, event | category | flops | bytes accessed | tf_op | source)
XLA Modules:
  0.0 1175.2 jit_solution(1787310209015399780)
XLA Ops:
  19.3 79.6 %all-reduce.18 = (bf16[2304]{0:T(1024)(128)(2,1)S(1)}, bf16[768]{0:T(1024)(128)(2,1)}, bf16[768]{0:T(1024)(128)(2,1)S(1)}, bf16[768]{0:T(1024)(128)(2,1)S(1)}, b...) all-reduce(bf16[2304]{0:T(1024)(128)(2,1)S(1)} %dynamic-update-slic, ...), channel_id=1, replica_groups=mesh['fsdp'=16,'rep'=2] {'fsdp'}, use_global_device_ids=true, to_apply=%add | all-reduce | flops 9984 | bytes 39936
  99.5 38.2 %all_gather.48 = bf16[128,64]{1,0:T(8,128)(2,1)} all-gather(bf16[8,64]{1,0:T(8,128)(2,1)S(1)} %convert_element_type.263), channel_id=1, replica_groups=mesh['fsdp'=16,'rep'=2] {'fsdp'}, dimensions={0}, use_global_device_ids=true | all-gather | bytes 17408 | tf_op jit(solution)/shard_map/all_gather | solution.py:76
  142.2 6.5 cosine_convert_fusion
  158.9 6.0 add_convert_fusion.1
  177.7 3.7 subtract_convert_fusion.2
  186.3 4.0 concatenate.42
  193.9 3.3 concatenate.46
  197.2 4.0 constant_dynamic-update-slice_fusion.1
  201.1 4.5 broadcast_dynamic-update-slice_fusion
  205.6 4.4 broadcast_dynamic-update-slice_fusion.2
  214.9 8.4 copy.103
  224.5 4.8 copy.102
  230.9 3.0 reshape_reshape.3
  234.7 72.5 %while.28 = (s32[]{:T(128)}, bf16[12,2,512,64]{2,3,1,0:T(8,128)(2,1)S(1)}, f32[12,2,512,1]{2,1,3,0:T(2,128)}, s32[12]{0:T(128)S(1)}, bf16[2,512,12,320]{1,3,0,2:...) while((s32[]{:T(128)}, ...), condition=%wide.region_3.4_spmd.clone, body=%wide.region_0.3_spmd.clone.sunk | while | flops 407370752 | bytes 8038051 | solution.py:130
  310.4 3.8 fusion.88
  314.9 38.1 %multiply_convert_fusion.1 = (bf16[1024,3072]{1,0:T(8,128)(2,1)}, f32[1024,3072]{1,0:T(8,128)}, f32[1024,3072]{1,0:T(8,128)}) fusion(f32[3072]{0:T(1024)S(1)} %convert_element_type.284, bf16[768,3072]{1,0:T(8,128)(2,1)} %all-gather.9.cloned.1.call-done, f32[1024,768]{0,1:T(8,128)S(1)} %get-tuple-element.379, f32[768]{0:T(1024)S(1)} %copy-done.49, ...), kind=kOutput, calls=%fused_computation.52 | convolution fusion | flops 5043388416 | bytes 39348224 | tf_op jit(solution)/shard_map/dot_general | solution.py:145
  353.0 9.2 fusion.89
  365.5 3.2 convert_reduce_fusion.3
  368.7 17.5 %convert_reduce_fusion = (f32[3072]{0:T(1024)S(1)}, bf16[1024,3072]{1,0:T(8,128)(2,1)}) fusion(f32[1024,3072]{1,0:T(8,128)} %get-tuple-element.349, bf16[1024,768]{0,1:T(8,128)(2,1)S(1)} %get-tuple-element.345, bf16[3072,768]{1,0:T(8,128)(2,1)} %all-gather.11.cloned.1.call-done, f32[1024,3072]{1,0:T(8,128)} %get-tuple-element.380, ...), kind=kOutput, calls=%fused_computation.50 | convolution fusion | flops 4885312512 | bytes 37773312 | tf_op jit(solution)/shard_map/td,fd->tf/dot_general | solution.py:163
  386.2 11.3 multiply_reduce_fusion.1
  399.0 2.9 fusion.76
  401.9 3.9 convolution_convert_fusion
  409.0 162.9 %while.29 = (s32[]{:T(128)}, f32[12,2,512,320]{2,3,1,0:T(8,128)}, f32[12,2,512,320]{2,3,1,0:T(8,128)}, bf16[12,2,512,64]{2,3,1,0:T(8,128)(2,1)S(1)}, s32[12]{0:T...) while((s32[]{:T(128)}, f32[12,2,512,320]{2,3,1,0:T(8,128)}, ...), condition=%wide.region_14.15_spmd.clone, body=%wide.region_12.14_spmd.clone.sunk | while | flops 1146747904 | bytes 21919948 | solution.py:226
  416.9 2.7 fusion.141
  430.4 2.7 fusion.141
  471.1 2.7 fusion.141
  498.1 2.8 fusion.141
  500.9 2.9 fusion.140
  511.9 2.8 fusion.141
  539.0 2.7 fusion.141
  541.7 2.7 fusion.140
  552.5 2.8 fusion.141
  571.9 13.9 %copy.135 = f32[12,2,40,8,512]{4,3,1,2,0:T(8,128)} copy(f32[12,2,40,8,512]{4,3,2,1,0:T(8,128)} %bitcast.206) | data formatting | bytes 31457280 | tf_op jit(solution)/shard_map/reshape | solution.py:227
  585.8 13.8 %copy.136 = f32[12,2,40,8,512]{4,3,1,2,0:T(8,128)} copy(f32[12,2,40,8,512]{4,3,2,1,0:T(8,128)} %bitcast.207) | data formatting | bytes 31457280 | tf_op jit(solution)/shard_map/reshape | solution.py:228
  601.7 6.5 subtract_convert_fusion.1
  608.2 5.3 fusion.50
  613.6 3.7 fusion.49
  618.5 9.2 convolution_bitcast_fusion.2
  627.7 8.0 copy.132
  637.1 10.2 fusion.90
  649.3 10.5 fusion.79
  669.2 75.3 %all-reduce.17 = (bf16[2304]{0:T(1024)(128)(2,1)S(1)}, bf16[128,64]{1,0:T(8,128)(2,1)S(1)}, bf16[768]{0:T(1024)(128)(2,1)S(1)}, bf16[768]{0:T(1024)(128)(2,1)S(1...) all-reduce(f32[2304]{0:T(1024)S(1)} %convert_reduce_fusion.1, ...), channel_id=3, replica_groups=mesh['fsdp'=16,'rep'=2] {'fsdp'}, use_global_device_ids=true, to_apply=%region_18.19.clone | all-reduce | flops 18176 | bytes 109056
  753.9 32.2 %reduce-scatter.13.cloned.1.call-done = f32[48,2304]{1,0:T(8,128)} async-done(((f32[768,2304]{1,0:T(8,128)}), f32[48,2304]{1,0:T(8,128)}) %reduce-scatter.13.cloned.1.call-update) | async-done | bytes 442384
  788.2 174.3 %reduce-scatter.11.cloned.1.call-done = f32[192,768]{1,0:T(8,128)} async-done(((f32[3072,768]{1,0:T(8,128)}), f32[192,768]{1,0:T(8,128)}) %reduce-scatter.11.cloned.1.call-update) | async-done | bytes 589840 | tf_op jit(solution)/shard_map/reduce_scatter | solution.py:173
  964.3 173.9 %reduce-scatter.9.cloned.1.call-done = f32[48,3072]{1,0:T(8,128)} async-done(((f32[768,3072]{1,0:T(8,128)}), f32[48,3072]{1,0:T(8,128)}) %reduce-scatter.9.cloned.1.call-update) | async-done | bytes 589840 | tf_op jit(solution)/shard_map/reduce_scatter | solution.py:171
  1140.1 8.9 convolution_add_fusion.1
  1149.0 3.7 copy.121
  1154.2 6.9 all-reduce.23.cloned.1.call-done
  (435 shorter events, 266.1 us)
Async XLA Ops:
  7.2 7.8 copy-start.55
  7.2 7.7 copy-start.58
  7.2 7.7 copy-start.59
  7.2 7.7 copy-start.60
  7.2 7.7 copy-start.61
  7.2 7.7 copy-start.62
  7.2 7.7 copy-start.63
  7.3 9.6 copy-start.56
  7.3 10.3 copy-start.57
  7.3 92.2 %copy-start.48 = (f32[8,64]{1,0:T(8,128)S(1)}, f32[8,64]{1,0:T(8,128)}, u32[]{:S(2)}) copy-start(f32[8,64]{1,0:T(8,128)} %param.27) | copy-start | bytes 6148
  7.3 130.4 %copy-start.45 = (s32[4,1024]{1,0:T(4,128)S(1)}, s32[4,1024]{1,0:T(4,128)}, u32[]{:S(2)}) copy-start(s32[4,1024]{1,0:T(4,128)} %param.24) | copy-start | bytes 49156
  7.3 141.4 %copy-start.52 = (s32[1024]{0:T(1024)S(1)}, s32[1024]{0:T(1024)}, u32[]{:S(2)}) copy-start(s32[1024]{0:T(1024)} %param.23) | copy-start | bytes 12292
  7.3 143.2 %copy-start.34 = (bf16[1024,768]{1,0:T(8,128)(2,1)S(1)}, bf16[1024,768]{1,0:T(8,128)(2,1)}, u32[]{:S(2)}) copy-start(bf16[1024,768]{1,0:T(8,128)(2,1)} %param.21) | copy-start | bytes 4718596
  7.3 151.6 %all-gather.5.cloned.1.call-start = ((), (), s32[]{:S(2)}) async-start(), calls=%async_computation.4 | async-start | bytes 3760128 | tf_op jit(solution)/shard_map/all_gather | solution.py:74
  9.2 301.1 %all-gather.7.cloned.1.call-start = ((), (), s32[]{:S(2)}) async-start(), calls=%async_computation.5 | async-start | bytes 1253376 | tf_op jit(solution)/shard_map/all_gather | solution.py:77
  10.9 303.8 %all-gather.9.cloned.1.call-start = ((), (), s32[]{:S(2)}) async-start(), calls=%async_computation.6 | async-start | bytes 5013504 | tf_op jit(solution)/shard_map/all_gather | solution.py:138
  12.7 143.3 %copy-start.33 = (bf16[1024,768]{1,0:T(8,128)(2,1)S(1)}, bf16[1024,768]{1,0:T(8,128)(2,1)}, u32[]{:S(2)}) copy-start(bf16[1024,768]{1,0:T(8,128)(2,1)} %param.22) | copy-start | bytes 4718596
  12.8 340.2 %all-gather.11.cloned.1.call-start = ((), (), s32[]{:S(2)}) async-start(), calls=%async_computation.7 | async-start | bytes 5013504 | tf_op jit(solution)/shard_map/all_gather | solution.py:140
  14.7 737.6 %reduce-scatter.7.cloned.1.call-start = ((), (), s32[]{:S(2)}) async-start(), calls=%async_computation.8 | async-start | bytes 2506752 | tf_op jit(solution)/shard_map/reduce_scatter | solution.py:268
  139.6 38.1 %copy-start.29 = (f32[1024,64]{0,1:T(8,128)}, f32[1024,64]{0,1:T(8,128)S(1)}, u32[]{:S(2)}) copy-start(f32[1024,64]{0,1:T(8,128)S(1)} %get-tuple-element.374) | copy-start | bytes 786436
  167.7 7.1 copy-start.3
  170.0 6.6 copy-start.1
  183.7 6.5 copy-start.9
  186.3 6.4 copy-start.11
  197.2 4.0 copy-start.15
  201.1 4.5 copy-start.41
  212.5 10.8 slice-start
  214.9 8.4 slice-start.1
  224.5 4.8 copy-start.8
  314.2 38.8 %copy-start.5 = (f32[1024,768]{0,1:T(8,128)}, f32[1024,768]{0,1:T(8,128)S(1)}, u32[]{:S(2)}) copy-start(f32[1024,768]{0,1:T(8,128)S(1)} %get-tuple-element.379) | copy-start | bytes 9437188
  314.6 38.4 %copy-start.50 = (f32[768]{0:T(1024)S(1)}, f32[768]{0:T(1024)}, u32[]{:S(2)}) copy-start(f32[768]{0:T(1024)} %convert_element_type.288) | copy-start | bytes 9220
  368.7 17.5 %copy-start.37 = (bf16[1024,768]{0,1:T(8,128)(2,1)}, bf16[1024,768]{0,1:T(8,128)(2,1)S(1)}, u32[]{:S(2)}) copy-start(bf16[1024,768]{0,1:T(8,128)(2,1)S(1)} %get-tuple-element.345) | copy-start | bytes 4718596
  386.2 11.4 copy-start.6
  408.7 377.4 %reduce-scatter.13.cloned.1.call-start = ((), (), s32[]{:S(2)}) async-start(), calls=%async_computation.11 | async-start | bytes 7520256
  601.6 15.7 %copy-start.13 = (bf16[96,8,2,512]{3,1,2,0:T(8,128)(2,1)}, bf16[96,8,2,512]{3,1,2,0:T(8,128)(2,1)S(1)}, u32[]{:S(2)}) copy-start(bf16[96,8,2,512]{3,1,2,0:T(8,128)(2,1)S(1)} %copy.138) | copy-start | bytes 4718596
  601.6 6.5 copy-start.40
  608.1 5.4 copy-start.20
  608.1 5.4 copy-start.22
  608.1 5.4 copy-start.16
  608.1 5.4 copy-start.18
  613.5 3.8 copy-start.24
  613.6 4.9 copy-start.35
  635.8 326.7 %reduce-scatter.11.cloned.1.call-start = ((), (), s32[]{:S(2)}) async-start(), calls=%async_computation.10 | async-start | bytes 10027008 | tf_op jit(solution)/shard_map/reduce_scatter | solution.py:173
  647.4 490.8 %reduce-scatter.9.cloned.1.call-start = ((), (), s32[]{:S(2)}) async-start(), calls=%async_computation.9 | async-start | bytes 10027008 | tf_op jit(solution)/shard_map/reduce_scatter | solution.py:171
  659.8 5.6 copy-start.4
  659.9 501.3 %all-reduce.23.cloned.1.call-start = ((), (), s32[]{:S(2)}) async-start(), calls=%async_computation.12 | async-start | bytes 2506752 | tf_op jit(solution)/shard_map/psum | solution.py:274
  669.1 470.9 %copy-start.25 = (bf16[1024,12,64]{0,2,1:T(8,128)(2,1)S(1)}, bf16[1024,12,64]{0,2,1:T(8,128)(2,1)}, u32[]{:S(2)}) copy-start(bf16[1024,12,64]{0,2,1:T(8,128)(2,1)} %copy-done.24) | copy-start | bytes 4718596
  1149.0 3.7 copy-start.12
  (27 other events, 50.7 us)
Sparse Core Ops, SparseCore 0:
  11.5 74.6 all-gather.4
  89.0 54.6 all-gather.6
  147.1 79.3 all-gather.8
  229.7 79.0 all-gather.10
  408.9 125.9 reduce-scatter.6
  635.9 150.2 reduce-scatter.12
  792.8 169.6 reduce-scatter.10
  968.2 170.0 reduce-scatter.8
  1142.1 18.9 all-reduce.22
where the time goes:
time: 1180 us
  waiting for transfers between devices  388 us (33%)
  matrix products  292 us (25%)
  blocking collectives  196 us (17%)
  local copies, waits for them, and re-layouts  157 us (13%)
  other arithmetic  75 us (6%)
  loops' own time  47.6 us (4%)
  between operations  20 us (2%)
    reduce_scatter x1, waiting for transfers between devices, per_device(): lax.psum_scatter(grad_w_down, 'fsdp', scatter_dimension=0, tiled=True)  174 us
    reduce_scatter x1, waiting for transfers between devices, per_device(): lax.psum_scatter(grad_w_up, 'fsdp', scatter_dimension=0, tiled=True)  174 us
    unnamed x2, blocking collectives  155 us
    unnamed x175, local copies, waits for them, and re-layouts  67 us
    dot_general x24, matrix products, head_scores(): jnp.einsum('nqd,nkd->nqk', q_head, k_head, preferred_element_type=f32)  54 us
    all_gather x1, blocking collectives, per_device(): lax.all_gather(low_cast(w_box), 'fsdp', axis=0, tiled=True)  38.2 us
    dot_general x1, matrix products, per_device(): jnp.dot(hidden_low, wu_full, preferred_element_type=f32)  38.1 us
    dot_general x12, matrix products, backward_head(): jnp.einsum('nqk,nqd->nkd', grad_scores, q_head, preferred_element_type=f32)  32.7 us
  transfers between devices with their start and end apart: 9, of which 4 were waited for; matrix products, arithmetic and copies ran while one was open for 38% of the time, Pallas kernels for 0%

commit v1 on v0

v1 whole, which is shorter than its diff:
```python
import functools
import math

import jax
import jax.numpy as jnp
from jax import lax
from jax.experimental import pallas as pl
from jax.experimental.pallas import tpu as pltpu
from jax.sharding import PartitionSpec as P

HEADS = 12
HD = 64
FREQ = 16
SLOT = 512
WAVE = 4 * FREQ
PAIR = 2 * HD
QUAD = 4 * HD

f32 = jnp.float32
bf16 = jnp.bfloat16
neg_large = -1e30
eps_norm = 1e-12
scale_factor = 1.0 / math.sqrt(HD)
vmem_limit = 64_000_000


def dot_nn(left, right):
    return lax.dot_general(left, right, (((1,), (0,)), ((), ())), preferred_element_type=f32)


def dot_nt(left, right):
    return lax.dot_general(left, right, (((1,), (1,)), ((), ())), preferred_element_type=f32)


def dot_tn(left, right):
    return lax.dot_general(left, right, (((0,), (0,)), ((), ())), preferred_element_type=f32)


def aligned(index, size):
    return pl.ds(pl.multiple_of(index * size, size), size)


def wave_rows(coord_bits):
    row = lax.broadcasted_iota(jnp.int32, (2 * WAVE, 16), 0)
    col = lax.broadcasted_iota(jnp.int32, (2 * WAVE, 16), 1)
    coord_of = (row % WAVE) // FREQ
    pick = jnp.where(col == coord_of, 32.0, jnp.where(col == coord_of + 4, 1.0, 0.0)).astype(bf16)
    coords = dot_nn(pick, coord_bits)
    rows = lax.broadcasted_iota(jnp.int32, coords.shape, 0)
    freq_index = (rows % FREQ).astype(f32)
    frequency = jnp.exp(-math.log(10000.0) * freq_index / FREQ)
    angle = coords * (100.0 / 1024.0) * frequency
    turns = jnp.floor(angle * (2.0 / math.pi) + 0.5)
    rest = ((angle - turns * 1.5703125) - turns * 4.837512969970703125e-4) - turns * 7.549789954891e-8
    square = rest * rest
    sine = rest + rest * square * (
        -1.6666654611e-1 + square * (8.3321608736e-3 + square * -1.9515295891e-4)
    )
    cosine = 1.0 - 0.5 * square + square * square * (
        4.166664568298827e-2 + square * (-1.388731625493765e-3 + square * 2.443315711809948e-5)
    )
    quadrant = turns.astype(jnp.int32) + jnp.where(rows >= WAVE, 1, 0)
    value = jnp.where((quadrant & 1) == 1, cosine, sine)
    value = jnp.where((quadrant & 2) == 2, -value, value)
    return value.astype(bf16).astype(f32)


def swap_lanes(value):
    return pltpu.roll(value, WAVE, 1)


def attend_forward(
    tok, coord_bits, segs, w_qkv, b_qkv, w_box,
    q8t, k8t, v_row, e_hbm, inv_total, ctx, ctx_t, wave_t,
    k_row, v_t, bias, wave_r, e_buf, e_sem,
):
    slot_count = tok.shape[0] // SLOT
    width = tok.shape[1]
    pairs = HEADS // 2
    wave_t[...] = wave_rows(coord_bits[...])
    wave_r[...] = jnp.transpose(wave_t[...])
    for slot in range(slot_count):
        seg = segs[slot : slot + 1, :].astype(f32)
        seg_i = jnp.broadcast_to(seg, (SLOT, SLOT))
        seg_j = jnp.transpose(seg_i)
        bias[slot] = jnp.where(seg_i == seg_j, 0.0, neg_large)

    def project(step, carry):
        quad, slot = step // slot_count, step % slot_count
        rows = tok[aligned(slot, SLOT), :]

        def columns(part):
            at = pl.ds(pl.multiple_of(part * width + quad * QUAD, QUAD), QUAD)
            return (dot_nn(rows, w_qkv[:, at]) + b_qkv[:, at]).astype(bf16)

        q, k, v = columns(0), columns(1), columns(2)
        qt = jnp.transpose(q.astype(f32) * scale_factor).astype(bf16)
        kt = jnp.transpose(k.astype(f32) * scale_factor).astype(bf16)
        vt = jnp.transpose(v.astype(f32)).astype(bf16)
        for part in range(2):
            pair = quad * 2 + part
            here = slice(part * PAIR, (part + 1) * PAIR)
            q8t[slot, pair] = qt[here]
            k8t[slot, pair] = kt[here]
            v_t[slot, pair] = vt[here]
            k_row[slot, pair] = k[:, here]
            v_row[slot, pair] = v[:, here]
        return carry

    lax.fori_loop(0, slot_count * (pairs // 2), project, 0)

    lane = lax.broadcasted_iota(jnp.int32, (SLOT, PAIR), 1)

    def attend(step, carry):
        pair, slot = step // slot_count, step % slot_count
        cols = aligned(slot, SLOT)
        place = step % 2

        @pl.when(step >= 2)
        def _():
            for head in range(2):
                pltpu.make_async_copy(e_buf.at[place, head], e_hbm.at[0], e_sem.at[place, head]).wait()

        sine_t, cosine_t = wave_t[:WAVE, cols], wave_t[WAVE:, cols]
        sc_t = (wave_t[:, cols] * scale_factor).astype(bf16)
        sc_r = wave_r[cols, :]
        cs_r = swap_lanes(sc_r)
        cc_r = jnp.where(lane < WAVE, cs_r, sc_r)
        ss_r = jnp.where(lane < WAVE, sc_r, -cs_r)
        cs_low = cs_r.astype(bf16)
        keys = k_row[slot, pair]
        heads_t = []
        for head in range(2):
            span = slice(head * HD, (head + 1) * HD)
            key_box = dot_nt(keys[:, span], w_box[...])
            k_side = (key_box * cc_r + swap_lanes(key_box) * ss_r).astype(bf16)
            q_t = q8t[slot, pair, span, :]
            query_box = dot_nn(w_box[...], q_t)
            first, second = query_box[:WAVE], query_box[WAVE:]
            q_side = jnp.concatenate(
                [first * sine_t + second * cosine_t, second * sine_t - first * cosine_t], axis=0
            ).astype(bf16)
            zero = jnp.zeros_like(q_t)
            q_pair = [q_t, zero] if head == 0 else [zero, q_t]
            k_full = jnp.concatenate([keys, cs_low, k_side], axis=1)
            q_full = jnp.concatenate(q_pair + [q_side, sc_t], axis=0)
            scores = dot_nn(k_full, q_full) + bias[slot]
            top = jnp.max(scores, axis=0, keepdims=True)
            exps = jnp.exp(scores - top)
            inverse = 1.0 / jnp.sum(exps, axis=0, keepdims=True)
            low_exps = exps.astype(bf16)
            e_buf[place, head] = low_exps
            pltpu.make_async_copy(
                e_buf.at[place, head], e_hbm.at[step * 2 + head], e_sem.at[place, head]
            ).start()
            inv_total[step * 2 + head] = inverse
            heads_t.append(dot_nn(v_t[slot, pair, span, :], low_exps) * inverse)
        both = jnp.concatenate(heads_t, axis=0)
        ctx_t[aligned(pair, PAIR), cols] = both.astype(bf16)
        ctx[cols, aligned(pair, PAIR)] = jnp.transpose(both).astype(bf16)
        return carry

    steps = slot_count * pairs
    lax.fori_loop(0, steps, attend, 0)
    for place in range(2):
        for head in range(2):
            pltpu.make_async_copy(e_buf.at[place, head], e_hbm.at[0], e_sem.at[place, head]).wait()


def attend_backward(
    tok_t, q8t, k8t, v_row, e_hbm, inv_total, ctx_t, g_ctx_t, wave_t, w_qkv, w_box, w_box_t, g_pre_one,
    g_tok, g_w_qkv, g_b_qkv, g_w_box,
    g_mix, e_buf, e_sem,
):
    slot_count = tok_t.shape[1] // SLOT
    width = tok_t.shape[0]
    pairs = HEADS // 2
    steps = slot_count * pairs
    g_w_box[...] = jnp.zeros_like(g_w_box)

    def fetch(step, place):
        for head in range(2):
            pltpu.make_async_copy(
                e_hbm.at[step * 2 + head], e_buf.at[place, head], e_sem.at[place, head]
            ).start()

    fetch(0, 0)

    def attend(step, carry):
        pair, slot = step // slot_count, step % slot_count
        cols = aligned(slot, SLOT)
        place = step % 2

        @pl.when(step + 1 < steps)
        def _():
            fetch(step + 1, 1 - place)

        for head in range(2):
            pltpu.make_async_copy(e_hbm.at[0], e_buf.at[place, head], e_sem.at[place, head]).wait()
        sine_t, cosine_t = wave_t[:WAVE, cols], wave_t[WAVE:, cols]
        sc_t = (wave_t[:, cols] * scale_factor).astype(bf16)
        cs_t = (jnp.concatenate([cosine_t, sine_t], axis=0) * scale_factor).astype(bf16)
        values = v_row[slot, pair]
        g_parts = [[], [], []]
        for head in range(2):
            span = slice(head * HD, (head + 1) * HD)
            at = pl.ds(pl.multiple_of(pair * PAIR + head * HD, HD), HD)
            g_rows = g_ctx_t[at, cols].astype(f32) * inv_total[step * 2 + head]
            row_dot = jnp.sum(g_rows * ctx_t[at, cols].astype(f32), axis=0, keepdims=True)
            g_low = g_rows.astype(bf16)
            zero = jnp.zeros_like(g_low)
            g_pair = jnp.concatenate([g_low, zero] if head == 0 else [zero, g_low], axis=0)
            low_exps = e_buf[place, head]
            g_probs = dot_nn(values, g_pair)
            g_scores = (low_exps.astype(f32) * (g_probs - row_dot)).astype(bf16)
            g_parts[2].append(dot_nt(g_low, low_exps))
            k_t, q_t = k8t[slot, pair, span, :], q8t[slot, pair, span, :]
            g_q = dot_nn(jnp.concatenate([k_t, cs_t], axis=0), g_scores)
            g_k = dot_nt(jnp.concatenate([q_t, sc_t], axis=0), g_scores)
            first, second = g_q[HD : HD + WAVE], g_q[HD + WAVE :]
            g_qbox = jnp.concatenate(
                [first * sine_t - second * cosine_t, first * cosine_t + second * sine_t], axis=0
            ).astype(bf16)
            first, second = g_k[HD : HD + WAVE], g_k[HD + WAVE :]
            g_kbox = jnp.concatenate(
                [first * cosine_t - second * sine_t, first * sine_t + second * cosine_t], axis=0
            ).astype(bf16)
            g_parts[0].append(g_q[:HD] + dot_nn(w_box_t[...], g_qbox))
            g_parts[1].append(g_k[:HD] + dot_nn(w_box_t[...], g_kbox))
            g_w_box[...] += dot_nt(g_qbox, q_t) + dot_nt(g_kbox, k_t)
        for part in range(3):
            g_mix[part, aligned(pair, PAIR), cols] = jnp.concatenate(g_parts[part], axis=0).astype(bf16)
        return carry

    lax.fori_loop(0, steps, attend, 0)
    g_w_box[...] = g_w_box[...] * (1.0 / scale_factor)

    ones = jnp.ones((16, tok_t.shape[1]), bf16)

    def weight_grad(step, carry):
        part, quad = step // (pairs // 2), step % (pairs // 2)
        grad = g_mix[part, aligned(quad, QUAD), :]
        at = pl.ds(pl.multiple_of(part * width + quad * QUAD, QUAD), QUAD)
        g_w_qkv[:, at] = dot_nt(tok_t[...], grad).astype(bf16)
        g_b_qkv[:, at] = dot_nt(ones, grad)[:1]
        return carry

    lax.fori_loop(0, 3 * (pairs // 2), weight_grad, 0)

    def token_grad(step, carry):
        cols = aligned(step, QUAD)
        total = dot_nn(w_qkv[:, :width], g_mix[0, :, cols])
        total += dot_nn(w_qkv[:, width : 2 * width], g_mix[1, :, cols])
        total += dot_nn(w_qkv[:, 2 * width :], g_mix[2, :, cols])
        g_tok[cols, :] = jnp.transpose(total) + g_pre_one[cols, :]
        return carry

    lax.fori_loop(0, tok_t.shape[1] // QUAD, token_grad, 0)


def gelu_parts(value):
    size = jnp.abs(value) * math.sqrt(0.5)
    t = 1.0 / (1.0 + 0.3275911 * size)
    bell = jnp.exp(-0.5 * value * value)
    tail = t * (
        0.254829592 + t * (-0.284496736 + t * (1.421413741 + t * (-1.453152027 + t * 1.061405429)))
    )
    half_tail = 0.5 * tail * bell
    return jnp.where(value >= 0, 1.0 - half_tail, half_tail), bell * (1.0 / math.sqrt(2.0 * math.pi))


def row_mean(value):
    return jnp.mean(value, axis=-1, keepdims=True)


ROWS = 256
FCOLS = 512


def feed_forward(
    tok, cot, ctx, ctx_t, w_out, b_out, gain_one, shift_one, w_up, b_up, w_down, b_down, gain_two, shift_two,
    layer_out, g_pre_one, g_ctx_t, tok_t, g_w_out, g_w_up, g_w_down, g_b_up, g_small,
    act, slope, normed, total, low_hidden, low_hidden_t, g_down, inv_one,
):
    width = tok.shape[1]
    row_blocks = tok.shape[0] // ROWS
    col_blocks = w_up.shape[1] // FCOLS
    g_small[...] = jnp.zeros_like(g_small)
    g_b_up[...] = jnp.zeros_like(g_b_up)

    def column_sum(value):
        return jnp.sum(value, axis=0, keepdims=True)

    def first_norm(block, carry):
        rows = aligned(block, ROWS)
        token_rows = tok[rows, :].astype(f32)
        tok_t[:, rows] = jnp.transpose(token_rows).astype(bf16)
        pre = token_rows + dot_nn(ctx[rows, :], w_out[...]) + b_out[...]
        center = pre - row_mean(pre)
        invdev = lax.rsqrt(row_mean(center * center) + eps_norm)
        unit = center * invdev
        inv_one[rows, :] = jnp.broadcast_to(invdev, (ROWS, 128))
        normed[rows, :] = unit
        hidden = unit * gain_one[...] + shift_one[...]
        low_hidden[rows, :] = hidden.astype(bf16)
        low_hidden_t[:, rows] = jnp.transpose(hidden).astype(bf16)
        return carry

    lax.fori_loop(0, row_blocks, first_norm, 0)

    def up_down(step, carry):
        col, block = step // row_blocks, step % row_blocks
        rows, cols = aligned(block, ROWS), aligned(col, FCOLS)
        up = dot_nn(low_hidden[rows, :], w_up[:, cols]) + b_up[:, cols]
        cdf, pdf = gelu_parts(up)
        low_act = (up * cdf).astype(bf16)
        act[col, rows, :] = low_act
        slope[col, rows, :] = (cdf + up * pdf).astype(bf16)
        down = dot_nn(low_act, w_down[cols, :])

        @pl.when(col == 0)
        def _():
            total[rows, :] = down

        @pl.when(col > 0)
        def _():
            total[rows, :] += down

        return carry

    lax.fori_loop(0, col_blocks * row_blocks, up_down, 0)

    def second_norm(block, carry):
        rows = aligned(block, ROWS)
        pre = normed[rows, :] * gain_one[...] + shift_one[...] + total[rows, :] + b_down[...]
        center = pre - row_mean(pre)
        invdev = lax.rsqrt(row_mean(center * center) + eps_norm)
        unit = center * invdev
        layer_out[rows, :] = (unit * gain_two[...] + shift_two[...]).astype(bf16)
        grad = cot[rows, :].astype(f32)
        scaled = grad * gain_two[...]
        g_pre = invdev * (scaled - row_mean(scaled) - unit * row_mean(scaled * unit))
        total[rows, :] = g_pre
        low_pre = g_pre.astype(bf16)
        g_down[rows, :] = low_pre
        g_small[0:1, :] += column_sum(grad * unit)
        g_small[1:2, :] += column_sum(grad)
        g_small[2:3, :] += column_sum(low_pre.astype(f32))
        return carry

    lax.fori_loop(0, row_blocks, second_norm, 0)

    def back_columns(col, carry):
        cols = aligned(col, FCOLS)

        def back_rows(block, inner):
            rows = aligned(block, ROWS)
            g_act = dot_nt(g_down[rows, :], w_down[cols, :])
            g_up = (g_act * slope[col, rows, :].astype(f32)).astype(bf16)
            slope[col, rows, :] = g_up
            g_b_up[:, cols] += column_sum(g_up.astype(f32))
            total[rows, :] += dot_nt(g_up, w_up[:, cols])
            return inner

        lax.fori_loop(0, row_blocks, back_rows, 0)
        g_w_down[cols, :] = dot_tn(act[col], g_down[...]).astype(bf16)
        g_w_up[:, cols] = dot_nn(low_hidden_t[...], slope[col]).astype(bf16)
        return carry

    lax.fori_loop(0, col_blocks, back_columns, 0)

    def first_back(block, carry):
        rows = aligned(block, ROWS)
        grad, unit = total[rows, :], normed[rows, :]
        scaled = grad * gain_one[...]
        g_pre = inv_one[rows, :1] * (scaled - row_mean(scaled) - unit * row_mean(scaled * unit))
        g_pre_one[rows, :] = g_pre
        low_pre = g_pre.astype(bf16)
        g_down[rows, :] = low_pre
        g_small[3:4, :] += column_sum(grad * unit)
        g_small[4:5, :] += column_sum(grad)
        g_small[5:6, :] += column_sum(low_pre.astype(f32))
        g_ctx_t[:, rows] = dot_nt(w_out[...], low_pre).astype(bf16)
        return carry

    lax.fori_loop(0, row_blocks, first_back, 0)

    def out_grad(block, carry):
        rows = aligned(block, ROWS)
        g_w_out[rows, :] = dot_nn(ctx_t[rows, :], g_down[...]).astype(bf16)
        return carry

    lax.fori_loop(0, width // ROWS, out_grad, 0)


def shaped(shape, dtype):
    return jax.ShapeDtypeStruct(shape, dtype)


def in_vmem(count):
    return [pl.BlockSpec(memory_space=pltpu.VMEM)] * count


def params():
    return pltpu.CompilerParams(vmem_limit_bytes=vmem_limit)


def run_forward(tokens, coord_bits, segs, w_qkv, b_qkv, w_box):
    count, width = tokens.shape
    slots, pairs = count // SLOT, HEADS // 2
    out_shape = [
        shaped((slots, pairs, PAIR, SLOT), bf16),
        shaped((slots, pairs, PAIR, SLOT), bf16),
        shaped((slots, pairs, SLOT, PAIR), bf16),
        shaped((slots * HEADS, SLOT, SLOT), bf16),
        shaped((slots * HEADS, 1, SLOT), f32),
        shaped((count, width), bf16),
        shaped((width, count), bf16),
        shaped((2 * WAVE, count), f32),
    ]
    out_specs = in_vmem(3) + [pl.BlockSpec(memory_space=pl.ANY)] + in_vmem(4)
    return pl.pallas_call(
        attend_forward,
        out_shape=out_shape,
        in_specs=in_vmem(6),
        out_specs=out_specs,
        scratch_shapes=[
            pltpu.VMEM((slots, pairs, SLOT, PAIR), bf16),
            pltpu.VMEM((slots, pairs, PAIR, SLOT), bf16),
            pltpu.VMEM((slots, SLOT, SLOT), f32),
            pltpu.VMEM((count, 2 * WAVE), f32),
            pltpu.VMEM((2, 2, SLOT, SLOT), bf16),
            pltpu.SemaphoreType.DMA((2, 2)),
        ],
        compiler_params=params(),
        name="attend_forward",
    )(tokens, coord_bits, segs, w_qkv, b_qkv, w_box)


def run_feed_forward(tok, cot, ctx, ctx_t, w_out, b_out, g1, s1, w_up, b_up, w_down, b_down, g2, s2):
    count, width = tok.shape
    ff = w_up.shape[1]
    out_shape = [
        shaped((count, width), bf16),
        shaped((count, width), f32),
        shaped((width, count), bf16),
        shaped((width, count), bf16),
        shaped(w_out.shape, bf16),
        shaped(w_up.shape, bf16),
        shaped(w_down.shape, bf16),
        shaped((1, ff), f32),
        shaped((8, width), f32),
    ]
    return pl.pallas_call(
        feed_forward,
        out_shape=out_shape,
        in_specs=in_vmem(14),
        out_specs=in_vmem(9),
        scratch_shapes=[
            pltpu.VMEM((ff // FCOLS, count, FCOLS), bf16),
            pltpu.VMEM((ff // FCOLS, count, FCOLS), bf16),
            pltpu.VMEM((count, width), f32),
            pltpu.VMEM((count, width), f32),
            pltpu.VMEM((count, width), bf16),
            pltpu.VMEM((width, count), bf16),
            pltpu.VMEM((count, width), bf16),
            pltpu.VMEM((count, 128), f32),
        ],
        compiler_params=params(),
        name="feed_forward",
    )(tok, cot, ctx, ctx_t, w_out, b_out, g1, s1, w_up, b_up, w_down, b_down, g2, s2)


def run_backward(tok_t, q8t, k8t, v_row, e_hbm, inv_total, ctx_t, g_ctx_t, wave_t, w_qkv, w_box, w_box_t, g_pre_one):
    width, count = tok_t.shape
    out_shape = [
        shaped((count, width), f32),
        shaped(w_qkv.shape, bf16),
        shaped((1, w_qkv.shape[1]), f32),
        shaped(w_box.shape, f32),
    ]
    return pl.pallas_call(
        attend_backward,
        out_shape=out_shape,
        in_specs=in_vmem(4) + [pl.BlockSpec(memory_space=pl.ANY)] + in_vmem(8),
        out_specs=in_vmem(4),
        scratch_shapes=[
            pltpu.VMEM((3, width, count), bf16),
            pltpu.VMEM((2, 2, SLOT, SLOT), bf16),
            pltpu.SemaphoreType.DMA((2, 2)),
        ],
        compiler_params=params(),
        name="attend_backward",
    )(tok_t, q8t, k8t, v_row, e_hbm, inv_total, ctx_t, g_ctx_t, wave_t, w_qkv, w_box, w_box_t, g_pre_one)


def per_device(
    fsdp, tokens, cotangent, segments, box_coords, w_qkv, b_qkv, w_box, w_out, b_out, gain_one, shift_one,
    w_up, b_up, w_down, b_down, gain_two, shift_two,
):
    count, width = tokens.shape
    low = lambda value: value.astype(bf16)
    gather = lambda value: lax.all_gather(low(value), "fsdp", axis=0, tiled=True)
    wq, wo, wu, wd = gather(w_qkv), gather(w_out), gather(w_up), gather(w_down)
    vectors = [b_qkv, b_out, gain_one, shift_one, b_up, b_down, gain_two, shift_two, w_box.reshape(-1)]
    sizes = [v.shape[0] for v in vectors]
    total = sum(sizes)
    padded = -(-total // 128) * 128
    packed = jnp.concatenate([low(v) for v in vectors] + [jnp.zeros((padded - total,), bf16)]).reshape(1, padded)
    table = lax.all_gather(packed, "fsdp", axis=0, tiled=True)
    full, at = [], 0
    for size in sizes:
        full.append(table[:, at : at + size].reshape(1, -1).astype(f32))
        at += size
    bq, bo, g1, s1, bu, bd, g2, s2 = full[:8]
    wb = full[8].reshape(-1, HD).astype(bf16)

    bits = jnp.concatenate([box_coords >> 5, box_coords & 31, jnp.zeros((8, count), jnp.int32)], axis=0).astype(bf16)
    segs = segments.reshape(-1, SLOT)
    q8t, k8t, v_row, e_hbm, inv_total, ctx, ctx_t, wave_t = run_forward(tokens, bits, segs, wq, bq, wb)
    layer_out, g_pre_one, g_ctx_t, tok_t, g_wo, g_wu, g_wd, g_bu, g_small = run_feed_forward(
        tokens, cotangent, ctx, ctx_t, wo, bo, g1, s1, wu, bu, wd, bd, g2, s2
    )
    g_tok, g_wq, g_bq, g_wb = run_backward(
        tok_t, q8t, k8t, v_row, e_hbm, inv_total, ctx_t, g_ctx_t, wave_t, wq, wb, wb.T, g_pre_one
    )

    def scatter(grad):
        part = lax.psum_scatter(grad, "fsdp", scatter_dimension=0, tiled=True)
        return lax.psum(part, "rep").astype(f32)

    p_wq, p_wo, p_wu, p_wd = scatter(g_wq), scatter(g_wo), scatter(g_wu), scatter(g_wd)
    small = [g_bq, g_small[5], g_small[3], g_small[4], g_bu, g_small[2], g_small[0], g_small[1], g_wb]
    rows = jnp.concatenate([s.reshape(fsdp, -1) for s in small], axis=1)
    mine = lax.psum(lax.psum_scatter(rows, "fsdp", scatter_dimension=0, tiled=True), "rep").reshape(-1)
    parts, at = [], 0
    for size in sizes:
        parts.append(mine[at : at + size])
        at += size
    p_bq, p_bo, p_g1, p_s1, p_bu, p_bd, p_g2, p_s2, p_wb = parts
    return (
        layer_out, g_tok, p_wq, p_bq, p_wb.reshape(w_box.shape), p_wo, p_bo, p_g1, p_s1,
        p_wu, p_bu, p_wd, p_bd, p_g2, p_s2,
    )


def solution(mesh):
    tokens = P(("fsdp", "rep"), None)
    matrix, vector = P("fsdp", None), P("fsdp")
    kinds = [matrix, vector, matrix, matrix, vector, vector, vector, matrix, vector, matrix, vector, vector, vector]
    return jax.shard_map(
        functools.partial(per_device, mesh.shape["fsdp"]),
        mesh=mesh,
        in_specs=(tokens, tokens, P(("fsdp", "rep")), P(None, ("fsdp", "rep")), *kinds),
        out_specs=(tokens, tokens, *kinds),
        check_vma=False,
    )
```

time: 1180 us -> 1080 us (0.915)
  waiting for transfers between devices: 388 us -> 833 us
  matrix products: 292 us -> 0 us
  Pallas kernels: 0 us -> 156 us
  blocking collectives: 196 us -> 45.4 us
  local copies, waits for them, and re-layouts: 157 us -> 14.5 us
  other arithmetic: 75 us -> 11.6 us
  loops' own time: 47.6 us -> 0 us
    dot_general x102 -> x0, matrix products: 292 us -> none  [the longest x24 54 us: head_scores(): jnp.einsum('nqd,nkd->nqk', q_head, k_head, preferred_element_type=f32)]
    all_gather x4, waiting for transfers between devices: 0.03 us -> 209 us  [per_device(): lax.all_gather(low(value), 'fsdp', axis=0, tiled=True)]
    pallas_call x0 -> x3, Pallas kernels: none -> 156 us  [the longest x1 78.7 us: run_feed_forward(): pl.pallas_call(feed_forward, out_shape=out_shape, in_specs=in_vmem(14), o...]
    unnamed x2 -> x0, blocking collectives: 155 us -> none
    reduce_scatter x3 -> x4, waiting for transfers between devices: 348 us -> 499 us  [scatter(): part = lax.psum_scatter(grad, 'fsdp', scatter_dimension=0, tiled=True)]
    unnamed x10 -> x11, waiting for transfers between devices: 32.4 us -> 109 us
    unnamed x175 -> x46, local copies, waits for them, and re-layouts: 67 us -> 2.22 us
    another operation x2 -> x0, loops' own time: 47.6 us -> none  [the longest x1 24 us: per_device(): lax.map(backward_head, (jnp.arange(HEADS), log_totals))]
  transfers between devices with their start and end apart: 9 -> 10, of which waited for: 4 -> 10; matrix products, arithmetic and copies ran while one was open for 38% -> 2% of each run, Pallas kernels for 0% -> 7%
where the time goes in v1:
time: 1080 us
  waiting for transfers between devices  833 us (77%)
  Pallas kernels  156 us (14%)
  blocking collectives  45.4 us (4%)
  local copies, waits for them, and re-layouts  14.5 us (1%)
  between operations  14.5 us (1%)
  other arithmetic  11.6 us (1%)
    reduce_scatter x4, waiting for transfers between devices, scatter(): part = lax.psum_scatter(grad, 'fsdp', scatter_dimension=0, tiled=True)  499 us
    all_gather x4, waiting for transfers between devices, per_device(): lax.all_gather(low(value), 'fsdp', axis=0, tiled=True)  209 us
    unnamed x11, waiting for transfers between devices  109 us
    pallas_call x1, Pallas kernels, run_feed_forward(): pl.pallas_call(feed_forward, out_shape=out_shape, in_specs=in_vmem(14), o...  78.7 us
    all_gather x1, blocking collectives, per_device(): table = lax.all_gather(packed, 'fsdp', axis=0, tiled=True)  43 us
    pallas_call x1, Pallas kernels, run_backward(): pl.pallas_call(attend_backward, out_shape=out_shape, in_specs=in_vmem(4)...  41.1 us
    pallas_call x1, Pallas kernels, run_forward(): pl.pallas_call(attend_forward, out_shape=out_shape, in_specs=in_vmem(6),...  35.8 us
  transfers between devices with their start and end apart: 10, of which 10 were waited for; matrix products, arithmetic and copies ran while one was open for 2% of the time, Pallas kernels for 7%

profile of v1, /device:TPU:0, one launch (start us, length us, event | category | flops | bytes accessed | tf_op | source)
XLA Modules:
  0.0 1075.2 jit_solution(16135578176300306407)
XLA Ops:
  7.2 1.8 convert_element_type.100
  9.2 1.6 convert_element_type.113
  10.9 0.7 convert_element_type.120
  11.7 0.7 convert_element_type.123
  12.8 0.1 concatenate.11
  12.9 43.0 %all-gather.1 = bf16[16,1,1152]{2,1,0:T(2,128)(2,1)S(1)} all-gather(bf16[1,1,1152]{2,1,0:T(2,128)(2,1)S(1)} %reshape.205), channel_id=2, replica_groups=mesh['fsdp'=16,'rep'=2] {'fsdp'}, dimensions={0}, use_global_device_ids=true | all-gather | bytes 39168 | tf_op jit(solution)/shard_map/all_gather | solution.py:510
  55.9 0.7 reshape.191.w_box
  56.6 0.7 reshape.196.b_qkv
  57.3 0.6 reshape.189.segs
  58.0 0.7 reshape.197.b_out
  58.7 0.7 reshape.198.gain_one
  59.3 0.7 reshape.199.shift_one
  60.0 0.7 reshape.201.b_down
  60.7 0.7 reshape.202.gain_two
  61.4 0.7 reshape.203.shift_two
  62.1 0.7 reshape.200.b_up
  62.9 0.7 maximum_maximum_fusion.coord_bits
  63.6 21.9 %all-gather.7.cloned.1.call-done.w_qkv = bf16[768,2304]{1,0:T(8,128)(2,1)} async-done(((bf16[48,2304]{1,0:T(8,128)(2,1)}), bf16[768,2304]{1,0:T(8,128)(2,1)}) %all-gather.7.cloned.1.call-update) | async-done | bytes 3538960 | tf_op jit(solution)/shard_map/all_gather | solution.py:503
  85.5 35.8 %attend_forward.1 = (bf16[2,6,128,512]{3,2,1,0:T(8,128)(2,1)}, bf16[2,6,128,512]{3,2,1,0:T(8,128)(2,1)}, bf16[2,6,512,128]{3,2,1,0:T(8,128)(2,1)}, bf16[24,512,5...) custom-call(bf16[1024,768]{1,0:T(8,128)(2,1)} %tok.3, ...), custom_call_target="tpu_custom_call" | custom-call | tf_op jit(solution)/shard_map/attend_forward/pallas_call | solution.py:422
  121.3 22.3 %all-gather.9.cloned.1.call-done.w_out = bf16[768,768]{1,0:T(8,128)(2,1)} async-done(((bf16[48,768]{1,0:T(8,128)(2,1)}), bf16[768,768]{1,0:T(8,128)(2,1)}) %all-gather.9.cloned.1.call-update) | async-done | bytes 1179664 | tf_op jit(solution)/shard_map/all_gather | solution.py:503
  143.6 82.8 %all-gather.11.cloned.1.call-done.w_up = bf16[768,3072]{1,0:T(8,128)(2,1)} async-done(((bf16[48,3072]{1,0:T(8,128)(2,1)}), bf16[768,3072]{1,0:T(8,128)(2,1)}) %all-gather.11.cloned.1.call-update) | async-done | bytes 4718608 | tf_op jit(solution)/shard_map/all_gather | solution.py:503
  226.4 82.3 %all-gather.13.cloned.1.call-done.w_down = bf16[3072,768]{1,0:T(8,128)(2,1)} async-done(((bf16[192,768]{1,0:T(8,128)(2,1)}), bf16[3072,768]{1,0:T(8,128)(2,1)}) %all-gather.13.cloned.1.call-update) | async-done | bytes 4718608 | tf_op jit(solution)/shard_map/all_gather | solution.py:503
  308.7 78.7 %feed_forward.1 = (bf16[1024,768]{1,0:T(8,128)(2,1)}, f32[1024,768]{1,0:T(8,128)}, bf16[768,1024]{1,0:T(8,128)(2,1)}, bf16[768,1024]{1,0:T(8,128)(2,1)}, bf16[76...) custom-call(bf16[1024,768]{1,0:T(8,128)(2,1)} %tok.3, ...), custom_call_target="tpu_custom_call" | custom-call | tf_op jit(solution)/shard_map/feed_forward/pallas_call | solution.py:454
  387.5 0.2 reduce-scatter.5.cloned.1.call-start
  387.7 0.7 copy.36
  388.4 41.1 %attend_backward.1 = (f32[1024,768]{1,0:T(8,128)}, bf16[768,2304]{1,0:T(8,128)(2,1)}, f32[1,2304]{1,0:T(1,128)}, f32[128,64]{1,0:T(8,128)}) custom-call(bf16[768,1024]{1,0:T(8,128)(2,1)} %get-tuple-element.39.tok_t, bf16[2,6,128,512]{3,2,1,0:T(8,128)(2,1)} %get-tuple-element.40.q8t, bf16[2,6,128,512]{3,2,1,0:T(8,128)(2,1)} %get-tuple-element.41.k8t, ...), custom_call_target="tpu_custom_call" | custom-call | tf_op jit(solution)/shard_map/attend_backward/pallas_call | solution.py:482
  429.7 0.7 reduce-scatter.11.cloned.1.call-update
  430.5 0.6 reduce-scatter.9.cloned.1.call-update
  432.0 0.5 broadcast.21
  432.5 0.7 reduce.20
  433.3 0.7 concatenate.12
  434.1 76.6 %reduce-scatter.7.cloned.1.call-done = bf16[48,768]{1,0:T(8,128)(2,1)} async-done(((bf16[768,768]{1,0:T(8,128)(2,1)}), bf16[48,768]{1,0:T(8,128)(2,1)}) %reduce-scatter.7.cloned.1.call-update) | async-done | bytes 73744 | tf_op jit(solution)/shard_map/reduce_scatter | solution.py:529
  510.7 138.2 %reduce-scatter.5.cloned.1.call-done = bf16[48,2304]{1,0:T(8,128)(2,1)} async-done(((bf16[768,2304]{1,0:T(8,128)(2,1)}), bf16[48,2304]{1,0:T(8,128)(2,1)}) %reduce-scatter.5.cloned.1.call-update) | async-done | bytes 221200 | tf_op jit(solution)/shard_map/reduce_scatter | solution.py:529
  648.8 141.8 %reduce-scatter.11.cloned.1.call-done = bf16[192,768]{1,0:T(8,128)(2,1)} async-done(((bf16[3072,768]{1,0:T(8,128)(2,1)}), bf16[192,768]{1,0:T(8,128)(2,1)}) %reduce-scatter.11.cloned.1.call-update) | async-done | bytes 294928 | tf_op jit(solution)/shard_map/reduce_scatter | solution.py:529
  790.7 142.5 %reduce-scatter.9.cloned.1.call-done = bf16[48,3072]{1,0:T(8,128)(2,1)} async-done(((bf16[768,3072]{1,0:T(8,128)(2,1)}), bf16[48,3072]{1,0:T(8,128)(2,1)}) %reduce-scatter.9.cloned.1.call-update) | async-done | bytes 294928 | tf_op jit(solution)/shard_map/reduce_scatter | solution.py:529
  933.2 0.6 dynamic-slice
  933.8 107.7 %all-reduce.5.cloned.1.call-done = f32[16,1136]{1,0:T(8,128)} async-done(((f32[16,1136]{1,0:T(8,128)}), f32[16,1136]{1,0:T(8,128)}) %all-reduce.5.cloned.1.call-update) | async-done | bytes 72720
  1041.4 1.4 constant_dynamic-slice_fusion
  1042.9 2.5 psum.36
  1045.3 0.6 slice.138
  1045.9 0.6 slice.143
  1046.6 0.7 reshape.195
  1047.3 0.6 slice_bitcast_fusion
  1047.9 15.3 %all-reduce.7.cloned.1.call-done = (bf16[48,2304]{1,0:T(8,128)(2,1)}, bf16[48,768]{1,0:T(8,128)(2,1)}, bf16[48,3072]{1,0:T(8,128)(2,1)}, bf16[192,768]{1,0:T(8,128)(2,1)}) async-done(((bf16[48,2304]{1,0:T(8,128)(2,1)}, bf16[48,768]{1,0:T(8,128)(2,1)}, bf16[48,3072]{1,0:T(8,128)(2,1)}, bf16[192,768]{1,0:T(8,128)(2,1)}), (bf16[48,2304]{1,0:T(8,128)(2,1)}, bf16[48,768]{1,0:T(8,128)(2,1)}, ...) | async-done | bytes 884752 | tf_op jit(solution)/shard_map/psum | solution.py:530
  1063.2 1.9 convert_element_type.132
  1065.1 1.8 convert_element_type.133
  1066.9 0.8 convert_element_type.130
  1067.7 0.7 convert_element_type.131
  (91 shorter events, 2.0 us)
Async XLA Ops:
  7.2 3.7 copy-start
  7.2 4.5 copy-start.1
  7.2 78.3 %all-gather.7.cloned.1.call-start = ((), (), s32[]{:S(2)}) async-start(), calls=%async_computation.4 | async-start | bytes 3760128 | tf_op jit(solution)/shard_map/all_gather | solution.py:503
  9.1 3.5 copy-start.10
  9.1 3.6 copy-start.12
  9.1 3.6 copy-start.14
  9.1 3.6 copy-start.15
  9.1 3.6 copy-start.16
  9.1 3.6 copy-start.13
  9.1 3.6 copy-start.17
  9.1 3.6 copy-start.18
  9.1 3.6 copy-start.19
  9.1 48.2 %copy-start.11 = (s32[1024]{0:T(1024)S(1)}, s32[1024]{0:T(1024)}, u32[]{:S(2)}) copy-start(s32[1024]{0:T(1024)} %param.19) | copy-start | bytes 12292
  9.2 53.7 %copy-start.6 = (s32[4,1024]{1,0:T(4,128)S(1)}, s32[4,1024]{1,0:T(4,128)}, u32[]{:S(2)}) copy-start(s32[4,1024]{1,0:T(4,128)} %param.20) | copy-start | bytes 49156
  9.2 134.5 %all-gather.9.cloned.1.call-start = ((), (), s32[]{:S(2)}) async-start(), calls=%async_computation.5 | async-start | bytes 1253376 | tf_op jit(solution)/shard_map/all_gather | solution.py:503
  10.8 215.6 %all-gather.11.cloned.1.call-start = ((), (), s32[]{:S(2)}) async-start(), calls=%async_computation.6 | async-start | bytes 5013504 | tf_op jit(solution)/shard_map/all_gather | solution.py:503
  11.6 297.1 %all-gather.13.cloned.1.call-start = ((), (), s32[]{:S(2)}) async-start(), calls=%async_computation.7 | async-start | bytes 5013504 | tf_op jit(solution)/shard_map/all_gather | solution.py:503
  12.5 498.2 %reduce-scatter.7.cloned.1.call-start = ((), (), s32[]{:S(2)}) async-start(), calls=%async_computation.9 | async-start | bytes 1253376 | tf_op jit(solution)/shard_map/reduce_scatter | solution.py:529
  308.7 79.0 %copy-start.2 = (bf16[128,64]{1,0:T(8,128)(2,1)S(1)}, bf16[128,64]{1,0:T(8,128)(2,1)}, u32[]{:S(2)}) copy-start(bf16[128,64]{1,0:T(8,128)(2,1)} %reshape.191.w_box) | copy-start | bytes 49156
  387.5 261.3 %reduce-scatter.5.cloned.1.call-start = ((), (), s32[]{:S(2)}) async-start(), calls=%async_computation.8 | async-start | bytes 3760128 | tf_op jit(solution)/shard_map/reduce_scatter | solution.py:529
  429.6 361.1 %reduce-scatter.11.cloned.1.call-start = ((), (), s32[]{:S(2)}) async-start(), calls=%async_computation.11 | async-start | bytes 5013504 | tf_op jit(solution)/shard_map/reduce_scatter | solution.py:529
  430.4 502.8 %reduce-scatter.9.cloned.1.call-start = ((), (), s32[]{:S(2)}) async-start(), calls=%async_computation.10 | async-start | bytes 5013504 | tf_op jit(solution)/shard_map/reduce_scatter | solution.py:529
  430.4 0.8 copy-start.5
  430.4 0.9 copy-start.9
  430.4 1.0 copy-start.7
  430.5 2.1 copy-start.8
  430.5 502.7 %copy-start.20 = (u32[32]{0:T(128)S(1)}, u32[32]{0:T(128)}, u32[]{:S(2)}) copy-start(u32[32]{0:T(128)} %constant.11) | copy-start | bytes 388
  431.1 610.3 %all-reduce.5.cloned.1.call-start = ((), (), s32[]{:S(2)}) async-start(), calls=%async_computation.12 | async-start | bytes 147456
  434.0 629.2 %all-reduce.7.cloned.1.call-start = ((), (), s32[]{:S(2)}) async-start(), calls=%async_computation.13 | async-start | bytes 1769472 | tf_op jit(solution)/shard_map/psum | solution.py:530
  1063.2 3.7 copy-start.3
  1063.2 4.5 copy-start.4
Sparse Core Ops, SparseCore 0:
  11.4 74.0 all-gather.6
  88.8 54.7 all-gather.8
  147.0 79.3 all-gather.10
  229.6 79.0 all-gather.12
  387.6 122.9 reduce-scatter.6
  515.6 133.1 reduce-scatter.4
  654.0 136.6 reduce-scatter.10
  796.7 136.4 reduce-scatter.8
  939.2 102.1 all-reduce.4
  1043.9 19.3 all-reduce.6

commit v2 on v1

v2 whole, which is shorter than its diff:
```python
import functools
import math

import jax
import jax.numpy as jnp
from jax import lax
from jax.experimental import pallas as pl
from jax.experimental.pallas import tpu as pltpu
from jax.sharding import PartitionSpec as P

HEADS = 12
HD = 64
FREQ = 16
SLOT = 512
WAVE = 4 * FREQ
PAIR = 2 * HD
QUAD = 4 * HD

f32 = jnp.float32
bf16 = jnp.bfloat16
neg_large = -1e30
eps_norm = 1e-12
scale_factor = 1.0 / math.sqrt(HD)
vmem_limit = 67_000_000


def dot_nn(left, right):
    return lax.dot_general(left, right, (((1,), (0,)), ((), ())), preferred_element_type=f32)


def dot_nt(left, right):
    return lax.dot_general(left, right, (((1,), (1,)), ((), ())), preferred_element_type=f32)


def dot_tn(left, right):
    return lax.dot_general(left, right, (((0,), (0,)), ((), ())), preferred_element_type=f32)


def aligned(index, size):
    return pl.ds(pl.multiple_of(index * size, size), size)


def wave_rows(coord_bits):
    row = lax.broadcasted_iota(jnp.int32, (2 * WAVE, 16), 0)
    col = lax.broadcasted_iota(jnp.int32, (2 * WAVE, 16), 1)
    coord_of = (row % WAVE) // FREQ
    pick = jnp.where(col == coord_of, 32.0, jnp.where(col == coord_of + 4, 1.0, 0.0)).astype(bf16)
    coords = dot_nn(pick, coord_bits)
    rows = lax.broadcasted_iota(jnp.int32, coords.shape, 0)
    freq_index = (rows % FREQ).astype(f32)
    frequency = jnp.exp(-math.log(10000.0) * freq_index / FREQ)
    angle = coords * (100.0 / 1024.0) * frequency
    turns = jnp.floor(angle * (2.0 / math.pi) + 0.5)
    rest = ((angle - turns * 1.5703125) - turns * 4.837512969970703125e-4) - turns * 7.549789954891e-8
    square = rest * rest
    sine = rest + rest * square * (
        -1.6666654611e-1 + square * (8.3321608736e-3 + square * -1.9515295891e-4)
    )
    cosine = 1.0 - 0.5 * square + square * square * (
        4.166664568298827e-2 + square * (-1.388731625493765e-3 + square * 2.443315711809948e-5)
    )
    quadrant = turns.astype(jnp.int32) + jnp.where(rows >= WAVE, 1, 0)
    value = jnp.where((quadrant & 1) == 1, cosine, sine)
    value = jnp.where((quadrant & 2) == 2, -value, value)
    return value.astype(bf16).astype(f32)


def swap_lanes(value):
    return pltpu.roll(value, WAVE, 1)


def gelu_parts(value):
    size = jnp.abs(value) * math.sqrt(0.5)
    t = 1.0 / (1.0 + 0.3275911 * size)
    bell = jnp.exp(-0.5 * value * value)
    tail = t * (
        0.254829592 + t * (-0.284496736 + t * (1.421413741 + t * (-1.453152027 + t * 1.061405429)))
    )
    half_tail = 0.5 * tail * bell
    return jnp.where(value >= 0, 1.0 - half_tail, half_tail), bell * (1.0 / math.sqrt(2.0 * math.pi))


def row_mean(value):
    return jnp.mean(value, axis=-1, keepdims=True)


ROWS = 256
BLOCK = 768
PIECE = 48
HALF = BLOCK // 2
SMALL = 512
STREAMS = 12
VECTORS = 6


def widths(width, ff):
    return 3 * width // 16, ff // 16, width // 16


class Route:
    def __init__(self):
        self.me = lax.axis_index("fsdp")
        self.core = lax.axis_index("rep")
        near_step, far_step = 1 + self.core, 2 - self.core
        near_move = near_step * (1 - 2 * ((self.me // near_step) % 2))
        far_move = far_step * (1 - 2 * ((self.me // far_step) % 2))
        self.near = self.me + near_move
        self.far = self.me + far_move
        self.across = self.me + near_move + far_move

    def column(self, base):
        return [(base + 4 * k) % 16 for k in range(4)]

    def peers(self):
        chips = self.column(self.me)[1:] + [self.near, self.far]
        return [(chip, self.core) for chip in chips] + [(self.me, 1 - self.core)]


def remote(source, target, send, recv, chip, core):
    return pltpu.make_async_remote_copy(
        src_ref=source, dst_ref=target, send_sem=send, recv_sem=recv,
        device_id=(chip, core), device_id_type=pl.DeviceIdType.MESH,
    )


class Streams:
    count = STREAMS

    def __init__(self, held, stage, final, sems):
        self.held, self.stage, self.final = held, stage, final
        self.gather_recv, self.gather_send, self.sum_recv, self.sum_send, self.final_sem = sems

    def window(self, stream, shard, half):
        lower = stream // 8
        row = (1 - lower) * (stream * BLOCK + PIECE * shard) + lower * (
            8 * BLOCK + PIECE * (stream - 8) + 4 * PIECE * shard
        )
        return self.held.at[pl.ds(pl.multiple_of(row, 16), PIECE), pl.ds(pl.multiple_of(half * HALF, HALF), HALF)]

    def several(self, pieces):
        return self.held.at[: PIECE * pieces, :HALF]

    def landing(self, stream, kind, index):
        row = stream * BLOCK + PIECE * (index + (0, 0, 8, 12)[kind])
        column = 0 if kind == 0 else HALF
        return self.stage.at[pl.ds(pl.multiple_of(row, 16), PIECE), column : column + HALF]

    def result(self, stream, half):
        return self.final.at[
            pl.ds(pl.multiple_of(stream * PIECE, 16), PIECE), pl.ds(pl.multiple_of(half * HALF, HALF), HALF)
        ]

    def results(self):
        return self.final.at[:, :HALF]


class Vectors:
    def __init__(self, held, stage, final, sems):
        self.held, self.stage, self.final = held, stage, final
        self.gather_recv, self.gather_send, self.sum_recv, self.sum_send, self.final_sem = sems

    def window(self, stream, shard, half):
        wide = SMALL // 2
        return self.held.at[pl.ds(pl.multiple_of(shard * 8, 8), 8), pl.ds(pl.multiple_of(half * wide, wide), wide)]

    def several(self, pieces):
        if pieces <= 16:
            return self.held.at[: 8 * pieces, : SMALL // 2]
        return self.stage.at[: 8 * pieces, :]

    def landing(self, stream, kind, index):
        row = 8 * (index + (0, 16, 24, 28)[kind])
        return self.stage.at[pl.ds(pl.multiple_of(row, 8), 8), :]

    def result(self, stream, half):
        wide = SMALL // 2
        return self.final.at[:, pl.ds(pl.multiple_of(half * wide, wide), wide)]

    def results(self):
        return self.final.at[:, : SMALL // 2]


def drain(view, sem):
    pltpu.make_async_copy(view, view, sem).wait()


class Exchange:
    def __init__(self, route, parts):
        self.route, self.parts = route, parts


    def share(self, stream, shard, chip, kind):
        p, r = self.parts, self.route
        view = p.window(stream, shard, r.core)
        remote(view, view, p.gather_send.at[stream, 0], p.gather_recv.at[stream, kind], chip, r.core).start()

    def hand_over(self, stream, shard):
        p, r = self.parts, self.route
        view = p.window(stream, shard, r.core)
        remote(view, view, p.gather_send.at[stream, 1], p.gather_recv.at[stream, 3], r.me, 1 - r.core).start()

    def gather_own(self, stream):
        r = self.route
        for peer in r.column(r.me)[1:]:
            self.share(stream, r.me, peer, 0)
        self.share(stream, r.me, r.near, 1)
        self.share(stream, r.me, r.far, 2)

    def gather_column(self, stream):
        p, r = self.parts, self.route
        drain(p.several(3), p.gather_recv.at[stream, 0])
        for shard in r.column(r.me)[1:]:
            self.share(stream, shard, r.near, 1)
            self.share(stream, shard, r.far, 2)
        for shard in r.column(r.me)[1:]:
            self.hand_over(stream, shard)

    def gather_near(self, stream):
        p, r = self.parts, self.route
        drain(p.several(4), p.gather_recv.at[stream, 1])
        for shard in r.column(r.near):
            self.share(stream, shard, r.far, 2)
        for shard in r.column(r.near):
            self.hand_over(stream, shard)

    def gather_far(self, stream):
        p, r = self.parts, self.route
        drain(p.several(8), p.gather_recv.at[stream, 2])
        for shard in r.column(r.far) + r.column(r.across):
            self.hand_over(stream, shard)

    def gathered(self, stream):
        p = self.parts
        drain(p.several(15), p.gather_recv.at[stream, 3])

    def gather_sent(self, stream):
        p = self.parts
        drain(p.several(15), p.gather_send.at[stream, 0])
        drain(p.several(15), p.gather_send.at[stream, 1])


    def add(self, stream, shard, kind, index):
        p, r = self.parts, self.route
        view = p.window(stream, shard, r.core)
        landed = p.landing(stream, kind, index)
        view[...] = (view[...].astype(f32) + landed[...].astype(f32)).astype(view.dtype)

    def pass_on(self, stream, shard, kind, index, chip):
        p, r = self.parts, self.route
        remote(
            p.window(stream, shard, r.core), p.landing(stream, kind, index),
            p.sum_send.at[stream], p.sum_recv.at[stream, kind], chip, r.core,
        ).start()

    def sum_cores(self, stream):
        p, r = self.parts, self.route
        for shard in range(16):
            remote(
                p.window(stream, shard, 1 - r.core), p.landing(stream, 0, shard),
                p.sum_send.at[stream], p.sum_recv.at[stream, 0], r.me, 1 - r.core,
            ).start()

    def sum_far(self, stream):
        p, r = self.parts, self.route
        drain(p.several(16), p.sum_recv.at[stream, 0])
        leaving = r.column(r.far) + r.column(r.across)
        for index, shard in enumerate(leaving):
            self.add(stream, shard, 0, shard)
        for index, shard in enumerate(leaving):
            self.pass_on(stream, shard, 1, index, r.far)
        for shard in r.column(r.me) + r.column(r.near):
            self.add(stream, shard, 0, shard)

    def sum_near(self, stream):
        p, r = self.parts, self.route
        drain(p.several(8), p.sum_recv.at[stream, 1])
        for index, shard in enumerate(r.column(r.near)):
            self.add(stream, shard, 1, 4 + index)
        for index, shard in enumerate(r.column(r.near)):
            self.pass_on(stream, shard, 2, index, r.near)
        for index, shard in enumerate(r.column(r.me)):
            self.add(stream, shard, 1, index)

    def sum_column(self, stream):
        p, r = self.parts, self.route
        drain(p.several(4), p.sum_recv.at[stream, 2])
        shards = r.column(r.me)
        for index in range(1, 4):
            self.add(stream, shards[index], 2, index)
        for index in range(1, 4):
            self.pass_on(stream, shards[index], 3, index - 1, shards[index])
        self.add(stream, shards[0], 2, 0)

    def sum_end(self, stream):
        p, r = self.parts, self.route
        drain(p.several(3), p.sum_recv.at[stream, 3])
        total = p.window(stream, r.me, r.core)[...].astype(f32)
        for index in range(3):
            total += p.landing(stream, 3, index)[...].astype(f32)
        view = p.result(stream, r.core)
        view[...] = total
        remote(view, view, p.final_sem.at[0], p.final_sem.at[1], r.me, 1 - r.core).start()

    def summed(self, stream):
        p = self.parts
        drain(p.several(31), p.sum_send.at[stream])

    def results_in(self):
        p = self.parts
        drain(p.results(), p.final_sem.at[0])
        drain(p.results(), p.final_sem.at[1])


def owner_tables(start, share, depth, order=None):
    col = lax.broadcasted_iota(jnp.int32, (depth, BLOCK), 1) + start
    source = col if order is None else order(col)
    pick = (source % share == lax.broadcasted_iota(jnp.int32, (depth, BLOCK), 0)).astype(bf16)
    col = lax.broadcasted_iota(jnp.int32, (128, BLOCK), 1) + start
    row = lax.broadcasted_iota(jnp.int32, (128, BLOCK), 0)
    source = col if order is None else order(col)
    return pick, source // share == row // 8, row % 8


def quad_order(col):
    return (col % BLOCK) // QUAD * BLOCK + col // BLOCK * QUAD + col % QUAD


def layer_kernel(comm, *refs):
    refs = list(refs)

    def take(count):
        taken, refs[:] = refs[:count], refs[count:]
        return taken

    tok_in, cot_in, bits, segs = take(4)
    if comm:
        w_qkv_in, w_out_in, w_up_in, w_down_in = take(4)
        small_in = take(9)
    else:
        held_in, w_box_in, b_qkv_in, b_up_in, vectors_in = take(5)
    layer_out, g_tok_out, e_hbm = take(3)
    if comm:
        p_qkv, p_out, p_up, p_down, p_small = take(5)
    else:
        g_held, g_w_box_out, g_b_qkv_out, g_b_up_out, g_vectors_out = take(5)
    (held, stage, slope, q8t, k8t, v_row, ctx_t, wave_t, wave_r, e_buf, normed, total, flip, g_down, tok_t, g_ctx_t,
     inv_one, inv_total, w_box, w_box_t, b_qkv, b_up, vectors, g_w_box, g_b_qkv, g_b_up, g_vectors, e_sem, io_sem) = take(29)
    if comm:
        final, small, small_stage, g_small, mid_sem = take(5)
        block_sems, small_sems, small_final_sems = take(5), take(4), take(1)

    count, width = tok_t.shape[1], tok_t.shape[0]
    ff = slope.shape[0] // count * BLOCK
    slots, pairs = count // SLOT, HEADS // 2
    row_blocks = count // ROWS
    up_blocks = ff // BLOCK
    quads = pairs // 2
    act = stage.at[: up_blocks * count]
    ctx = stage.at[up_blocks * count : (up_blocks + 1) * count]
    low = stage.at[(up_blocks + 1) * count : (up_blocks + 2) * count]
    cot = stage.at[(up_blocks + 2) * count : (up_blocks + 3) * count]
    tok = stage.at[(up_blocks + 3) * count : (up_blocks + 4) * count]
    up_at, down_at = 4 * BLOCK, 8 * BLOCK

    def copy_in(source, target, index=0):
        return pltpu.make_async_copy(source, target, io_sem.at[index])

    tok_copy = copy_in(tok_in, tok, 0)
    cot_copy = copy_in(cot_in, cot, 1)
    tok_copy.start()
    cot_copy.start()

    if comm:
        route = Route()
        blocks = Exchange(route, Streams(held, stage, final, block_sems))
        extras = Exchange(route, Vectors(small, small_stage, p_small, [*small_sems, *small_final_sems]))
        sums = Exchange(route, Vectors(g_small, small_stage, p_small, [*small_sems, *small_final_sems]))
        barrier = pltpu.get_barrier_semaphore()
        for chip, core in route.peers():
            pl.semaphore_signal(barrier, inc=1, device_id=(chip, core), device_id_type=pl.DeviceIdType.MESH)
        moves = []
        for quad in range(quads):
            for part in range(3):
                moves.append((
                    w_qkv_in.at[:, part * width + quad * QUAD : part * width + (quad + 1) * QUAD],
                    total.at[quad * PIECE : (quad + 1) * PIECE, part * QUAD : (part + 1) * QUAD],
                ))
        moves.append((w_out_in, total.at[3 * PIECE : 4 * PIECE]))
        for block in range(up_blocks):
            moves.append((
                w_up_in.at[:, block * BLOCK : (block + 1) * BLOCK],
                total.at[(4 + block) * PIECE : (5 + block) * PIECE],
            ))
        moves.append((w_down_in, total.at[8 * PIECE : 12 * PIECE]))
        for index, (source, target) in enumerate(moves):
            copy_in(source, target, 2 + index).start()
        small_in = [ref[...].astype(bf16).astype(f32) for ref in small_in]
        g_small[:8, :] = jnp.zeros((8, SMALL), f32)
        g_small[:8, :HD] = small_in[8]
        for row in range(8):
            value = small_in[row]
            g_small[row : row + 1, 128 : 128 + value.shape[1]] = value
        small[pl.ds(pl.multiple_of(route.me * 8, 8), 8), :] = g_small[:8, :]
        for index, (source, target) in enumerate(moves):
            copy_in(source, target, 2 + index).wait()
        for block in range(STREAMS - up_blocks):
            at = pl.ds(pl.multiple_of(block * BLOCK + PIECE * route.me, 16), PIECE)
            held[at, :] = total[block * PIECE : (block + 1) * PIECE, :].astype(bf16)
        at = pl.ds(pl.multiple_of(down_at + 4 * PIECE * route.me, 16), 4 * PIECE)
        held[at, :] = total[8 * PIECE : 12 * PIECE, :].astype(bf16)
        pl.semaphore_wait(barrier, 6)
        extras.gather_own(0)
        for stream in range(4):
            blocks.gather_own(stream)
    else:
        copy_in(held_in, held, 2).start()
        w_box[...] = w_box_in[...]
        b_qkv[...] = b_qkv_in[...]
        b_up[...] = b_up_in[...]
        vectors[...] = vectors_in[...]

    wave_t[...] = wave_rows(bits[...])
    wave_r[...] = jnp.transpose(wave_t[...])
    for slot in range(slots):
        seg_i = jnp.broadcast_to(segs[slot : slot + 1, :].astype(f32), (SLOT, SLOT))
        seg_j = jnp.transpose(seg_i)
        normed[slot * SLOT : (slot + 1) * SLOT, :SLOT] = jnp.where(seg_i == seg_j, 0.0, neg_large)
    g_w_box[...] = jnp.zeros_like(g_w_box)
    g_b_up[...] = jnp.zeros_like(g_b_up)
    g_vectors[...] = jnp.zeros_like(g_vectors)
    tok_copy.wait()

    if comm:
        extras.gather_column(0)
        blocks.gather_column(0)
        extras.gather_near(0)
        blocks.gather_near(0)
        blocks.gather_column(1)
        extras.gather_far(0)
        blocks.gather_far(0)
        blocks.gather_near(1)
        blocks.gather_column(2)
        extras.gathered(0)
        table = small[...].astype(bf16)
        w_box[...] = table[:, :HD]
        share_qkv, share_up, share = widths(width, ff)
        for row, columns, share_of, depth, order, target in (
            (0, 3 * width, share_qkv, 256, quad_order, b_qkv),
            (1, ff, share_up, 256, None, b_up),
            (None, width, share, 128, None, vectors),
        ):
            @pl.loop(0, columns // BLOCK)
            def _(block):
                pick, owned, row_of = owner_tables(block * BLOCK, share_of, depth, order)
                spread = dot_nn(table[:, 128 : 128 + depth], pick)
                keep = owned if row is None else owned & (row_of == row)
                rows = jnp.sum(jnp.where(keep, spread, 0.0).reshape(16, 8, BLOCK), axis=0)
                target[:, aligned(block, BLOCK)] = rows if row is None else jnp.sum(rows, axis=0, keepdims=True)

    else:
        copy_in(held_in, held, 2).wait()
    w_box_t[...] = jnp.transpose(w_box[...].astype(f32)).astype(bf16)

    def gather_tick(step):
        if not comm:
            return
        for ahead, act_on in enumerate((blocks.gather_far, blocks.gather_near, blocks.gather_column, blocks.gather_own)):
            pl.when(step + ahead < STREAMS)(functools.partial(act_on, step + ahead))

    def need(stream):
        if comm:
            blocks.gathered(stream)

    b_out, gain_one, shift_one, b_down, gain_two, shift_two = [vectors[2 + i : 3 + i, :] for i in range(VECTORS)]
    lane = lax.broadcasted_iota(jnp.int32, (SLOT, PAIR), 1)

    def project(quad, slot):
        rows = tok[aligned(slot, SLOT), :]

        def columns(part):
            weight = held[aligned(quad, BLOCK), part * QUAD : (part + 1) * QUAD]
            shift = b_qkv[:, pl.ds(pl.multiple_of(quad * BLOCK + part * QUAD, QUAD), QUAD)]
            return (dot_nn(rows, weight) + shift).astype(bf16)

        q, k, v = columns(0), columns(1), columns(2)
        low[aligned(slot, SLOT), aligned(quad, QUAD)] = k
        flip[aligned(quad, QUAD), aligned(slot, SLOT)] = jnp.transpose(v.astype(f32)).astype(bf16)
        qt = jnp.transpose(q.astype(f32) * scale_factor).astype(bf16)
        kt = jnp.transpose(k.astype(f32) * scale_factor).astype(bf16)
        for part in range(2):
            here = slice(part * PAIR, (part + 1) * PAIR)
            q8t[slot, quad * 2 + part] = qt[here]
            k8t[slot, quad * 2 + part] = kt[here]
            v_row[slot, quad * 2 + part] = v[:, here]

    def e_copy(place, head, index, out):
        pair = (e_buf.at[place, head], e_hbm.at[index])
        return pltpu.make_async_copy(*(pair if out else pair[::-1]), e_sem.at[place, head])

    def attend(step):
        pair, slot = step // slots, step % slots
        cols = aligned(slot, SLOT)
        place = step % 2

        @pl.when(step >= 2)
        def _():
            for head in range(2):
                e_copy(place, head, 0, True).wait()

        sine_t, cosine_t = wave_t[:WAVE, cols], wave_t[WAVE:, cols]
        sc_t = (wave_t[:, cols] * scale_factor).astype(bf16)
        sc_r = wave_r[cols, :]
        cs_r = swap_lanes(sc_r)
        cc_r = jnp.where(lane < WAVE, cs_r, sc_r)
        ss_r = jnp.where(lane < WAVE, sc_r, -cs_r)
        cs_low = cs_r.astype(bf16)
        keys = low[cols, aligned(pair, PAIR)]
        heads_t = []
        for head in range(2):
            span = slice(head * HD, (head + 1) * HD)
            key_box = dot_nt(keys[:, span], w_box[...])
            k_side = (key_box * cc_r + swap_lanes(key_box) * ss_r).astype(bf16)
            q_t = q8t[slot, pair, span, :]
            query_box = dot_nn(w_box[...], q_t)
            first, second = query_box[:WAVE], query_box[WAVE:]
            q_side = jnp.concatenate(
                [first * sine_t + second * cosine_t, second * sine_t - first * cosine_t], axis=0
            ).astype(bf16)
            zero = jnp.zeros_like(q_t)
            q_pair = [q_t, zero] if head == 0 else [zero, q_t]
            k_full = jnp.concatenate([keys, cs_low, k_side], axis=1)
            q_full = jnp.concatenate(q_pair + [q_side, sc_t], axis=0)
            scores = dot_nn(k_full, q_full) + normed[cols, :SLOT]
            top = jnp.max(scores, axis=0, keepdims=True)
            exps = jnp.exp(scores - top)
            inverse = 1.0 / jnp.sum(exps, axis=0, keepdims=True)
            low_exps = exps.astype(bf16)
            e_buf[place, head] = low_exps
            e_copy(place, head, step * 2 + head, True).start()
            inv_total[step * 2 + head] = inverse
            at = pl.ds(pl.multiple_of(pair * PAIR + head * HD, HD), HD)
            heads_t.append(dot_nn(flip[at, cols], low_exps) * inverse)
        both = jnp.concatenate(heads_t, axis=0)
        ctx_t[aligned(pair, PAIR), cols] = both.astype(bf16)
        ctx[cols, aligned(pair, PAIR)] = jnp.transpose(both).astype(bf16)

    steps = slots * pairs
    quad_steps = 2 * slots

    @pl.loop(0, quads)
    def _(quad):
        need(quad)

        @pl.loop(0, slots)
        def _(slot):
            project(quad, slot)

        @pl.loop(0, quad_steps)
        def _(inner):
            step = quad * quad_steps + inner
            if comm:
                pl.when(step % 2 == 1)(functools.partial(gather_tick, (step + 1) // 2))
            attend(step)

    for place in range(2):
        for head in range(2):
            e_copy(place, head, 0, True).wait()

    def column_sum(value):
        return jnp.sum(value, axis=0, keepdims=True)

    need(3)
    gather_tick(7)

    @pl.loop(0, row_blocks)
    def _(block):
        rows = aligned(block, ROWS)
        token_rows = tok[rows, :].astype(f32)
        tok_t[:, rows] = jnp.transpose(token_rows).astype(bf16)
        pre = token_rows + dot_nn(ctx[rows, :], held[3 * BLOCK : 4 * BLOCK, :]) + b_out
        center = pre - row_mean(pre)
        invdev = lax.rsqrt(row_mean(center * center) + eps_norm)
        unit = center * invdev
        inv_one[rows, :] = jnp.broadcast_to(invdev, (ROWS, 128))
        normed[rows, :] = unit
        hidden = unit * gain_one + shift_one
        low[rows, :] = hidden.astype(bf16)
        flip[:, rows] = jnp.transpose(hidden).astype(bf16)

    @pl.loop(0, up_blocks)
    def _(block):
        gather_tick(8 + block)
        need(4 + block)

        @pl.loop(0, row_blocks)
        def _(row):
            rows = aligned(row, ROWS)
            at = pl.ds(pl.multiple_of(block * count + row * ROWS, ROWS), ROWS)
            weight = held[pl.ds(pl.multiple_of(up_at + block * BLOCK, BLOCK), BLOCK), :]
            up = dot_nn(low[rows, :], weight) + b_up[:, aligned(block, BLOCK)]
            cdf, pdf = gelu_parts(up)
            act[at, :] = (up * cdf).astype(bf16)
            slope[at, :] = (cdf + up * pdf).astype(bf16)

    for block in range(up_blocks):
        need(8 + block)
    cot_copy.wait()

    @pl.loop(0, row_blocks)
    def _(block):
        rows = aligned(block, ROWS)
        pre = normed[rows, :] * gain_one + shift_one + b_down
        for part in range(up_blocks):
            at = pl.ds(pl.multiple_of(part * count + block * ROWS, ROWS), ROWS)
            pre += dot_nn(act[at, :], held[down_at + part * BLOCK : down_at + (part + 1) * BLOCK, :])
        center = pre - row_mean(pre)
        invdev = lax.rsqrt(row_mean(center * center) + eps_norm)
        unit = center * invdev
        grad = cot[rows, :].astype(f32)
        cot[rows, :] = (unit * gain_two + shift_two).astype(bf16)
        scaled = grad * gain_two
        g_pre = invdev * (scaled - row_mean(scaled) - unit * row_mean(scaled * unit))
        total[rows, :] = g_pre
        low_pre = g_pre.astype(bf16)
        g_down[rows, :] = low_pre
        g_vectors[5:6, :] += column_sum(low_pre.astype(f32))
        g_vectors[6:7, :] += column_sum(grad * unit)
        g_vectors[7:8, :] += column_sum(grad)

    out_copy = pltpu.make_async_copy(cot, layer_out, io_sem.at[0])
    out_copy.start()
    if comm:
        for stream in range(STREAMS):
            blocks.gather_sent(stream)
        extras.gather_sent(0)

    @pl.loop(0, up_blocks)
    def _(block):
        down_rows = pl.ds(pl.multiple_of(down_at + block * BLOCK, BLOCK), BLOCK)

        @pl.loop(0, row_blocks)
        def _(row):
            rows = aligned(row, ROWS)
            at = pl.ds(pl.multiple_of(block * count + row * ROWS, ROWS), ROWS)
            g_act = dot_nt(g_down[rows, :], held[down_rows, :])
            g_up = (g_act * slope[at, :].astype(f32)).astype(bf16)
            slope[at, :] = g_up
            g_b_up[:, aligned(block, BLOCK)] += column_sum(g_up.astype(f32))

        @pl.loop(0, BLOCK // ROWS)
        def _(part):
            at = pl.ds(pl.multiple_of(down_at + block * BLOCK + part * ROWS, ROWS), ROWS)
            held[at, :] = dot_tn(act[aligned(block, count), aligned(part, ROWS)], g_down[...]).astype(bf16)

    out_copy.wait()

    def last(step):
        return STREAMS - 1 - step

    def sum_start(step):
        if comm:
            blocks.sum_cores(last(step))

    def sum_tick(step):
        if not comm:
            return
        for behind, act_on in enumerate((blocks.sum_far, blocks.sum_near, blocks.sum_column, blocks.sum_end)):
            at = step - behind
            if isinstance(at, int):
                if 0 <= at < STREAMS:
                    act_on(last(at))
            else:
                pl.when((at >= 0) & (at < STREAMS))(functools.partial(act_on, last(at)))

    if comm:
        for chip, core in route.peers():
            pl.semaphore_signal(mid_sem, inc=1, device_id=(chip, core), device_id_type=pl.DeviceIdType.MESH)
        pl.semaphore_wait(mid_sem, 6)

    for step in range(up_blocks):
        sum_start(step)

    @pl.loop(0, up_blocks)
    def _(index):
        block = up_blocks - 1 - index
        up_rows = pl.ds(pl.multiple_of(up_at + block * BLOCK, BLOCK), BLOCK)

        @pl.loop(0, row_blocks)
        def _(row):
            rows = aligned(row, ROWS)
            at = pl.ds(pl.multiple_of(block * count + row * ROWS, ROWS), ROWS)
            total[rows, :] += dot_nt(slope[at, :], held[up_rows, :])

        @pl.loop(0, BLOCK // ROWS)
        def _(part):
            at = pl.ds(pl.multiple_of(up_at + block * BLOCK + part * ROWS, ROWS), ROWS)
            held[at, :] = dot_nn(flip[aligned(part, ROWS), :], slope[aligned(block, count), :]).astype(bf16)

        sum_start(up_blocks + index)
        sum_tick(index)

    @pl.loop(0, row_blocks)
    def _(block):
        rows = aligned(block, ROWS)
        grad, unit = total[rows, :], normed[rows, :]
        scaled = grad * gain_one
        g_pre = inv_one[rows, :1] * (scaled - row_mean(scaled) - unit * row_mean(scaled * unit))
        total[rows, :] = g_pre
        low_pre = g_pre.astype(bf16)
        g_down[rows, :] = low_pre
        g_vectors[2:3, :] += column_sum(low_pre.astype(f32))
        g_vectors[3:4, :] += column_sum(grad * unit)
        g_vectors[4:5, :] += column_sum(grad)
        g_ctx_t[:, rows] = dot_nt(held[3 * BLOCK : 4 * BLOCK, :], low_pre).astype(bf16)

    @pl.loop(0, BLOCK // ROWS)
    def _(part):
        at = pl.ds(pl.multiple_of(3 * BLOCK + part * ROWS, ROWS), ROWS)
        held[at, :] = dot_nn(ctx_t[aligned(part, ROWS), :], g_down[...]).astype(bf16)

    sum_start(8)
    sum_tick(4)

    def e_step(order):
        quad = quads - 1 - order // quad_steps
        return quad * quad_steps + order % quad_steps

    def fetch(order):
        for head in range(2):
            e_copy(order % 2, head, e_step(order) * 2 + head, False).start()

    fetch(0)
    ones = jnp.ones((16, count), bf16)

    def attend_back(order):
        step = e_step(order)
        pair, slot = step // slots, step % slots
        cols = aligned(slot, SLOT)
        place = order % 2

        @pl.when(order + 1 < steps)
        def _():
            fetch(order + 1)

        for head in range(2):
            e_copy(place, head, 0, False).wait()
        sine_t, cosine_t = wave_t[:WAVE, cols], wave_t[WAVE:, cols]
        sc_t = (wave_t[:, cols] * scale_factor).astype(bf16)
        cs_t = (jnp.concatenate([cosine_t, sine_t], axis=0) * scale_factor).astype(bf16)
        values = v_row[slot, pair]
        g_parts = [[], [], []]
        for head in range(2):
            span = slice(head * HD, (head + 1) * HD)
            at = pl.ds(pl.multiple_of(pair * PAIR + head * HD, HD), HD)
            g_rows = g_ctx_t[at, cols].astype(f32) * inv_total[step * 2 + head]
            row_dot = jnp.sum(g_rows * ctx_t[at, cols].astype(f32), axis=0, keepdims=True)
            g_low = g_rows.astype(bf16)
            zero = jnp.zeros_like(g_low)
            g_pair = jnp.concatenate([g_low, zero] if head == 0 else [zero, g_low], axis=0)
            low_exps = e_buf[place, head]
            g_probs = dot_nn(values, g_pair)
            g_scores = (low_exps.astype(f32) * (g_probs - row_dot)).astype(bf16)
            g_parts[2].append(dot_nt(g_low, low_exps))
            k_t, q_t = k8t[slot, pair, span, :], q8t[slot, pair, span, :]
            g_q = dot_nn(jnp.concatenate([k_t, cs_t], axis=0), g_scores)
            g_k = dot_nt(jnp.concatenate([q_t, sc_t], axis=0), g_scores)
            first, second = g_q[HD : HD + WAVE], g_q[HD + WAVE :]
            g_qbox = jnp.concatenate(
                [first * sine_t - second * cosine_t, first * cosine_t + second * sine_t], axis=0
            ).astype(bf16)
            first, second = g_k[HD : HD + WAVE], g_k[HD + WAVE :]
            g_kbox = jnp.concatenate(
                [first * cosine_t - second * sine_t, first * sine_t + second * cosine_t], axis=0
            ).astype(bf16)
            g_parts[0].append(g_q[:HD] + dot_nn(w_box_t[...], g_qbox))
            g_parts[1].append(g_k[:HD] + dot_nn(w_box_t[...], g_kbox))
            g_w_box[...] += dot_nt(g_qbox, q_t) + dot_nt(g_kbox, k_t)
        for part in range(3):
            at = pl.ds(pl.multiple_of(part * QUAD + pair % 2 * PAIR, PAIR), PAIR)
            flip[at, cols] = jnp.concatenate(g_parts[part], axis=0).astype(bf16)

    def token_grad(quad):
        @pl.loop(0, row_blocks)
        def _(block):
            rows = aligned(block, ROWS)
            part = dot_nn(held[aligned(quad, BLOCK), :], flip[:, rows])
            total[rows, :] += jnp.transpose(part)

    @pl.loop(0, quads)
    def _(turn):
        quad = quads - 1 - turn

        @pl.loop(0, quad_steps)
        def _(inner):
            order = turn * quad_steps + inner
            if comm:
                pl.when(order % 2 == 1)(functools.partial(sum_tick, 5 + order // 2))
            attend_back(order)

        token_grad(quad)

        @pl.loop(0, BLOCK // ROWS)
        def _(part):
            at = pl.ds(pl.multiple_of(quad * BLOCK + part * ROWS, ROWS), ROWS)
            held[at, :] = dot_nt(tok_t[aligned(part, ROWS), :], flip[...]).astype(bf16)

        g_b_qkv[:, aligned(quad, BLOCK)] = dot_nt(ones, flip[...])[:1]
        sum_start(9 + turn)

    g_w_box[...] = g_w_box[...] * (1.0 / scale_factor)
    tok_out = pltpu.make_async_copy(total, g_tok_out, io_sem.at[0])
    tok_out.start()

    if comm:
        g_small[...] = jnp.zeros_like(g_small)
        g_small[:, :HD] = g_w_box[...]
        share_qkv, share_up, share = widths(width, ff)
        for row, columns, share_of, order, source in (
            (0, 3 * width, share_qkv, quad_order, g_b_qkv),
            (1, ff, share_up, None, g_b_up),
            (None, width, share, None, g_vectors),
        ):
            @pl.loop(0, columns // BLOCK)
            def _(block):
                pick, owned, row_of = owner_tables(block * BLOCK, share_of, 256, order)
                keep = owned if row is None else owned & (row_of == row)
                wide = 1 if row is not None else 8
                full = source[:, aligned(block, BLOCK)].reshape(1, wide, BLOCK)
                spread = jnp.broadcast_to(full, (16, 8, BLOCK)).reshape(128, BLOCK)
                spread = jnp.where(keep, spread, 0.0)
                upper = spread.astype(bf16)
                g_small[:, 128:384] += dot_nt(upper, pick) + dot_nt((spread - upper.astype(f32)).astype(bf16), pick)

        sums.sum_cores(0)
        sum_tick(11)
        sums.sum_far(0)
        sum_tick(12)
        sums.sum_near(0)
        sum_tick(13)
        sums.sum_column(0)
        sum_tick(14)
        sums.sum_end(0)
        for stream in range(STREAMS):
            blocks.summed(stream)
        sums.summed(0)
        blocks.results_in()
        sums.results_in()
        moves = []
        for quad in range(quads):
            for part in range(3):
                moves.append((
                    final.at[quad * PIECE : (quad + 1) * PIECE, part * QUAD : (part + 1) * QUAD],
                    p_qkv.at[:, part * width + quad * QUAD : part * width + (quad + 1) * QUAD],
                ))
        moves.append((final.at[3 * PIECE : 4 * PIECE], p_out))
        for block in range(up_blocks):
            moves.append((
                final.at[(4 + block) * PIECE : (5 + block) * PIECE],
                p_up.at[:, block * BLOCK : (block + 1) * BLOCK],
            ))
        moves.append((final.at[8 * PIECE : 12 * PIECE], p_down))
        for index, (source, target) in enumerate(moves):
            copy_in(source, target, 2 + index).start()
        for index, (source, target) in enumerate(moves):
            copy_in(source, target, 2 + index).wait()
    else:
        g_w_box_out[...] = g_w_box[...]
        g_b_qkv_out[...] = g_b_qkv[...]
        g_b_up_out[...] = g_b_up[...]
        g_vectors_out[...] = g_vectors[...]
        out = copy_in(held, g_held, 2)
        out.start()
        out.wait()
    tok_out.wait()


def shaped(shape, dtype):
    return jax.ShapeDtypeStruct(shape, dtype)


def in_vmem(count):
    return [pl.BlockSpec(memory_space=pltpu.VMEM)] * count


def in_hbm(count):
    return [pl.BlockSpec(memory_space=pl.ANY)] * count


def run_layer(comm, tokens, cotangent, bits, segs, big, little, shard_shapes):
    count, width = tokens.shape
    ff = 4 * BLOCK
    slots, pairs = count // SLOT, HEADS // 2
    held_shape = (STREAMS * BLOCK, BLOCK)
    out_shape = [
        shaped((count, width), bf16),
        shaped((count, width), f32),
        shaped((slots * HEADS, SLOT, SLOT), bf16),
    ]
    out_specs = in_hbm(3)
    if comm:
        out_shape += [shaped(shape, f32) for shape in shard_shapes] + [shaped((8, SMALL), f32)]
        out_specs += in_hbm(4) + in_vmem(1)
    else:
        out_shape += [shaped(held_shape, bf16), shaped((2 * WAVE, HD), f32), shaped((1, 3 * width), f32)]
        out_shape += [shaped((1, ff), f32), shaped((8, width), f32)]
        out_specs += in_hbm(1) + in_vmem(4)
    vmem = pltpu.VMEM
    dma = pltpu.SemaphoreType.DMA
    scratch = [
        vmem(held_shape, bf16),
        vmem(held_shape, bf16),
        vmem((ff // BLOCK * count, BLOCK), bf16),
        vmem((slots, pairs, PAIR, SLOT), bf16),
        vmem((slots, pairs, PAIR, SLOT), bf16),
        vmem((slots, pairs, SLOT, PAIR), bf16),
        vmem((width, count), bf16),
        vmem((2 * WAVE, count), f32),
        vmem((count, 2 * WAVE), f32),
        vmem((2, 2, SLOT, SLOT), bf16),
        vmem((count, width), f32),
        vmem((count, width), f32),
        vmem((width, count), bf16),
        vmem((count, width), bf16),
        vmem((width, count), bf16),
        vmem((width, count), bf16),
        vmem((count, 128), f32),
        vmem((slots * HEADS, 1, SLOT), f32),
        vmem((2 * WAVE, HD), bf16),
        vmem((HD, 2 * WAVE), bf16),
        vmem((1, 3 * width), f32),
        vmem((1, ff), f32),
        vmem((8, width), f32),
        vmem((2 * WAVE, HD), f32),
        vmem((1, 3 * width), f32),
        vmem((1, ff), f32),
        vmem((8, width), f32),
        dma((2, 2)),
        dma((20,)),
    ]
    if comm:
        scratch += [
            vmem((STREAMS * PIECE, BLOCK), f32),
            vmem((128, SMALL), f32),
            vmem((256, SMALL // 2), f32),
            vmem((128, SMALL), f32),
            pltpu.SemaphoreType.REGULAR,
            dma((STREAMS, 4)), dma((STREAMS, 2)), dma((STREAMS, 4)), dma((STREAMS,)), dma((2,)),
            dma((1, 4)), dma((1, 2)), dma((1, 4)), dma((1,)),
            dma((2,)),
        ]
        extra = dict(collective_id=0, has_side_effects=True)
    else:
        extra = {}
    return pl.pallas_call(
        functools.partial(layer_kernel, comm),
        out_shape=out_shape,
        in_specs=in_hbm(2) + in_vmem(2) + in_hbm(len(big)) + in_vmem(len(little)),
        out_specs=out_specs,
        scratch_shapes=scratch,
        compiler_params=pltpu.CompilerParams(vmem_limit_bytes=vmem_limit, **extra),
        name="layer",
    )(tokens, cotangent, bits, segs, *big, *little)


def to_blocks(w_qkv, w_out, w_up, w_down):
    width = w_out.shape[1]
    qkv = w_qkv.reshape(width, 3, width // QUAD, QUAD).transpose(2, 0, 1, 3).reshape(-1, BLOCK)
    up = w_up.reshape(width, -1, BLOCK).transpose(1, 0, 2).reshape(-1, BLOCK)
    return jnp.concatenate([qkv, w_out, up, w_down], axis=0)


def from_blocks(held, width):
    qkv = held[: 3 * BLOCK].reshape(width // QUAD, width, 3, QUAD).transpose(1, 2, 0, 3).reshape(width, -1)
    up = held[4 * BLOCK : 8 * BLOCK].reshape(-1, width, BLOCK).transpose(1, 0, 2).reshape(width, -1)
    return qkv, held[3 * BLOCK : 4 * BLOCK], up, held[8 * BLOCK :]


def per_device(
    mesh_shape, tokens, cotangent, segments, box_coords, w_qkv, b_qkv, w_box, w_out, b_out, gain_one, shift_one,
    w_up, b_up, w_down, b_down, gain_two, shift_two,
):
    count, width = tokens.shape
    bits = jnp.concatenate([box_coords >> 5, box_coords & 31, jnp.zeros((8, count), jnp.int32)], axis=0).astype(bf16)
    segs = segments.reshape(-1, SLOT)
    vectors = [b_qkv, b_up, b_out, gain_one, shift_one, b_down, gain_two, shift_two]
    if mesh_shape == (16, 2):
        little = [v.reshape(1, -1) for v in vectors] + [w_box]
        big = [w_qkv, w_out, w_up, w_down]
        layer_out, g_tok, _, p_wq, p_wo, p_wu, p_wd, small = run_layer(
            True, tokens, cotangent, bits, segs, big, little, [w.shape for w in big]
        )
        p_wb = small[:, :HD]
        p_bq, p_bu, p_bo, p_g1, p_s1, p_bd, p_g2, p_s2 = [
            small[row, 128 : 128 + v.shape[0]] for row, v in enumerate(vectors)
        ]
    else:
        low = lambda value: value.astype(bf16)
        gather = lambda value: lax.all_gather(low(value), "fsdp", axis=0, tiled=True)
        held = to_blocks(gather(w_qkv), gather(w_out), gather(w_up), gather(w_down))
        wb, bq, bu, *six = [gather(v) for v in [w_box] + vectors]
        order = quad_order(jnp.arange(3 * width))
        rows = jnp.stack([jnp.zeros((width,), bf16)] * 2 + six).astype(f32)
        layer_out, g_tok, _, g_held, g_wb, g_bq, g_bu, g_six = run_layer(
            False, tokens, cotangent, bits, segs, [held],
            [wb, bq[order].astype(f32).reshape(1, -1), bu.astype(f32).reshape(1, -1), rows], None,
        )

        def scatter(grad):
            part = lax.psum_scatter(grad, "fsdp", scatter_dimension=0, tiled=True)
            return lax.psum(part, "rep").astype(f32)

        p_wq, p_wo, p_wu, p_wd = [scatter(g) for g in from_blocks(g_held, width)]
        g_bq = jnp.zeros((3 * width,), f32).at[order].set(g_bq[0])
        p_wb, p_bq, p_bu = scatter(g_wb), scatter(g_bq), scatter(g_bu[0])
        p_bo, p_g1, p_s1, p_bd, p_g2, p_s2 = [scatter(g_six[2 + i]) for i in range(VECTORS)]
    return (
        layer_out, g_tok, p_wq, p_bq, p_wb, p_wo, p_bo, p_g1, p_s1,
        p_wu, p_bu, p_wd, p_bd, p_g2, p_s2,
    )


def solution(mesh):
    tokens = P(("fsdp", "rep"), None)
    matrix, vector = P("fsdp", None), P("fsdp")
    kinds = [matrix, vector, matrix, matrix, vector, vector, vector, matrix, vector, matrix, vector, vector, vector]
    return jax.shard_map(
        functools.partial(per_device, (mesh.shape["fsdp"], mesh.shape["rep"])),
        mesh=mesh,
        in_specs=(tokens, tokens, P(("fsdp", "rep")), P(None, ("fsdp", "rep")), *kinds),
        out_specs=(tokens, tokens, *kinds),
        check_vma=False,
    )
```

time: 1080 us -> 227 us (0.21)
  waiting for transfers between devices: 833 us -> 0 us
  Pallas kernels: 156 us -> 210 us
  blocking collectives: 45.4 us -> 0 us
  between operations: 14.5 us -> 0.68 us
    reduce_scatter x4 -> x0, waiting for transfers between devices: 499 us -> none  [scatter(): part = lax.psum_scatter(grad, 'fsdp', scatter_dimension=0, tiled=True)]
    all_gather x4 -> x0, waiting for transfers between devices: 209 us -> none  [per_device(): lax.all_gather(low(value), 'fsdp', axis=0, tiled=True)]
    unnamed x11 -> x0, waiting for transfers between devices: 109 us -> none
    pallas_call x3 -> x1, Pallas kernels: 156 us -> 210 us  [run_layer(): pl.pallas_call(functools.partial(layer_kernel, comm), out_shape=out_shape...]
    all_gather x1 -> x0, blocking collectives: 43 us -> none  [per_device(): table = lax.all_gather(packed, 'fsdp', axis=0, tiled=True)]
    psum x1 -> x0, waiting for transfers between devices: 15.3 us -> none  [scatter(): return lax.psum(part, 'rep').astype(f32)]
  transfers between devices with their start and end apart: 10 -> 0, of which waited for: 10 -> 0; matrix products, arithmetic and copies ran while one was open for 2% -> 0% of each run, Pallas kernels for 7% -> 0%
where the time goes in v2:
time: 227 us; the launch traced here: 226 us
  Pallas kernels  210 us (93%)
  local copies, waits for them, and re-layouts  14.1 us (6%)
    pallas_call x1, Pallas kernels, run_layer(): pl.pallas_call(functools.partial(layer_kernel, comm), out_shape=out_shape...  210 us
    unnamed x16, local copies, waits for them, and re-layouts  7.54 us

profile of v2, /device:TPU:0, one launch (start us, length us, event | category | flops | bytes accessed | tf_op | source)
XLA Modules:
  0.0 226.3 jit_solution(17782598095826683710)
XLA Ops:
  0.7 0.1 pad.2.clone
  0.7 1.3 reshape.57.refs_3_
  2.0 0.7 shift-right-arithmetic_convert_fusion
  2.7 0.7 maximum_maximum_fusion.refs_2_
  3.4 210.1 %layer.1 = (bf16[1024,768]{1,0:T(8,128)(2,1)}, f32[1024,768]{1,0:T(8,128)}, bf16[24,512,512]{2,1,0:T(8,128)(2,1)}, f32[48,2304]{1,0:T(8,128)}, f32[48,768]{1,0:T...) custom-call(bf16[1024,768]{1,0:T(8,128)(2,1)} %refs_0_.1, bf16[1024,768]{1,0:T(8,128)(2,1)} %refs_1_.1, ...), custom_call_target="tpu_custom_call" | custom-call | tf_op jit(solution)/shard_map/layer/pallas_call | solution.py:954
  213.6 1.3 slice.32
  214.8 1.3 slice.27
  216.1 1.4 slice_bitcast_fusion
  217.5 1.3 slice.28
  218.8 0.0 copy-start
  218.8 2.8 %copy.38 = bf16[1024,768]{1,0:T(8,128)(2,1)} copy(bf16[1024,768]{1,0:T(8,128)(2,1)} %get-tuple-element.52) | data formatting | bytes 3145728
  221.6 0.0 copy-done
  221.6 0.0 copy-start.3
  221.6 0.0 copy-start.4
  221.6 1.7 copy.39
  223.3 0.0 copy-done.3
  223.3 0.0 copy-start.2
  223.3 0.0 copy-start.1
  223.3 0.8 copy.40
  224.0 0.0 copy-done.4
  224.0 0.7 copy.41
  224.7 0.0 copy-done.2
  224.7 0.8 copy.42
  225.5 0.0 copy-done.1
  225.5 0.8 copy.43
  (1 shorter events, 0.0 us)
Async XLA Ops:
  218.8 2.8 %copy-start = (f32[1024,768]{1,0:T(8,128)S(1)}, f32[1024,768]{1,0:T(8,128)}, u32[]{:S(2)}) copy-start(f32[1024,768]{1,0:T(8,128)} %get-tuple-element.53) | copy-start | bytes 9437188
  221.6 1.7 copy-start.3
  221.6 2.4 %copy-start.4 = (f32[48,768]{1,0:T(8,128)S(1)}, f32[48,768]{1,0:T(8,128)}, u32[]{:S(2)}) copy-start(f32[48,768]{1,0:T(8,128)} %get-tuple-element.57) | copy-start | bytes 442372
  223.3 1.4 copy-start.2
  223.3 2.2 copy-start.1

commit v3 on v2

--- a/solution.py
+++ b/solution.py
@@ -40,16 +40,13 @@
     return pl.ds(pl.multiple_of(index * size, size), size)
 
 
-def wave_rows(coord_bits):
-    row = lax.broadcasted_iota(jnp.int32, (2 * WAVE, 16), 0)
-    col = lax.broadcasted_iota(jnp.int32, (2 * WAVE, 16), 1)
-    coord_of = (row % WAVE) // FREQ
-    pick = jnp.where(col == coord_of, 32.0, jnp.where(col == coord_of + 4, 1.0, 0.0)).astype(bf16)
-    coords = dot_nn(pick, coord_bits)
-    rows = lax.broadcasted_iota(jnp.int32, coords.shape, 0)
-    freq_index = (rows % FREQ).astype(f32)
-    frequency = jnp.exp(-math.log(10000.0) * freq_index / FREQ)
-    angle = coords * (100.0 / 1024.0) * frequency
+def wave_rows(coords):
+    count = coords.shape[1]
+    spread = [jnp.broadcast_to(coords[c : c + 1, :].astype(f32), (FREQ, count)) for c in range(4)]
+    scaled = jnp.concatenate(spread + spread, axis=0) * (100.0 / 1024.0)
+    rows = lax.broadcasted_iota(jnp.int32, scaled.shape, 0)
+    frequency = jnp.exp(-math.log(10000.0) * (rows & (FREQ - 1)).astype(f32) / FREQ)
+    angle = scaled * frequency
     turns = jnp.floor(angle * (2.0 / math.pi) + 0.5)
     rest = ((angle - turns * 1.5703125) - turns * 4.837512969970703125e-4) - turns * 7.549789954891e-8
     square = rest * rest
@@ -141,7 +138,7 @@
         return self.held.at[: PIECE * pieces, :HALF]
 
     def landing(self, stream, kind, index):
-        row = stream * BLOCK + PIECE * (index + (0, 0, 8, 12)[kind])
+        row = (stream + 8) % STREAMS * BLOCK + PIECE * (index + (0, 0, 8, 12)[kind])
         column = 0 if kind == 0 else HALF
         return self.stage.at[pl.ds(pl.multiple_of(row, 16), PIECE), column : column + HALF]
 
@@ -312,13 +309,12 @@
 
 
 def owner_tables(start, share, depth, order=None):
-    col = lax.broadcasted_iota(jnp.int32, (depth, BLOCK), 1) + start
+    col = lax.broadcasted_iota(jnp.int32, (1, BLOCK), 1) + start
     source = col if order is None else order(col)
-    pick = (source % share == lax.broadcasted_iota(jnp.int32, (depth, BLOCK), 0)).astype(bf16)
-    col = lax.broadcasted_iota(jnp.int32, (128, BLOCK), 1) + start
+    owner, entry = source // share, source % share
+    pick = (entry == lax.broadcasted_iota(jnp.int32, (depth, BLOCK), 0)).astype(bf16)
     row = lax.broadcasted_iota(jnp.int32, (128, BLOCK), 0)
-    source = col if order is None else order(col)
-    return pick, source // share == row // 8, row % 8
+    return pick, owner == (row >> 3), row & 7
 
 
 def quad_order(col):
@@ -332,7 +328,7 @@
         taken, refs[:] = refs[:count], refs[count:]
         return taken
 
-    tok_in, cot_in, bits, segs = take(4)
+    tok_in, cot_in, coords_in, segs_in = take(4)
     if comm:
         w_qkv_in, w_out_in, w_up_in, w_down_in = take(4)
         small_in = take(9)
@@ -340,13 +336,14 @@
         held_in, w_box_in, b_qkv_in, b_up_in, vectors_in = take(5)
     layer_out, g_tok_out, e_hbm = take(3)
     if comm:
-        p_qkv, p_out, p_up, p_down, p_small = take(5)
+        final_out, small_out = take(2)
     else:
         g_held, g_w_box_out, g_b_qkv_out, g_b_up_out, g_vectors_out = take(5)
     (held, stage, slope, q8t, k8t, v_row, ctx_t, wave_t, wave_r, e_buf, normed, total, flip, g_down, tok_t, g_ctx_t,
-     inv_one, inv_total, w_box, w_box_t, b_qkv, b_up, vectors, g_w_box, g_b_qkv, g_b_up, g_vectors, e_sem, io_sem) = take(29)
+     inv_one, inv_total, w_box, w_box_t, b_qkv, b_up, vectors, g_w_box, g_b_qkv, g_b_up, g_vectors, e_sem, io_sem, coords, segs) = take(31)
     if comm:
-        final, small, small_stage, g_small, mid_sem = take(5)
+        final, small, small_stage, g_small, small_final, mid_sem = take(6)
+        small_held = take(9)
         block_sems, small_sems, small_final_sems = take(5), take(4), take(1)
 
     count, width = tok_t.shape[1], tok_t.shape[0]
@@ -355,11 +352,8 @@
     row_blocks = count // ROWS
     up_blocks = ff // BLOCK
     quads = pairs // 2
-    act = stage.at[: up_blocks * count]
-    ctx = stage.at[up_blocks * count : (up_blocks + 1) * count]
-    low = stage.at[(up_blocks + 1) * count : (up_blocks + 2) * count]
-    cot = stage.at[(up_blocks + 2) * count : (up_blocks + 3) * count]
-    tok = stage.at[(up_blocks + 3) * count : (up_blocks + 4) * count]
+    ctx, low, cot, tok = [stage.at[part * count : (part + 1) * count] for part in range(4)]
+    act = stage.at[STREAMS * BLOCK - up_blocks * count :]
     up_at, down_at = 4 * BLOCK, 8 * BLOCK
 
     def copy_in(source, target, index=0):
@@ -367,14 +361,14 @@
 
     tok_copy = copy_in(tok_in, tok, 0)
     cot_copy = copy_in(cot_in, cot, 1)
-    tok_copy.start()
-    cot_copy.start()
+    coord_copy = copy_in(coords_in, coords, 2)
+    seg_copy = copy_in(segs_in, segs, 3)
 
     if comm:
         route = Route()
         blocks = Exchange(route, Streams(held, stage, final, block_sems))
-        extras = Exchange(route, Vectors(small, small_stage, p_small, [*small_sems, *small_final_sems]))
-        sums = Exchange(route, Vectors(g_small, small_stage, p_small, [*small_sems, *small_final_sems]))
+        extras = Exchange(route, Vectors(small, small_stage, small_final, [*small_sems, *small_final_sems]))
+        sums = Exchange(route, Vectors(g_small, small_stage, small_final, [*small_sems, *small_final_sems]))
         barrier = pltpu.get_barrier_semaphore()
         for chip, core in route.peers():
             pl.semaphore_signal(barrier, inc=1, device_id=(chip, core), device_id_type=pl.DeviceIdType.MESH)
@@ -392,37 +386,56 @@
                 total.at[(4 + block) * PIECE : (5 + block) * PIECE],
             ))
         moves.append((w_down_in, total.at[8 * PIECE : 12 * PIECE]))
-        for index, (source, target) in enumerate(moves):
-            copy_in(source, target, 2 + index).start()
-        small_in = [ref[...].astype(bf16).astype(f32) for ref in small_in]
+        moves += list(zip(small_in, small_held))
+        moves = [copy_in(source, target, 4 + index) for index, (source, target) in enumerate(moves)]
+        first = 3 * quads
+        for copy in moves[:first] + moves[first + 1 + up_blocks + 1 :] + moves[first : first + 1 + up_blocks + 1]:
+            copy.start()
+        for copy in (coord_copy, seg_copy, tok_copy, cot_copy):
+            copy.start()
+
+        def round_block(block):
+            at = pl.ds(pl.multiple_of(block * BLOCK + PIECE * route.me, 16), PIECE)
+            held[at, :] = total[block * PIECE : (block + 1) * PIECE, :].astype(bf16)
+
         g_small[:8, :] = jnp.zeros((8, SMALL), f32)
-        g_small[:8, :HD] = small_in[8]
+        for copy in moves[:first]:
+            copy.wait()
+        for block in range(quads):
+            round_block(block)
+        for copy in moves[first + 1 + up_blocks + 1 :]:
+            copy.wait()
+        g_small[:8, :HD] = small_held[8][...].astype(bf16).astype(f32)
         for row in range(8):
-            value = small_in[row]
+            value = small_held[row][...].astype(bf16).astype(f32)
             g_small[row : row + 1, 128 : 128 + value.shape[1]] = value
         small[pl.ds(pl.multiple_of(route.me * 8, 8), 8), :] = g_small[:8, :]
-        for index, (source, target) in enumerate(moves):
-            copy_in(source, target, 2 + index).wait()
-        for block in range(STREAMS - up_blocks):
-            at = pl.ds(pl.multiple_of(block * BLOCK + PIECE * route.me, 16), PIECE)
-            held[at, :] = total[block * PIECE : (block + 1) * PIECE, :].astype(bf16)
+        pl.semaphore_wait(barrier, 6)
+        extras.gather_own(0)
+        for stream in range(quads):
+            blocks.gather_own(stream)
+        for copy in moves[first : first + 1 + up_blocks + 1]:
+            copy.wait()
+        for block in range(quads, STREAMS - up_blocks):
+            round_block(block)
         at = pl.ds(pl.multiple_of(down_at + 4 * PIECE * route.me, 16), 4 * PIECE)
         held[at, :] = total[8 * PIECE : 12 * PIECE, :].astype(bf16)
-        pl.semaphore_wait(barrier, 6)
-        extras.gather_own(0)
-        for stream in range(4):
-            blocks.gather_own(stream)
+        blocks.gather_own(quads)
     else:
-        copy_in(held_in, held, 2).start()
+        for copy in (coord_copy, seg_copy, tok_copy, cot_copy):
+            copy.start()
+        copy_in(held_in, held, 4).start()
         w_box[...] = w_box_in[...]
         b_qkv[...] = b_qkv_in[...]
         b_up[...] = b_up_in[...]
         vectors[...] = vectors_in[...]
 
-    wave_t[...] = wave_rows(bits[...])
+    coord_copy.wait()
+    seg_copy.wait()
+    wave_t[...] = wave_rows(coords[...])
     wave_r[...] = jnp.transpose(wave_t[...])
     for slot in range(slots):
-        seg_i = jnp.broadcast_to(segs[slot : slot + 1, :].astype(f32), (SLOT, SLOT))
+        seg_i = jnp.broadcast_to(segs[:, slot * SLOT : (slot + 1) * SLOT].astype(f32), (SLOT, SLOT))
         seg_j = jnp.transpose(seg_i)
         normed[slot * SLOT : (slot + 1) * SLOT, :SLOT] = jnp.where(seg_i == seg_j, 0.0, neg_large)
     g_w_box[...] = jnp.zeros_like(g_w_box)
@@ -458,7 +471,7 @@
                 target[:, aligned(block, BLOCK)] = rows if row is None else jnp.sum(rows, axis=0, keepdims=True)
 
     else:
-        copy_in(held_in, held, 2).wait()
+        copy_in(held_in, held, 4).wait()
     w_box_t[...] = jnp.transpose(w_box[...].astype(f32)).astype(bf16)
 
     def gather_tick(step):
@@ -634,70 +647,64 @@
             blocks.gather_sent(stream)
         extras.gather_sent(0)
 
+    def last(step):
+        turn = step // 4
+        return STREAMS - 1 - step + (14 - 6 * turn) * turn - 4
+
+    def sum_start(step):
+        if comm:
+            blocks.sum_cores(last(step))
+
+    def sum_tick(step, stages=(0, 1, 2, 3)):
+        if not comm:
+            return
+        acts = (blocks.sum_far, blocks.sum_near, blocks.sum_column, blocks.sum_end)
+        for behind in stages:
+            at = step - behind
+            if isinstance(at, int):
+                if 0 <= at < STREAMS:
+                    acts[behind](last(at))
+            else:
+                pl.when((at >= 0) & (at < STREAMS))(functools.partial(acts[behind], last(at)))
+
+    def meet(sem):
+        if comm:
+            for chip, core in route.peers():
+                pl.semaphore_signal(sem, inc=1, device_id=(chip, core), device_id_type=pl.DeviceIdType.MESH)
+            pl.semaphore_wait(sem, 6)
+
+    out_copy.wait()
+    if comm:
+        meet(mid_sem.at[0])
+
     @pl.loop(0, up_blocks)
-    def _(block):
+    def _(index):
+        block = up_blocks - 1 - index
         down_rows = pl.ds(pl.multiple_of(down_at + block * BLOCK, BLOCK), BLOCK)
-
-        @pl.loop(0, row_blocks)
-        def _(row):
-            rows = aligned(row, ROWS)
-            at = pl.ds(pl.multiple_of(block * count + row * ROWS, ROWS), ROWS)
+        up_rows = pl.ds(pl.multiple_of(up_at + block * BLOCK, BLOCK), BLOCK)
+        for row in range(2):
+            rows = slice(row * (count // 2), (row + 1) * (count // 2))
+            at = pl.ds(pl.multiple_of(block * count + row * (count // 2), count // 2), count // 2)
             g_act = dot_nt(g_down[rows, :], held[down_rows, :])
             g_up = (g_act * slope[at, :].astype(f32)).astype(bf16)
             slope[at, :] = g_up
             g_b_up[:, aligned(block, BLOCK)] += column_sum(g_up.astype(f32))
-
-        @pl.loop(0, BLOCK // ROWS)
-        def _(part):
-            at = pl.ds(pl.multiple_of(down_at + block * BLOCK + part * ROWS, ROWS), ROWS)
-            held[at, :] = dot_tn(act[aligned(block, count), aligned(part, ROWS)], g_down[...]).astype(bf16)
-
-    out_copy.wait()
-
-    def last(step):
-        return STREAMS - 1 - step
-
-    def sum_start(step):
-        if comm:
-            blocks.sum_cores(last(step))
-
-    def sum_tick(step):
-        if not comm:
-            return
-        for behind, act_on in enumerate((blocks.sum_far, blocks.sum_near, blocks.sum_column, blocks.sum_end)):
-            at = step - behind
-            if isinstance(at, int):
-                if 0 <= at < STREAMS:
-                    act_on(last(at))
-            else:
-                pl.when((at >= 0) & (at < STREAMS))(functools.partial(act_on, last(at)))
+            total[rows, :] += dot_nt(g_up, held[up_rows, :])
+        g_up = slope[aligned(block, count), :]
+        for part in range(2):
+            at = pl.ds(pl.multiple_of(up_at + block * BLOCK + part * HALF, HALF), HALF)
+            held[at, :] = dot_nn(flip[part * HALF : (part + 1) * HALF, :], g_up).astype(bf16)
+        sum_start(index)
+        for part in range(2):
+            at = pl.ds(pl.multiple_of(down_at + block * BLOCK + part * HALF, HALF), HALF)
+            grads = dot_tn(act[aligned(block, count), part * HALF : (part + 1) * HALF], g_down[...])
+            held[at, :] = grads.astype(bf16)
+        sum_tick(index)
 
     if comm:
-        for chip, core in route.peers():
-            pl.semaphore_signal(mid_sem, inc=1, device_id=(chip, core), device_id_type=pl.DeviceIdType.MESH)
-        pl.semaphore_wait(mid_sem, 6)
-
+        meet(mid_sem.at[1])
     for step in range(up_blocks):
-        sum_start(step)
-
-    @pl.loop(0, up_blocks)
-    def _(index):
-        block = up_blocks - 1 - index
-        up_rows = pl.ds(pl.multiple_of(up_at + block * BLOCK, BLOCK), BLOCK)
-
-        @pl.loop(0, row_blocks)
-        def _(row):
-            rows = aligned(row, ROWS)
-            at = pl.ds(pl.multiple_of(block * count + row * ROWS, ROWS), ROWS)
-            total[rows, :] += dot_nt(slope[at, :], held[up_rows, :])
-
-        @pl.loop(0, BLOCK // ROWS)
-        def _(part):
-            at = pl.ds(pl.multiple_of(up_at + block * BLOCK + part * ROWS, ROWS), ROWS)
-            held[at, :] = dot_nn(flip[aligned(part, ROWS), :], slope[aligned(block, count), :]).astype(bf16)
-
-        sum_start(up_blocks + index)
-        sum_tick(index)
+        sum_start(up_blocks + step)
 
     @pl.loop(0, row_blocks)
     def _(block):
@@ -779,11 +786,11 @@
             at = pl.ds(pl.multiple_of(part * QUAD + pair % 2 * PAIR, PAIR), PAIR)
             flip[at, cols] = jnp.concatenate(g_parts[part], axis=0).astype(bf16)
 
-    def token_grad(quad):
+    def token_grad():
         @pl.loop(0, row_blocks)
         def _(block):
             rows = aligned(block, ROWS)
-            part = dot_nn(held[aligned(quad, BLOCK), :], flip[:, rows])
+            part = dot_nn(slope[:BLOCK, :], flip[:, rows])
             total[rows, :] += jnp.transpose(part)
 
     @pl.loop(0, quads)
@@ -794,18 +801,17 @@
         def _(inner):
             order = turn * quad_steps + inner
             if comm:
-                pl.when(order % 2 == 1)(functools.partial(sum_tick, 5 + order // 2))
+                pl.when(order % 2 == 0)(functools.partial(sum_tick, 5 + order // 2, (0,)))
+                pl.when(order % 2 == 1)(functools.partial(sum_tick, 5 + order // 2, (1, 2, 3)))
             attend_back(order)
 
-        token_grad(quad)
-
-        @pl.loop(0, BLOCK // ROWS)
-        def _(part):
-            at = pl.ds(pl.multiple_of(quad * BLOCK + part * ROWS, ROWS), ROWS)
-            held[at, :] = dot_nt(tok_t[aligned(part, ROWS), :], flip[...]).astype(bf16)
-
+        slope[:BLOCK, :] = held[aligned(quad, BLOCK), :]
+        for part in range(2):
+            at = pl.ds(pl.multiple_of(quad * BLOCK + part * HALF, HALF), HALF)
+            held[at, :] = dot_nt(tok_t[part * HALF : (part + 1) * HALF, :], flip[...]).astype(bf16)
+        sum_start(9 + turn)
         g_b_qkv[:, aligned(quad, BLOCK)] = dot_nt(ones, flip[...])[:1]
-        sum_start(9 + turn)
+        token_grad()
 
     g_w_box[...] = g_w_box[...] * (1.0 / scale_factor)
     tok_out = pltpu.make_async_copy(total, g_tok_out, io_sem.at[0])
@@ -832,37 +838,27 @@
                 g_small[:, 128:384] += dot_nt(upper, pick) + dot_nt((spread - upper.astype(f32)).astype(bf16), pick)
 
         sums.sum_cores(0)
-        sum_tick(11)
+        sum_tick(11, (1, 2, 3))
+        sum_tick(11, (0,))
         sums.sum_far(0)
-        sum_tick(12)
+        sum_tick(12, (2, 3))
+        sum_tick(12, (1,))
         sums.sum_near(0)
-        sum_tick(13)
+        sum_tick(13, (3,))
+        sum_tick(13, (2,))
         sums.sum_column(0)
-        sum_tick(14)
+        sum_tick(14, (3,))
         sums.sum_end(0)
         for stream in range(STREAMS):
             blocks.summed(stream)
         sums.summed(0)
         blocks.results_in()
         sums.results_in()
-        moves = []
-        for quad in range(quads):
-            for part in range(3):
-                moves.append((
-                    final.at[quad * PIECE : (quad + 1) * PIECE, part * QUAD : (part + 1) * QUAD],
-                    p_qkv.at[:, part * width + quad * QUAD : part * width + (quad + 1) * QUAD],
-                ))
-        moves.append((final.at[3 * PIECE : 4 * PIECE], p_out))
-        for block in range(up_blocks):
-            moves.append((
-                final.at[(4 + block) * PIECE : (5 + block) * PIECE],
-                p_up.at[:, block * BLOCK : (block + 1) * BLOCK],
-            ))
-        moves.append((final.at[8 * PIECE : 12 * PIECE], p_down))
-        for index, (source, target) in enumerate(moves):
-            copy_in(source, target, 2 + index).start()
-        for index, (source, target) in enumerate(moves):
-            copy_in(source, target, 2 + index).wait()
+        moves = [copy_in(final, final_out, 2), copy_in(small_final, small_out, 3)]
+        for copy in moves:
+            copy.start()
+        for copy in moves:
+            copy.wait()
     else:
         g_w_box_out[...] = g_w_box[...]
         g_b_qkv_out[...] = g_b_qkv[...]
@@ -886,7 +882,7 @@
     return [pl.BlockSpec(memory_space=pl.ANY)] * count
 
 
-def run_layer(comm, tokens, cotangent, bits, segs, big, little, shard_shapes):
+def run_layer(comm, tokens, cotangent, coords, segs, big, little):
     count, width = tokens.shape
     ff = 4 * BLOCK
     slots, pairs = count // SLOT, HEADS // 2
@@ -898,8 +894,8 @@
     ]
     out_specs = in_hbm(3)
     if comm:
-        out_shape += [shaped(shape, f32) for shape in shard_shapes] + [shaped((8, SMALL), f32)]
-        out_specs += in_hbm(4) + in_vmem(1)
+        out_shape += [shaped((STREAMS * PIECE, BLOCK), f32), shaped((8, SMALL), f32)]
+        out_specs += in_hbm(2)
     else:
         out_shape += [shaped(held_shape, bf16), shaped((2 * WAVE, HD), f32), shaped((1, 3 * width), f32)]
         out_shape += [shaped((1, ff), f32), shaped((8, width), f32)]
@@ -935,7 +931,9 @@
         vmem((1, ff), f32),
         vmem((8, width), f32),
         dma((2, 2)),
-        dma((20,)),
+        dma((32,)),
+        vmem(coords.shape, jnp.int32),
+        vmem(segs.shape, jnp.int32),
     ]
     if comm:
         scratch += [
@@ -943,7 +941,9 @@
             vmem((128, SMALL), f32),
             vmem((256, SMALL // 2), f32),
             vmem((128, SMALL), f32),
-            pltpu.SemaphoreType.REGULAR,
+            vmem((8, SMALL), f32),
+            pltpu.SemaphoreType.REGULAR((2,)),
+            *[vmem(value.shape, f32) for value in little],
             dma((STREAMS, 4)), dma((STREAMS, 2)), dma((STREAMS, 4)), dma((STREAMS,)), dma((2,)),
             dma((1, 4)), dma((1, 2)), dma((1, 4)), dma((1,)),
             dma((2,)),
@@ -954,12 +954,82 @@
     return pl.pallas_call(
         functools.partial(layer_kernel, comm),
         out_shape=out_shape,
-        in_specs=in_hbm(2) + in_vmem(2) + in_hbm(len(big)) + in_vmem(len(little)),
+        in_specs=in_hbm(4 + len(big)) + (in_hbm if comm else in_vmem)(len(little)),
         out_specs=out_specs,
         scratch_shapes=scratch,
         compiler_params=pltpu.CompilerParams(vmem_limit_bytes=vmem_limit, **extra),
         name="layer",
-    )(tokens, cotangent, bits, segs, *big, *little)
+    )(tokens, cotangent, coords, segs, *big, *little)
+
+
+def finish_kernel(*refs):
+    layer_in, tok_in, blocks_in, small_in = refs[:4]
+    layer_out, tok_out, p_qkv, p_out, p_up, p_down = refs[4:10]
+    small_out = refs[10:19]
+    layer, tok, blocks, small = refs[19:23]
+    small_rows = refs[23:32]
+    load_sem, store_sem = refs[32:]
+    width = layer_in.shape[1]
+    loads, stores = [], []
+    parts = 4
+    rows = layer_in.shape[0] // parts
+    small_load = pltpu.make_async_copy(small_in, small, load_sem.at[0])
+    loads.append((pltpu.make_async_copy(blocks_in, blocks, load_sem.at[1]), []))
+    for quad in range(width // QUAD):
+        for part in range(3):
+            loads[0][1].append((
+                blocks.at[quad * PIECE : (quad + 1) * PIECE, part * QUAD : (part + 1) * QUAD],
+                p_qkv.at[:, part * width + quad * QUAD : part * width + (quad + 1) * QUAD],
+            ))
+    loads[0][1].append((blocks.at[3 * PIECE : 4 * PIECE], p_out))
+    for block in range(4):
+        loads[0][1].append((
+            blocks.at[(4 + block) * PIECE : (5 + block) * PIECE], p_up.at[:, block * BLOCK : (block + 1) * BLOCK]
+        ))
+    loads[0][1].append((blocks.at[8 * PIECE : 12 * PIECE], p_down))
+    for source, held, target in ((tok_in, tok, tok_out), (layer_in, layer, layer_out)):
+        for part in range(parts):
+            at = slice(part * rows, (part + 1) * rows)
+            copy = pltpu.make_async_copy(source.at[at], held.at[at], load_sem.at[1 + len(loads)])
+            loads.append((copy, [(held.at[at], target.at[at])]))
+    small_load.start()
+    for copy, _ in loads:
+        copy.start()
+
+    def store(source, target):
+        stores.append(pltpu.make_async_copy(source, target, store_sem.at[len(stores)]))
+        stores[-1].start()
+
+    small_load.wait()
+    for row in range(8):
+        small_rows[row][...] = small[row : row + 1, 128 : 128 + small_rows[row].shape[1]]
+    small_rows[8][...] = small[:, :HD]
+    for source, target in zip(small_rows, small_out):
+        store(source, target)
+    for copy, moves in loads:
+        copy.wait()
+        for source, target in moves:
+            store(source, target)
+    for copy in stores:
+        copy.wait()
+
+
+def run_finish(layer_out, g_tok, blocks, small, big, little):
+    shapes = [shaped(layer_out.shape, bf16), shaped(g_tok.shape, f32)]
+    shapes += [shaped(w.shape, f32) for w in big + little]
+    dma = pltpu.SemaphoreType.DMA
+    return pl.pallas_call(
+        finish_kernel,
+        out_shape=shapes,
+        in_specs=in_hbm(4),
+        out_specs=in_hbm(len(shapes)),
+        scratch_shapes=[
+            pltpu.VMEM(layer_out.shape, bf16), pltpu.VMEM(g_tok.shape, f32), pltpu.VMEM(blocks.shape, f32),
+            pltpu.VMEM(small.shape, f32), *[pltpu.VMEM(v.shape, f32) for v in little], dma((16,)), dma((40,)),
+        ],
+        compiler_params=pltpu.CompilerParams(vmem_limit_bytes=16_000_000),
+        name="finish",
+    )(layer_out, g_tok, blocks, small)
 
 
 def to_blocks(w_qkv, w_out, w_up, w_down):
@@ -980,19 +1050,15 @@
     w_up, b_up, w_down, b_down, gain_two, shift_two,
 ):
     count, width = tokens.shape
-    bits = jnp.concatenate([box_coords >> 5, box_coords & 31, jnp.zeros((8, count), jnp.int32)], axis=0).astype(bf16)
-    segs = segments.reshape(-1, SLOT)
+    segs = segments.reshape(1, -1)
     vectors = [b_qkv, b_up, b_out, gain_one, shift_one, b_down, gain_two, shift_two]
     if mesh_shape == (16, 2):
         little = [v.reshape(1, -1) for v in vectors] + [w_box]
         big = [w_qkv, w_out, w_up, w_down]
-        layer_out, g_tok, _, p_wq, p_wo, p_wu, p_wd, small = run_layer(
-            True, tokens, cotangent, bits, segs, big, little, [w.shape for w in big]
-        )
-        p_wb = small[:, :HD]
-        p_bq, p_bu, p_bo, p_g1, p_s1, p_bd, p_g2, p_s2 = [
-            small[row, 128 : 128 + v.shape[0]] for row, v in enumerate(vectors)
-        ]
+        layer_out, g_tok, _, blocks, small = run_layer(True, tokens, cotangent, box_coords, segs, big, little)
+        layer_out, g_tok, p_wq, p_wo, p_wu, p_wd, *rest = run_finish(layer_out, g_tok, blocks, small, big, little)
+        p_bq, p_bu, p_bo, p_g1, p_s1, p_bd, p_g2, p_s2 = [v.reshape(-1) for v in rest[:8]]
+        p_wb = rest[8]
     else:
         low = lambda value: value.astype(bf16)
         gather = lambda value: lax.all_gather(low(value), "fsdp", axis=0, tiled=True)
@@ -1001,8 +1067,8 @@
         order = quad_order(jnp.arange(3 * width))
         rows = jnp.stack([jnp.zeros((width,), bf16)] * 2 + six).astype(f32)
         layer_out, g_tok, _, g_held, g_wb, g_bq, g_bu, g_six = run_layer(
-            False, tokens, cotangent, bits, segs, [held],
-            [wb, bq[order].astype(f32).reshape(1, -1), bu.astype(f32).reshape(1, -1), rows], None,
+            False, tokens, cotangent, box_coords, segs, [held],
+            [wb, bq[order].astype(f32).reshape(1, -1), bu.astype(f32).reshape(1, -1), rows],
         )
 
         def scatter(grad):

time: 227 us -> 208 us (0.916)
  local copies, waits for them, and re-layouts: 14.1 us -> 5.48 us
  Pallas kernels: 210 us -> 202 us
    pallas_call x1, Pallas kernels: 210 us -> 197 us  [run_layer(): pl.pallas_call(functools.partial(layer_kernel, comm), out_shape=out_shape...]
    pallas_call x0 -> x1, Pallas kernels: none -> 4.76 us  [run_finish(): pl.pallas_call(finish_kernel, out_shape=shapes, in_specs=in_hbm(4), out_s...]
    slice x3 -> x0, local copies, waits for them, and re-layouts: 3.8 us -> none  [the longest x2 2.52 us: per_device(): small[row, 128:128 + v.shape[0]]]
    unnamed x16 -> x8, local copies, waits for them, and re-layouts: 7.54 us -> 5.48 us
where the time goes in v3:
time: 208 us
  Pallas kernels  202 us (97%)
  local copies, waits for them, and re-layouts  5.48 us (3%)
    pallas_call x1, Pallas kernels, run_layer(): pl.pallas_call(functools.partial(layer_kernel, comm), out_shape=out_shape...  197 us
    unnamed x8, local copies, waits for them, and re-layouts  5.48 us
    pallas_call x1, Pallas kernels, run_finish(): pl.pallas_call(finish_kernel, out_shape=shapes, in_specs=in_hbm(4), out_s...  4.76 us

profile of v3, /device:TPU:0, one launch (start us, length us, event | category | flops | bytes accessed | tf_op | source)
XLA Modules:
  0.0 208.0 jit_solution(5560300070255180176)
XLA Ops:
  0.7 196.9 %layer.1 = (bf16[1024,768]{1,0:T(8,128)(2,1)}, f32[1024,768]{1,0:T(8,128)}, bf16[24,512,512]{2,1,0:T(8,128)(2,1)}, f32[576,768]{1,0:T(8,128)}, f32[8,512]{1,0:T(8,128)}) custom-call(bf16[1024,768]{1,0:T(8,128)(2,1)} %refs_0_.1, bf16[1024,768]{1,0:T(8,128)(2,1)} %refs_1_.1, s32[4,1024]{1,0:T(4,128)} %refs_2_.1, s32[1,1024]{1,0:T(1,128)} %bitcast.17, ...), custom_call_target="tpu_custom_call" | custom-call | tf_op jit(solution)/shard_map/layer/pallas_call | solution.py:954
  197.6 0.0 copy-start
  197.6 1.9 copy-done
  199.5 0.0 copy-start.1
  199.5 1.5 copy-done.1
  200.9 0.0 copy-start.2
  200.9 1.4 copy-done.2
  202.3 0.0 copy-start.3
  202.4 0.7 copy-done.3
  203.1 4.8 %finish.1 = (bf16[1024,768]{1,0:T(8,128)(2,1)}, f32[1024,768]{1,0:T(8,128)}, f32[48,2304]{1,0:T(8,128)}, f32[48,768]{1,0:T(8,128)}, f32[48,3072]{1,0:T(8,128)}, ...) custom-call(bf16[1024,768]{1,0:T(8,128)(2,1)S(1)} %copy-done.2, ...), custom_call_target="tpu_custom_call" | custom-call | tf_op jit(solution)/shard_map/finish/pallas_call | solution.py:1021
Async XLA Ops:
  197.6 1.9 copy-start
  199.5 1.5 copy-start.1
  200.9 1.4 copy-start.2
  202.3 0.7 copy-start.3

commit v4 on v3

--- a/solution.py
+++ b/solution.py
@@ -96,8 +96,9 @@
 
 class Route:
     def __init__(self):
-        self.me = lax.axis_index("fsdp")
+        chip = lax.axis_index("fsdp")
         self.core = lax.axis_index("rep")
+        self.level, self.me = chip // 4, chip % 4
         near_step, far_step = 1 + self.core, 2 - self.core
         near_move = near_step * (1 - 2 * ((self.me // near_step) % 2))
         far_move = far_step * (1 - 2 * ((self.me // far_step) % 2))
@@ -105,12 +106,16 @@
         self.far = self.me + far_move
         self.across = self.me + near_move + far_move
 
-    def column(self, base):
-        return [(base + 4 * k) % 16 for k in range(4)]
+    def chip(self, level, place):
+        return level * 4 + place
+
+    def levels(self):
+        return [(self.level + k) % 4 for k in range(1, 4)]
 
     def peers(self):
-        chips = self.column(self.me)[1:] + [self.near, self.far]
-        return [(chip, self.core) for chip in chips] + [(self.me, 1 - self.core)]
+        chips = [self.chip(level, self.me) for level in self.levels()]
+        chips += [self.chip(self.level, self.near), self.chip(self.level, self.far)]
+        return [(chip, self.core) for chip in chips] + [(self.chip(self.level, self.me), 1 - self.core)]
 
 
 def remote(source, target, send, recv, chip, core):
@@ -120,32 +125,40 @@
     )
 
 
+def half_columns(half, size):
+    return pl.ds(pl.multiple_of(half * size, size), size)
+
+
 class Streams:
-    count = STREAMS
-
     def __init__(self, held, stage, final, sems):
-        self.held, self.stage, self.final = held, stage, final
+        self.held = held
+        self.upper = held.at[: 8 * BLOCK].reshape(8, 4, 4, PIECE, BLOCK)
+        self.lower = held.at[8 * BLOCK :].reshape(4, 4, 4, PIECE, BLOCK)
+        self.stage = stage.reshape(STREAMS, 4, 4, PIECE, BLOCK)
+        self.final = final
         self.gather_recv, self.gather_send, self.sum_recv, self.sum_send, self.final_sem = sems
 
-    def window(self, stream, shard, half):
-        lower = stream // 8
-        row = (1 - lower) * (stream * BLOCK + PIECE * shard) + lower * (
-            8 * BLOCK + PIECE * (stream - 8) + 4 * PIECE * shard
-        )
-        return self.held.at[pl.ds(pl.multiple_of(row, 16), PIECE), pl.ds(pl.multiple_of(half * HALF, HALF), HALF)]
+    def on(self, stream, act):
+        if isinstance(stream, int):
+            act(self.upper.at[stream] if stream < 8 else self.lower.at[:, :, stream - 8])
+        else:
+            pl.when(stream < 8)(lambda: act(self.upper.at[stream]))
+            pl.when(stream >= 8)(lambda: act(self.lower.at[:, :, stream - 8]))
+
+    def half(self, half):
+        return half_columns(half, HALF)
 
     def several(self, pieces):
         return self.held.at[: PIECE * pieces, :HALF]
 
-    def landing(self, stream, kind, index):
-        row = (stream + 8) % STREAMS * BLOCK + PIECE * (index + (0, 0, 8, 12)[kind])
-        column = 0 if kind == 0 else HALF
-        return self.stage.at[pl.ds(pl.multiple_of(row, 16), PIECE), column : column + HALF]
+    def landing(self, stream, kind):
+        block = self.stage.at[(stream + 8) % STREAMS]
+        if kind == 0:
+            return block.at[:, :, :, :HALF]
+        return block.at[(0, 0, 2, 3)[kind] : (0, 2, 3, 4)[kind], :, :, HALF:]
 
     def result(self, stream, half):
-        return self.final.at[
-            pl.ds(pl.multiple_of(stream * PIECE, 16), PIECE), pl.ds(pl.multiple_of(half * HALF, HALF), HALF)
-        ]
+        return self.final.at[pl.ds(pl.multiple_of(stream * PIECE, 16), PIECE), self.half(half)]
 
     def results(self):
         return self.final.at[:, :HALF]
@@ -153,25 +166,27 @@
 
 class Vectors:
     def __init__(self, held, stage, final, sems):
-        self.held, self.stage, self.final = held, stage, final
+        self.held, self.flat, self.final = held, stage, final
+        self.shards = held.reshape(4, 4, 8, SMALL)
+        self.stage = stage.reshape(8, 4, 8, SMALL // 2)
         self.gather_recv, self.gather_send, self.sum_recv, self.sum_send, self.final_sem = sems
 
-    def window(self, stream, shard, half):
-        wide = SMALL // 2
-        return self.held.at[pl.ds(pl.multiple_of(shard * 8, 8), 8), pl.ds(pl.multiple_of(half * wide, wide), wide)]
+    def on(self, stream, act):
+        act(self.shards)
+
+    def half(self, half):
+        return half_columns(half, SMALL // 2)
 
     def several(self, pieces):
         if pieces <= 16:
             return self.held.at[: 8 * pieces, : SMALL // 2]
-        return self.stage.at[: 8 * pieces, :]
-
-    def landing(self, stream, kind, index):
-        row = 8 * (index + (0, 16, 24, 28)[kind])
-        return self.stage.at[pl.ds(pl.multiple_of(row, 8), 8), :]
+        return self.flat.at[: 8 * pieces, :]
+
+    def landing(self, stream, kind):
+        return self.stage.at[(0, 4, 6, 7)[kind] : (4, 6, 7, 8)[kind]]
 
     def result(self, stream, half):
-        wide = SMALL // 2
-        return self.final.at[:, pl.ds(pl.multiple_of(half * wide, wide), wide)]
+        return self.final.at[:, self.half(half)]
 
     def results(self):
         return self.final.at[:, : SMALL // 2]
@@ -185,46 +200,67 @@
     def __init__(self, route, parts):
         self.route, self.parts = route, parts
 
-
-    def share(self, stream, shard, chip, kind):
+    def send(self, source, target, send, recv, level, place, core):
+        remote(source, target, send, recv, self.route.chip(level, place), core).start()
+
+
+    def share(self, stream, view, place, kind):
         p, r = self.parts, self.route
-        view = p.window(stream, shard, r.core)
-        remote(view, view, p.gather_send.at[stream, 0], p.gather_recv.at[stream, kind], chip, r.core).start()
-
-    def hand_over(self, stream, shard):
+        self.send(
+            view, view, p.gather_send.at[stream, 0], p.gather_recv.at[stream, kind], r.level, place, r.core
+        )
+
+    def hand_over(self, stream, view):
         p, r = self.parts, self.route
-        view = p.window(stream, shard, r.core)
-        remote(view, view, p.gather_send.at[stream, 1], p.gather_recv.at[stream, 3], r.me, 1 - r.core).start()
+        self.send(
+            view, view, p.gather_send.at[stream, 1], p.gather_recv.at[stream, 3], r.level, r.me, 1 - r.core
+        )
 
     def gather_own(self, stream):
-        r = self.route
-        for peer in r.column(r.me)[1:]:
-            self.share(stream, r.me, peer, 0)
-        self.share(stream, r.me, r.near, 1)
-        self.share(stream, r.me, r.far, 2)
+        p, r = self.parts, self.route
+
+        def act(shards):
+            view = shards.at[r.level, r.me, :, p.half(r.core)]
+            for level in r.levels():
+                self.send(
+                    view, view, p.gather_send.at[stream, 0], p.gather_recv.at[stream, 0], level, r.me, r.core
+                )
+
+        p.on(stream, act)
 
     def gather_column(self, stream):
         p, r = self.parts, self.route
         drain(p.several(3), p.gather_recv.at[stream, 0])
-        for shard in r.column(r.me)[1:]:
-            self.share(stream, shard, r.near, 1)
-            self.share(stream, shard, r.far, 2)
-        for shard in r.column(r.me)[1:]:
-            self.hand_over(stream, shard)
+
+        def act(shards):
+            view = shards.at[:, r.me, :, p.half(r.core)]
+            self.share(stream, view, r.near, 1)
+            self.share(stream, view, r.far, 2)
+            for level in r.levels():
+                self.hand_over(stream, shards.at[level, r.me, :, p.half(r.core)])
+
+        p.on(stream, act)
 
     def gather_near(self, stream):
         p, r = self.parts, self.route
         drain(p.several(4), p.gather_recv.at[stream, 1])
-        for shard in r.column(r.near):
-            self.share(stream, shard, r.far, 2)
-        for shard in r.column(r.near):
-            self.hand_over(stream, shard)
+
+        def act(shards):
+            view = shards.at[:, r.near, :, p.half(r.core)]
+            self.share(stream, view, r.far, 2)
+            self.hand_over(stream, view)
+
+        p.on(stream, act)
 
     def gather_far(self, stream):
         p, r = self.parts, self.route
         drain(p.several(8), p.gather_recv.at[stream, 2])
-        for shard in r.column(r.far) + r.column(r.across):
-            self.hand_over(stream, shard)
+
+        def act(shards):
+            for place in (r.far, r.across):
+                self.hand_over(stream, shards.at[:, place, :, p.half(r.core)])
+
+        p.on(stream, act)
 
     def gathered(self, stream):
         p = self.parts
@@ -236,67 +272,82 @@
         drain(p.several(15), p.gather_send.at[stream, 1])
 
 
-    def add(self, stream, shard, kind, index):
+    def pass_on(self, stream, view, landing, kind, level, place):
         p, r = self.parts, self.route
-        view = p.window(stream, shard, r.core)
-        landed = p.landing(stream, kind, index)
-        view[...] = (view[...].astype(f32) + landed[...].astype(f32)).astype(view.dtype)
-
-    def pass_on(self, stream, shard, kind, index, chip):
-        p, r = self.parts, self.route
-        remote(
-            p.window(stream, shard, r.core), p.landing(stream, kind, index),
-            p.sum_send.at[stream], p.sum_recv.at[stream, kind], chip, r.core,
-        ).start()
+        self.send(view, landing, p.sum_send.at[stream], p.sum_recv.at[stream, kind], level, place, r.core)
 
     def sum_cores(self, stream):
         p, r = self.parts, self.route
-        for shard in range(16):
-            remote(
-                p.window(stream, shard, 1 - r.core), p.landing(stream, 0, shard),
-                p.sum_send.at[stream], p.sum_recv.at[stream, 0], r.me, 1 - r.core,
-            ).start()
+
+        def act(shards):
+            self.send(
+                shards.at[:, :, :, p.half(1 - r.core)], p.landing(stream, 0),
+                p.sum_send.at[stream], p.sum_recv.at[stream, 0], r.level, r.me, 1 - r.core,
+            )
+
+        p.on(stream, act)
 
     def sum_far(self, stream):
         p, r = self.parts, self.route
         drain(p.several(16), p.sum_recv.at[stream, 0])
-        leaving = r.column(r.far) + r.column(r.across)
-        for index, shard in enumerate(leaving):
-            self.add(stream, shard, 0, shard)
-        for index, shard in enumerate(leaving):
-            self.pass_on(stream, shard, 1, index, r.far)
-        for shard in r.column(r.me) + r.column(r.near):
-            self.add(stream, shard, 0, shard)
+        landed, target = p.landing(stream, 0), p.landing(stream, 1)
+
+        def act(shards):
+            def add(place):
+                view = shards.at[:, place, :, p.half(r.core)]
+                view[...] += landed[:, place]
+                return view
+
+            for index, place in enumerate((r.far, r.across)):
+                self.pass_on(stream, add(place), target.at[index], 1, r.level, r.far)
+            for place in (r.me, r.near):
+                add(place)
+
+        p.on(stream, act)
 
     def sum_near(self, stream):
         p, r = self.parts, self.route
         drain(p.several(8), p.sum_recv.at[stream, 1])
-        for index, shard in enumerate(r.column(r.near)):
-            self.add(stream, shard, 1, 4 + index)
-        for index, shard in enumerate(r.column(r.near)):
-            self.pass_on(stream, shard, 2, index, r.near)
-        for index, shard in enumerate(r.column(r.me)):
-            self.add(stream, shard, 1, index)
+        landed, target = p.landing(stream, 1), p.landing(stream, 2)
+
+        def act(shards):
+            view = shards.at[:, r.near, :, p.half(r.core)]
+            view[...] += landed[1]
+            self.pass_on(stream, view, target.at[0], 2, r.level, r.near)
+            view = shards.at[:, r.me, :, p.half(r.core)]
+            view[...] += landed[0]
+
+        p.on(stream, act)
 
     def sum_column(self, stream):
         p, r = self.parts, self.route
         drain(p.several(4), p.sum_recv.at[stream, 2])
-        shards = r.column(r.me)
-        for index in range(1, 4):
-            self.add(stream, shards[index], 2, index)
-        for index in range(1, 4):
-            self.pass_on(stream, shards[index], 3, index - 1, shards[index])
-        self.add(stream, shards[0], 2, 0)
+        landed, target = p.landing(stream, 2), p.landing(stream, 3)
+
+        def act(shards):
+            view = shards.at[:, r.me, :, p.half(r.core)]
+            view[...] += landed[0]
+            for index, level in enumerate(r.levels()):
+                self.pass_on(
+                    stream, shards.at[level, r.me, :, p.half(r.core)], target.at[0, index], 3, level, r.me
+                )
+
+        p.on(stream, act)
 
     def sum_end(self, stream):
         p, r = self.parts, self.route
         drain(p.several(3), p.sum_recv.at[stream, 3])
-        total = p.window(stream, r.me, r.core)[...].astype(f32)
-        for index in range(3):
-            total += p.landing(stream, 3, index)[...].astype(f32)
+        landed = p.landing(stream, 3)
         view = p.result(stream, r.core)
-        view[...] = total
-        remote(view, view, p.final_sem.at[0], p.final_sem.at[1], r.me, 1 - r.core).start()
+
+        def act(shards):
+            total = shards[r.level, r.me, :, p.half(r.core)].astype(f32)
+            for index in range(3):
+                total += landed[0, index].astype(f32)
+            view[...] = total
+
+        p.on(stream, act)
+        self.send(view, view, p.final_sem.at[0], p.final_sem.at[1], r.level, r.me, 1 - r.core)
 
     def summed(self, stream):
         p = self.parts
@@ -366,12 +417,13 @@
 
     if comm:
         route = Route()
+        chip = route.chip(route.level, route.me)
         blocks = Exchange(route, Streams(held, stage, final, block_sems))
         extras = Exchange(route, Vectors(small, small_stage, small_final, [*small_sems, *small_final_sems]))
         sums = Exchange(route, Vectors(g_small, small_stage, small_final, [*small_sems, *small_final_sems]))
         barrier = pltpu.get_barrier_semaphore()
-        for chip, core in route.peers():
-            pl.semaphore_signal(barrier, inc=1, device_id=(chip, core), device_id_type=pl.DeviceIdType.MESH)
+        for peer, core in route.peers():
+            pl.semaphore_signal(barrier, inc=1, device_id=(peer, core), device_id_type=pl.DeviceIdType.MESH)
         moves = []
         for quad in range(quads):
             for part in range(3):
@@ -395,7 +447,7 @@
             copy.start()
 
         def round_block(block):
-            at = pl.ds(pl.multiple_of(block * BLOCK + PIECE * route.me, 16), PIECE)
+            at = pl.ds(pl.multiple_of(block * BLOCK + PIECE * chip, 16), PIECE)
             held[at, :] = total[block * PIECE : (block + 1) * PIECE, :].astype(bf16)
 
         g_small[:8, :] = jnp.zeros((8, SMALL), f32)
@@ -409,7 +461,7 @@
         for row in range(8):
             value = small_held[row][...].astype(bf16).astype(f32)
             g_small[row : row + 1, 128 : 128 + value.shape[1]] = value
-        small[pl.ds(pl.multiple_of(route.me * 8, 8), 8), :] = g_small[:8, :]
+        small[pl.ds(pl.multiple_of(chip * 8, 8), 8), :] = g_small[:8, :]
         pl.semaphore_wait(barrier, 6)
         extras.gather_own(0)
         for stream in range(quads):
@@ -418,9 +470,10 @@
             copy.wait()
         for block in range(quads, STREAMS - up_blocks):
             round_block(block)
-        at = pl.ds(pl.multiple_of(down_at + 4 * PIECE * route.me, 16), 4 * PIECE)
+        at = pl.ds(pl.multiple_of(down_at + 4 * PIECE * chip, 16), 4 * PIECE)
         held[at, :] = total[8 * PIECE : 12 * PIECE, :].astype(bf16)
-        blocks.gather_own(quads)
+        for stream in range(quads, STREAMS):
+            blocks.gather_own(stream)
     else:
         for copy in (coord_copy, seg_copy, tok_copy, cot_copy):
             copy.start()
@@ -453,6 +506,7 @@
         blocks.gather_far(0)
         blocks.gather_near(1)
         blocks.gather_column(2)
+        blocks.gather_column(3)
         extras.gathered(0)
         table = small[...].astype(bf16)
         w_box[...] = table[:, :HD]
@@ -477,8 +531,12 @@
     def gather_tick(step):
         if not comm:
             return
-        for ahead, act_on in enumerate((blocks.gather_far, blocks.gather_near, blocks.gather_column, blocks.gather_own)):
-            pl.when(step + ahead < STREAMS)(functools.partial(act_on, step + ahead))
+        for ahead, act_on in ((1, blocks.gather_near), (3, blocks.gather_column), (0, blocks.gather_far)):
+            if isinstance(step, int):
+                if step + ahead < STREAMS:
+                    act_on(step + ahead)
+            else:
+                pl.when(step + ahead < STREAMS)(functools.partial(act_on, step + ahead))
 
     def need(stream):
         if comm:
@@ -572,7 +630,7 @@
         def _(inner):
             step = quad * quad_steps + inner
             if comm:
-                pl.when(step % 2 == 1)(functools.partial(gather_tick, (step + 1) // 2))
+                pl.when((step % 2 == 0) & (step > 0))(functools.partial(gather_tick, step // 2))
             attend(step)
 
     for place in range(2):
@@ -583,7 +641,7 @@
         return jnp.sum(value, axis=0, keepdims=True)
 
     need(3)
-    gather_tick(7)
+    gather_tick(6)
 
     @pl.loop(0, row_blocks)
     def _(block):
@@ -602,7 +660,7 @@
 
     @pl.loop(0, up_blocks)
     def _(block):
-        gather_tick(8 + block)
+        gather_tick(7 + block)
         need(4 + block)
 
         @pl.loop(0, row_blocks)
@@ -615,6 +673,7 @@
             act[at, :] = (up * cdf).astype(bf16)
             slope[at, :] = (cdf + up * pdf).astype(bf16)
 
+    gather_tick(11)
     for block in range(up_blocks):
         need(8 + block)
     cot_copy.wait()
@@ -669,8 +728,8 @@
 
     def meet(sem):
         if comm:
-            for chip, core in route.peers():
-                pl.semaphore_signal(sem, inc=1, device_id=(chip, core), device_id_type=pl.DeviceIdType.MESH)
+            for peer, core in route.peers():
+                pl.semaphore_signal(sem, inc=1, device_id=(peer, core), device_id_type=pl.DeviceIdType.MESH)
             pl.semaphore_wait(sem, 6)
 
     out_copy.wait()
@@ -690,6 +749,8 @@
             slope[at, :] = g_up
             g_b_up[:, aligned(block, BLOCK)] += column_sum(g_up.astype(f32))
             total[rows, :] += dot_nt(g_up, held[up_rows, :])
+        sum_tick(index - 1, (0,))
+        sum_tick(index - 1, (1, 2, 3))
         g_up = slope[aligned(block, count), :]
         for part in range(2):
             at = pl.ds(pl.multiple_of(up_at + block * BLOCK + part * HALF, HALF), HALF)
@@ -699,10 +760,10 @@
             at = pl.ds(pl.multiple_of(down_at + block * BLOCK + part * HALF, HALF), HALF)
             grads = dot_tn(act[aligned(block, count), part * HALF : (part + 1) * HALF], g_down[...])
             held[at, :] = grads.astype(bf16)
-        sum_tick(index)
 
     if comm:
         meet(mid_sem.at[1])
+    sum_tick(3)
     for step in range(up_blocks):
         sum_start(up_blocks + step)
 
@@ -786,12 +847,8 @@
             at = pl.ds(pl.multiple_of(part * QUAD + pair % 2 * PAIR, PAIR), PAIR)
             flip[at, cols] = jnp.concatenate(g_parts[part], axis=0).astype(bf16)
 
-    def token_grad():
-        @pl.loop(0, row_blocks)
-        def _(block):
-            rows = aligned(block, ROWS)
-            part = dot_nn(slope[:BLOCK, :], flip[:, rows])
-            total[rows, :] += jnp.transpose(part)
+    kept = slope.at[3 * count : 3 * count + BLOCK]
+    kept_last = g_down.at[:BLOCK]
 
     @pl.loop(0, quads)
     def _(turn):
@@ -801,21 +858,48 @@
         def _(inner):
             order = turn * quad_steps + inner
             if comm:
-                pl.when(order % 2 == 0)(functools.partial(sum_tick, 5 + order // 2, (0,)))
-                pl.when(order % 2 == 1)(functools.partial(sum_tick, 5 + order // 2, (1, 2, 3)))
+                pl.when(order % 2 == 1)(functools.partial(sum_tick, 5 + order // 2, (0,)))
+                pl.when((order % 2 == 0) & (order > 0))(functools.partial(sum_tick, 4 + order // 2, (1, 2, 3)))
             attend_back(order)
 
-        slope[:BLOCK, :] = held[aligned(quad, BLOCK), :]
+        if comm:
+            pl.when(turn == quads - 1)(functools.partial(sum_tick, 10, (1, 2, 3)))
+
+        @pl.when(turn < quads - 1)
+        def _():
+            kept[...] = held[aligned(quad, BLOCK), :]
+
+        @pl.when(turn == quads - 1)
+        def _():
+            kept_last[...] = held[aligned(quad, BLOCK), :]
+
         for part in range(2):
             at = pl.ds(pl.multiple_of(quad * BLOCK + part * HALF, HALF), HALF)
             held[at, :] = dot_nt(tok_t[part * HALF : (part + 1) * HALF, :], flip[...]).astype(bf16)
         sum_start(9 + turn)
         g_b_qkv[:, aligned(quad, BLOCK)] = dot_nt(ones, flip[...])[:1]
-        token_grad()
+
+        @pl.when(turn == 0)
+        def _():
+            for block in range(row_blocks):
+                rows = slice(block * ROWS, (block + 1) * ROWS)
+                total[rows, :] += jnp.transpose(dot_nn(kept[...], flip[:, rows]))
+
+        @pl.when(turn == 1)
+        def _():
+            for block in range(row_blocks):
+                rows = slice(block * ROWS, (block + 1) * ROWS)
+                slope[rows, :] = jnp.transpose(flip[:, rows].astype(f32)).astype(bf16)
 
     g_w_box[...] = g_w_box[...] * (1.0 / scale_factor)
-    tok_out = pltpu.make_async_copy(total, g_tok_out, io_sem.at[0])
-    tok_out.start()
+    tok_out = []
+
+    def token_grad(block):
+        rows = slice(block * ROWS, (block + 1) * ROWS)
+        last_part = jnp.transpose(dot_nn(kept_last[...], flip[:, rows]))
+        total[rows, :] += last_part + dot_nt(slope[rows, :], kept[...])
+        tok_out.append(pltpu.make_async_copy(total.at[rows], g_tok_out.at[rows], io_sem.at[4 + block]))
+        tok_out[-1].start()
 
     if comm:
         g_small[...] = jnp.zeros_like(g_small)
@@ -842,11 +926,15 @@
         sum_tick(11, (0,))
         sums.sum_far(0)
         sum_tick(12, (2, 3))
+        token_grad(0)
+        token_grad(1)
         sum_tick(12, (1,))
         sums.sum_near(0)
+        token_grad(2)
         sum_tick(13, (3,))
         sum_tick(13, (2,))
         sums.sum_column(0)
+        token_grad(3)
         sum_tick(14, (3,))
         sums.sum_end(0)
         for stream in range(STREAMS):
@@ -860,6 +948,8 @@
         for copy in moves:
             copy.wait()
     else:
+        for block in range(row_blocks):
+            token_grad(block)
         g_w_box_out[...] = g_w_box[...]
         g_b_qkv_out[...] = g_b_qkv[...]
         g_b_up_out[...] = g_b_up[...]
@@ -867,7 +957,8 @@
         out = copy_in(held, g_held, 2)
         out.start()
         out.wait()
-    tok_out.wait()
+    for copy in tok_out:
+        copy.wait()
 
 
 def shaped(shape, dtype):
@@ -1027,7 +1118,7 @@
             pltpu.VMEM(layer_out.shape, bf16), pltpu.VMEM(g_tok.shape, f32), pltpu.VMEM(blocks.shape, f32),
             pltpu.VMEM(small.shape, f32), *[pltpu.VMEM(v.shape, f32) for v in little], dma((16,)), dma((40,)),
         ],
-        compiler_params=pltpu.CompilerParams(vmem_limit_bytes=16_000_000),
+        compiler_params=pltpu.CompilerParams(vmem_limit_bytes=vmem_limit),
         name="finish",
     )(layer_out, g_tok, blocks, small)
 

time: 208 us -> 197 us (0.947)
  Pallas kernels: 202 us -> 196 us
  local copies, waits for them, and re-layouts: 5.48 us -> 0 us
    pallas_call x1, Pallas kernels: 197 us -> 191 us  [run_layer(): pl.pallas_call(functools.partial(layer_kernel, comm), out_shape=out_shape...]
    unnamed x8 -> x0, local copies, waits for them, and re-layouts: 5.48 us -> none
where the time goes in v4:
time: 197 us
  Pallas kernels  196 us (99%)
    pallas_call x1, Pallas kernels, run_layer(): pl.pallas_call(functools.partial(layer_kernel, comm), out_shape=out_shape...  191 us
    pallas_call x1, Pallas kernels, run_finish(): pl.pallas_call(finish_kernel, out_shape=shapes, in_specs=in_hbm(4), out_s...  5.21 us

profile of v4, /device:TPU:0, one launch (start us, length us, event | category | flops | bytes accessed | tf_op | source)
XLA Modules:
  0.0 196.6 jit_solution(17742340434956130567)
XLA Ops:
  0.7 190.5 %layer.1 = (bf16[1024,768]{1,0:T(8,128)(2,1)}, f32[1024,768]{1,0:T(8,128)}, bf16[24,512,512]{2,1,0:T(8,128)(2,1)}, f32[576,768]{1,0:T(8,128)}, f32[8,512]{1,0:T(8,128)}) custom-call(bf16[1024,768]{1,0:T(8,128)(2,1)} %refs_0_.1, bf16[1024,768]{1,0:T(8,128)(2,1)} %refs_1_.1, s32[4,1024]{1,0:T(4,128)} %refs_2_.1, s32[1,1024]{1,0:T(1,128)} %bitcast.17, ...), custom_call_target="tpu_custom_call" | custom-call | tf_op jit(solution)/shard_map/layer/pallas_call | solution.py:1045
  191.2 5.2 %finish.1 = (bf16[1024,768]{1,0:T(8,128)(2,1)}, f32[1024,768]{1,0:T(8,128)}, f32[48,2304]{1,0:T(8,128)}, f32[48,768]{1,0:T(8,128)}, f32[48,3072]{1,0:T(8,128)}, ...) custom-call(bf16[1024,768]{1,0:T(8,128)(2,1)} %get-tuple-element.34., ...), custom_call_target="tpu_custom_call" | custom-call | tf_op jit(solution)/shard_map/finish/pallas_call | solution.py:1112

commit v5 on v4

--- a/solution.py
+++ b/solution.py
@@ -67,13 +67,11 @@
 
 
 def gelu_parts(value):
-    size = jnp.abs(value) * math.sqrt(0.5)
-    t = 1.0 / (1.0 + 0.3275911 * size)
-    bell = jnp.exp(-0.5 * value * value)
-    tail = t * (
-        0.254829592 + t * (-0.284496736 + t * (1.421413741 + t * (-1.453152027 + t * 1.061405429)))
+    t = 1.0 / (1.0 + (0.3275911 * math.sqrt(0.5)) * jnp.abs(value))
+    bell = jnp.exp2(value * value * (-0.5 * math.log2(math.e)))
+    half_tail = bell * t * (
+        0.127414796 + t * (-0.142248368 + t * (0.7107068705 + t * (-0.7265760135 + t * 0.5307027145)))
     )
-    half_tail = 0.5 * tail * bell
     return jnp.where(value >= 0, 1.0 - half_tail, half_tail), bell * (1.0 / math.sqrt(2.0 * math.pi))
 
 
@@ -391,7 +389,7 @@
     else:
         g_held, g_w_box_out, g_b_qkv_out, g_b_up_out, g_vectors_out = take(5)
     (held, stage, slope, q8t, k8t, v_row, ctx_t, wave_t, wave_r, e_buf, normed, total, flip, g_down, tok_t, g_ctx_t,
-     inv_one, inv_total, w_box, w_box_t, b_qkv, b_up, vectors, g_w_box, g_b_qkv, g_b_up, g_vectors, e_sem, io_sem, coords, segs) = take(31)
+     inv_one, inv_total, w_box, w_box_t, b_qkv, b_up, vectors, g_w_box, g_b_qkv, g_b_up, g_vectors, e_sem, io_sem, coords, segs, w_pair, w_pair_t) = take(33)
     if comm:
         final, small, small_stage, g_small, small_final, mid_sem = take(6)
         small_held = take(9)
@@ -527,6 +525,10 @@
     else:
         copy_in(held_in, held, 4).wait()
     w_box_t[...] = jnp.transpose(w_box[...].astype(f32)).astype(bf16)
+    blank = jnp.zeros((2 * WAVE, HD), bf16)
+    w_pair_t[: 2 * WAVE, :] = jnp.concatenate([w_box[...], blank], axis=1)
+    w_pair_t[2 * WAVE :, :] = jnp.concatenate([blank, w_box[...]], axis=1)
+    w_pair[...] = jnp.transpose(w_pair_t[...].astype(f32)).astype(bf16)
 
     def gather_tick(step):
         if not comm:
@@ -544,6 +546,7 @@
 
     b_out, gain_one, shift_one, b_down, gain_two, shift_two = [vectors[2 + i : 3 + i, :] for i in range(VECTORS)]
     lane = lax.broadcasted_iota(jnp.int32, (SLOT, PAIR), 1)
+    scores = total.reshape(2, SLOT, width)
 
     def project(quad, slot):
         rows = tok[aligned(slot, SLOT), :]
@@ -586,31 +589,35 @@
         ss_r = jnp.where(lane < WAVE, sc_r, -cs_r)
         cs_low = cs_r.astype(bf16)
         keys = low[cols, aligned(pair, PAIR)]
-        heads_t = []
+        queries = q8t[slot, pair]
+        key_box = dot_nn(keys, w_pair[...])
+        query_box = dot_nn(w_pair_t[...], queries)
+        low_exps, inverse, heads_t = [], [], []
         for head in range(2):
-            span = slice(head * HD, (head + 1) * HD)
-            key_box = dot_nt(keys[:, span], w_box[...])
-            k_side = (key_box * cc_r + swap_lanes(key_box) * ss_r).astype(bf16)
-            q_t = q8t[slot, pair, span, :]
-            query_box = dot_nn(w_box[...], q_t)
-            first, second = query_box[:WAVE], query_box[WAVE:]
+            here = slice(head * 2 * WAVE, (head + 1) * 2 * WAVE)
+            side = key_box[:, here]
+            k_side = (side * cc_r + swap_lanes(side) * ss_r).astype(bf16)
+            first, second = query_box[here][:WAVE], query_box[here][WAVE:]
             q_side = jnp.concatenate(
                 [first * sine_t + second * cosine_t, second * sine_t - first * cosine_t], axis=0
             ).astype(bf16)
+            q_t = queries[head * HD : (head + 1) * HD]
             zero = jnp.zeros_like(q_t)
             q_pair = [q_t, zero] if head == 0 else [zero, q_t]
             k_full = jnp.concatenate([keys, cs_low, k_side], axis=1)
             q_full = jnp.concatenate(q_pair + [q_side, sc_t], axis=0)
-            scores = dot_nn(k_full, q_full) + normed[cols, :SLOT]
-            top = jnp.max(scores, axis=0, keepdims=True)
-            exps = jnp.exp(scores - top)
-            inverse = 1.0 / jnp.sum(exps, axis=0, keepdims=True)
-            low_exps = exps.astype(bf16)
-            e_buf[place, head] = low_exps
+            scores[head, :, :SLOT] = dot_nn(k_full, q_full) + normed[cols, :SLOT]
+        for head in range(2):
+            masked = scores[head, :, :SLOT]
+            exps = jnp.exp(masked - jnp.max(masked, axis=0, keepdims=True))
+            inverse.append(1.0 / jnp.sum(exps, axis=0, keepdims=True))
+            low_exps.append(exps.astype(bf16))
+            e_buf[place, head] = low_exps[head]
             e_copy(place, head, step * 2 + head, True).start()
-            inv_total[step * 2 + head] = inverse
+            inv_total[step * 2 + head] = inverse[head]
+        for head in range(2):
             at = pl.ds(pl.multiple_of(pair * PAIR + head * HD, HD), HD)
-            heads_t.append(dot_nn(flip[at, cols], low_exps) * inverse)
+            heads_t.append(dot_nn(flip[at, cols], low_exps[head]) * inverse[head])
         both = jnp.concatenate(heads_t, axis=0)
         ctx_t[aligned(pair, PAIR), cols] = both.astype(bf16)
         ctx[cols, aligned(pair, PAIR)] = jnp.transpose(both).astype(bf16)
@@ -663,12 +670,13 @@
         gather_tick(7 + block)
         need(4 + block)
 
-        @pl.loop(0, row_blocks)
-        def _(row):
-            rows = aligned(row, ROWS)
+        weight = held[pl.ds(pl.multiple_of(up_at + block * BLOCK, BLOCK), BLOCK), :]
+        for row in range(row_blocks):
+            rows = slice(row * ROWS, (row + 1) * ROWS)
+            total[rows, :] = dot_nn(low[rows, :], weight) + b_up[:, aligned(block, BLOCK)]
+        for row in range(row_blocks):
             at = pl.ds(pl.multiple_of(block * count + row * ROWS, ROWS), ROWS)
-            weight = held[pl.ds(pl.multiple_of(up_at + block * BLOCK, BLOCK), BLOCK), :]
-            up = dot_nn(low[rows, :], weight) + b_up[:, aligned(block, BLOCK)]
+            up = total[row * ROWS : (row + 1) * ROWS, :]
             cdf, pdf = gelu_parts(up)
             act[at, :] = (up * cdf).astype(bf16)
             slope[at, :] = (cdf + up * pdf).astype(bf16)
@@ -779,12 +787,13 @@
         g_vectors[2:3, :] += column_sum(low_pre.astype(f32))
         g_vectors[3:4, :] += column_sum(grad * unit)
         g_vectors[4:5, :] += column_sum(grad)
-        g_ctx_t[:, rows] = dot_nt(held[3 * BLOCK : 4 * BLOCK, :], low_pre).astype(bf16)
-
-    @pl.loop(0, BLOCK // ROWS)
-    def _(part):
-        at = pl.ds(pl.multiple_of(3 * BLOCK + part * ROWS, ROWS), ROWS)
-        held[at, :] = dot_nn(ctx_t[aligned(part, ROWS), :], g_down[...]).astype(bf16)
+
+    for part in range(2):
+        rows = slice(part * (count // 2), (part + 1) * (count // 2))
+        g_ctx_t[:, rows] = dot_nt(held[3 * BLOCK : 4 * BLOCK, :], g_down[rows, :]).astype(bf16)
+    for part in range(2):
+        at = slice(3 * BLOCK + part * HALF, 3 * BLOCK + (part + 1) * HALF)
+        held[at, :] = dot_nn(ctx_t[part * HALF : (part + 1) * HALF, :], g_down[...]).astype(bf16)
 
     sum_start(8)
     sum_tick(4)
@@ -816,22 +825,28 @@
         sc_t = (wave_t[:, cols] * scale_factor).astype(bf16)
         cs_t = (jnp.concatenate([cosine_t, sine_t], axis=0) * scale_factor).astype(bf16)
         values = v_row[slot, pair]
+        g_lows, row_dots, g_probs, g_scores, g_qs, g_ks = [], [], [], [], [], []
         g_parts = [[], [], []]
+        spans = [slice(head * HD, (head + 1) * HD) for head in range(2)]
         for head in range(2):
-            span = slice(head * HD, (head + 1) * HD)
             at = pl.ds(pl.multiple_of(pair * PAIR + head * HD, HD), HD)
             g_rows = g_ctx_t[at, cols].astype(f32) * inv_total[step * 2 + head]
-            row_dot = jnp.sum(g_rows * ctx_t[at, cols].astype(f32), axis=0, keepdims=True)
-            g_low = g_rows.astype(bf16)
-            zero = jnp.zeros_like(g_low)
-            g_pair = jnp.concatenate([g_low, zero] if head == 0 else [zero, g_low], axis=0)
-            low_exps = e_buf[place, head]
-            g_probs = dot_nn(values, g_pair)
-            g_scores = (low_exps.astype(f32) * (g_probs - row_dot)).astype(bf16)
-            g_parts[2].append(dot_nt(g_low, low_exps))
-            k_t, q_t = k8t[slot, pair, span, :], q8t[slot, pair, span, :]
-            g_q = dot_nn(jnp.concatenate([k_t, cs_t], axis=0), g_scores)
-            g_k = dot_nt(jnp.concatenate([q_t, sc_t], axis=0), g_scores)
+            row_dots.append(jnp.sum(g_rows * ctx_t[at, cols].astype(f32), axis=0, keepdims=True))
+            g_lows.append(g_rows.astype(bf16))
+            zero = jnp.zeros_like(g_lows[head])
+            g_pair = jnp.concatenate([g_lows[head], zero] if head == 0 else [zero, g_lows[head]], axis=0)
+            g_probs.append(dot_nn(values, g_pair))
+        for head in range(2):
+            g_scores.append((e_buf[place, head].astype(f32) * (g_probs[head] - row_dots[head])).astype(bf16))
+        for head in range(2):
+            g_qs.append(dot_nn(jnp.concatenate([k8t[slot, pair, spans[head], :], cs_t], axis=0), g_scores[head]))
+        for head in range(2):
+            g_ks.append(dot_nt(jnp.concatenate([q8t[slot, pair, spans[head], :], sc_t], axis=0), g_scores[head]))
+        for head in range(2):
+            g_parts[2].append(dot_nt(g_lows[head], e_buf[place, head]))
+        for head in range(2):
+            k_t, q_t = k8t[slot, pair, spans[head], :], q8t[slot, pair, spans[head], :]
+            g_q, g_k = g_qs[head], g_ks[head]
             first, second = g_q[HD : HD + WAVE], g_q[HD + WAVE :]
             g_qbox = jnp.concatenate(
                 [first * sine_t - second * cosine_t, first * cosine_t + second * sine_t], axis=0
@@ -1025,6 +1040,8 @@
         dma((32,)),
         vmem(coords.shape, jnp.int32),
         vmem(segs.shape, jnp.int32),
+        vmem((PAIR, 4 * WAVE), bf16),
+        vmem((4 * WAVE, PAIR), bf16),
     ]
     if comm:
         scratch += [

time: 197 us -> 191 us (0.970)
  Pallas kernels: 196 us -> 190 us
    pallas_call x1, Pallas kernels: 191 us -> 185 us  [run_layer(): pl.pallas_call(functools.partial(layer_kernel, comm), out_shape=out_shape...]
where the time goes in v5:
time: 191 us
  Pallas kernels  190 us (99%)
    pallas_call x1, Pallas kernels, run_layer(): pl.pallas_call(functools.partial(layer_kernel, comm), out_shape=out_shape...  185 us
    pallas_call x1, Pallas kernels, run_finish(): pl.pallas_call(finish_kernel, out_shape=shapes, in_specs=in_hbm(4), out_s...  5.21 us

profile of v5, /device:TPU:0, one launch (start us, length us, event | category | flops | bytes accessed | tf_op | source)
XLA Modules:
  0.0 191.1 jit_solution(4428000978131943413)
XLA Ops:
  0.7 185.0 %layer.1 = (bf16[1024,768]{1,0:T(8,128)(2,1)}, f32[1024,768]{1,0:T(8,128)}, bf16[24,512,512]{2,1,0:T(8,128)(2,1)}, f32[576,768]{1,0:T(8,128)}, f32[8,512]{1,0:T(8,128)}) custom-call(bf16[1024,768]{1,0:T(8,128)(2,1)} %refs_0_.1, bf16[1024,768]{1,0:T(8,128)(2,1)} %refs_1_.1, s32[4,1024]{1,0:T(4,128)} %refs_2_.1, s32[1,1024]{1,0:T(1,128)} %bitcast.17, ...), custom_call_target="tpu_custom_call" | custom-call | tf_op jit(solution)/shard_map/layer/pallas_call | solution.py:1062
  185.7 5.2 %finish.1 = (bf16[1024,768]{1,0:T(8,128)(2,1)}, f32[1024,768]{1,0:T(8,128)}, f32[48,2304]{1,0:T(8,128)}, f32[48,768]{1,0:T(8,128)}, f32[48,3072]{1,0:T(8,128)}, ...) custom-call(bf16[1024,768]{1,0:T(8,128)(2,1)} %get-tuple-element.34., ...), custom_call_target="tpu_custom_call" | custom-call | tf_op jit(solution)/shard_map/finish/pallas_call | solution.py:1129

commit v6 on v5

--- a/solution.py
+++ b/solution.py
@@ -86,6 +86,7 @@
 SMALL = 512
 STREAMS = 12
 VECTORS = 6
+LEVEL_FIRST = 7
 
 
 def widths(width, ff):
@@ -257,6 +258,53 @@
         def act(shards):
             for place in (r.far, r.across):
                 self.hand_over(stream, shards.at[:, place, :, p.half(r.core)])
+
+        p.on(stream, act)
+
+
+    def level_own(self, stream):
+        p, r = self.parts, self.route
+
+        def act(shards):
+            view = shards.at[r.level, r.me, :, p.half(r.core)]
+            self.share(stream, view, r.near, 1)
+            self.share(stream, view, r.far, 2)
+
+        p.on(stream, act)
+
+    def level_near(self, stream):
+        p, r = self.parts, self.route
+        drain(p.several(1), p.gather_recv.at[stream, 1])
+
+        def act(shards):
+            view = shards.at[r.level, r.near, :, p.half(r.core)]
+            self.share(stream, view, r.far, 2)
+            self.hand_over(stream, view)
+
+        p.on(stream, act)
+
+    def level_far(self, stream):
+        p, r = self.parts, self.route
+        drain(p.several(2), p.gather_recv.at[stream, 2])
+
+        def act(shards):
+            view = shards.at[r.level, :, :, p.half(r.core)]
+            for level in r.levels():
+                self.send(
+                    view, view, p.gather_send.at[stream, 0], p.gather_recv.at[stream, 0], level, r.me, r.core
+                )
+            for place in (r.far, r.across):
+                self.hand_over(stream, shards.at[r.level, place, :, p.half(r.core)])
+
+        p.on(stream, act)
+
+    def level_column(self, stream):
+        p, r = self.parts, self.route
+        drain(p.several(12), p.gather_recv.at[stream, 0])
+
+        def act(shards):
+            for level in r.levels():
+                self.hand_over(stream, shards.at[level, :, :, p.half(r.core)])
 
         p.on(stream, act)
 
@@ -470,8 +518,10 @@
             round_block(block)
         at = pl.ds(pl.multiple_of(down_at + 4 * PIECE * chip, 16), 4 * PIECE)
         held[at, :] = total[8 * PIECE : 12 * PIECE, :].astype(bf16)
+        blocks.level_own(LEVEL_FIRST)
         for stream in range(quads, STREAMS):
-            blocks.gather_own(stream)
+            if stream != LEVEL_FIRST:
+                blocks.gather_own(stream)
     else:
         for copy in (coord_copy, seg_copy, tok_copy, cot_copy):
             copy.start()
@@ -504,7 +554,7 @@
         blocks.gather_far(0)
         blocks.gather_near(1)
         blocks.gather_column(2)
-        blocks.gather_column(3)
+        blocks.level_near(LEVEL_FIRST)
         extras.gathered(0)
         table = small[...].astype(bf16)
         w_box[...] = table[:, :HD]
@@ -533,12 +583,17 @@
     def gather_tick(step):
         if not comm:
             return
+
+        def stream_of(order):
+            return order + order // LEVEL_FIRST
+
         for ahead, act_on in ((1, blocks.gather_near), (3, blocks.gather_column), (0, blocks.gather_far)):
-            if isinstance(step, int):
-                if step + ahead < STREAMS:
-                    act_on(step + ahead)
+            order = step + ahead
+            if isinstance(order, int):
+                if order < STREAMS - 1:
+                    act_on(stream_of(order))
             else:
-                pl.when(step + ahead < STREAMS)(functools.partial(act_on, step + ahead))
+                pl.when(order < STREAMS - 1)(functools.partial(act_on, stream_of(order)))
 
     def need(stream):
         if comm:
@@ -637,6 +692,11 @@
         def _(inner):
             step = quad * quad_steps + inner
             if comm:
+                @pl.when(step == 1)
+                def _():
+                    blocks.gather_column(quads)
+                    blocks.level_far(LEVEL_FIRST)
+
                 pl.when((step % 2 == 0) & (step > 0))(functools.partial(gather_tick, step // 2))
             attend(step)
 
@@ -668,6 +728,8 @@
     @pl.loop(0, up_blocks)
     def _(block):
         gather_tick(7 + block)
+        if comm:
+            pl.when(block == 2)(functools.partial(blocks.level_column, LEVEL_FIRST))
         need(4 + block)
 
         weight = held[pl.ds(pl.multiple_of(up_at + block * BLOCK, BLOCK), BLOCK), :]
@@ -681,7 +743,6 @@
             act[at, :] = (up * cdf).astype(bf16)
             slope[at, :] = (cdf + up * pdf).astype(bf16)
 
-    gather_tick(11)
     for block in range(up_blocks):
         need(8 + block)
     cot_copy.wait()

time: 191 us -> 187 us (0.979)
  Pallas kernels: 190 us -> 186 us
    pallas_call x1, Pallas kernels: 185 us -> 180 us  [run_layer(): pl.pallas_call(functools.partial(layer_kernel, comm), out_shape=out_shape...]
where the time goes in v6:
time: 187 us
  Pallas kernels  186 us (99%)
    pallas_call x1, Pallas kernels, run_layer(): pl.pallas_call(functools.partial(layer_kernel, comm), out_shape=out_shape...  180 us
    pallas_call x1, Pallas kernels, run_finish(): pl.pallas_call(finish_kernel, out_shape=shapes, in_specs=in_hbm(4), out_s...  5.21 us

profile of v6, /device:TPU:0, one launch (start us, length us, event | category | flops | bytes accessed | tf_op | source)
XLA Modules:
  0.0 186.5 jit_solution(13839878288895054332)
XLA Ops:
  0.7 180.5 %layer.1 = (bf16[1024,768]{1,0:T(8,128)(2,1)}, f32[1024,768]{1,0:T(8,128)}, bf16[24,512,512]{2,1,0:T(8,128)(2,1)}, f32[576,768]{1,0:T(8,128)}, f32[8,512]{1,0:T(8,128)}) custom-call(bf16[1024,768]{1,0:T(8,128)(2,1)} %refs_0_.1, bf16[1024,768]{1,0:T(8,128)(2,1)} %refs_1_.1, s32[4,1024]{1,0:T(4,128)} %refs_2_.1, s32[1,1024]{1,0:T(1,128)} %bitcast.17, ...), custom_call_target="tpu_custom_call" | custom-call | tf_op jit(solution)/shard_map/layer/pallas_call | solution.py:1123
  181.2 5.2 %finish.1 = (bf16[1024,768]{1,0:T(8,128)(2,1)}, f32[1024,768]{1,0:T(8,128)}, f32[48,2304]{1,0:T(8,128)}, f32[48,768]{1,0:T(8,128)}, f32[48,3072]{1,0:T(8,128)}, ...) custom-call(bf16[1024,768]{1,0:T(8,128)(2,1)} %get-tuple-element.34., ...), custom_call_target="tpu_custom_call" | custom-call | tf_op jit(solution)/shard_map/finish/pallas_call | solution.py:1190

commit v7 on v6

--- a/solution.py
+++ b/solution.py
@@ -159,8 +159,8 @@
     def result(self, stream, half):
         return self.final.at[pl.ds(pl.multiple_of(stream * PIECE, 16), PIECE), self.half(half)]
 
-    def results(self):
-        return self.final.at[:, :HALF]
+    def results(self, last):
+        return self.final.at[:PIECE, :HALF] if last else self.final.at[PIECE:, :HALF]
 
 
 class Vectors:
@@ -187,7 +187,7 @@
     def result(self, stream, half):
         return self.final.at[:, self.half(half)]
 
-    def results(self):
+    def results(self, last):
         return self.final.at[:, : SMALL // 2]
 
 
@@ -393,16 +393,17 @@
             view[...] = total
 
         p.on(stream, act)
-        self.send(view, view, p.final_sem.at[0], p.final_sem.at[1], r.level, r.me, 1 - r.core)
+        last = 1 if isinstance(stream, int) and stream == 0 else 0
+        self.send(view, view, p.final_sem.at[last, 0], p.final_sem.at[last, 1], r.level, r.me, 1 - r.core)
 
     def summed(self, stream):
         p = self.parts
         drain(p.several(31), p.sum_send.at[stream])
 
-    def results_in(self):
+    def results_in(self, last):
         p = self.parts
-        drain(p.results(), p.final_sem.at[0])
-        drain(p.results(), p.final_sem.at[1])
+        for side in range(2):
+            drain(p.results(last), p.final_sem.at[last, side])
 
 
 def owner_tables(start, share, depth, order=None):
@@ -858,6 +859,26 @@
 
     sum_start(8)
     sum_tick(4)
+
+    def fold(block, row, share_of, source, order=None):
+        pick, owned, row_of = owner_tables(block * BLOCK, share_of, 256, order)
+        keep = owned if row is None else owned & (row_of == row)
+        wide = 1 if row is not None else 8
+        full = source[:, aligned(block, BLOCK)].reshape(1, wide, BLOCK)
+        spread = jnp.broadcast_to(full, (16, 8, BLOCK)).reshape(128, BLOCK)
+        spread = jnp.where(keep, spread, 0.0)
+        upper = spread.astype(bf16)
+        g_small[:, 128:384] += dot_nt(upper, pick) + dot_nt((spread - upper.astype(f32)).astype(bf16), pick)
+
+    if comm:
+        g_small[...] = jnp.zeros_like(g_small)
+        share_qkv, share_up, share = widths(width, ff)
+
+        @pl.loop(0, up_blocks)
+        def _(block):
+            fold(block, 1, share_up, g_b_up)
+
+        fold(0, None, share, g_vectors)
 
     def e_step(order):
         quad = quads - 1 - order // quad_steps
@@ -923,7 +944,7 @@
             at = pl.ds(pl.multiple_of(part * QUAD + pair % 2 * PAIR, PAIR), PAIR)
             flip[at, cols] = jnp.concatenate(g_parts[part], axis=0).astype(bf16)
 
-    kept = slope.at[3 * count : 3 * count + BLOCK]
+    kept = [slope.at[(2 + turn) * count : (2 + turn) * count + BLOCK] for turn in range(2)]
     kept_last = g_down.at[:BLOCK]
 
     @pl.loop(0, quads)
@@ -943,7 +964,8 @@
 
         @pl.when(turn < quads - 1)
         def _():
-            kept[...] = held[aligned(quad, BLOCK), :]
+            at = pl.ds(pl.multiple_of((2 + turn) * count, count), BLOCK)
+            slope[at, :] = held[aligned(quad, BLOCK), :]
 
         @pl.when(turn == quads - 1)
         def _():
@@ -954,18 +976,15 @@
             held[at, :] = dot_nt(tok_t[part * HALF : (part + 1) * HALF, :], flip[...]).astype(bf16)
         sum_start(9 + turn)
         g_b_qkv[:, aligned(quad, BLOCK)] = dot_nt(ones, flip[...])[:1]
-
-        @pl.when(turn == 0)
+        if comm:
+            fold(quad, 0, share_qkv, g_b_qkv, quad_order)
+
+        @pl.when(turn < quads - 1)
         def _():
             for block in range(row_blocks):
+                at = pl.ds(pl.multiple_of(turn * count + block * ROWS, ROWS), ROWS)
                 rows = slice(block * ROWS, (block + 1) * ROWS)
-                total[rows, :] += jnp.transpose(dot_nn(kept[...], flip[:, rows]))
-
-        @pl.when(turn == 1)
-        def _():
-            for block in range(row_blocks):
-                rows = slice(block * ROWS, (block + 1) * ROWS)
-                slope[rows, :] = jnp.transpose(flip[:, rows].astype(f32)).astype(bf16)
+                slope[at, :] = jnp.transpose(flip[:, rows].astype(f32)).astype(bf16)
 
     g_w_box[...] = g_w_box[...] * (1.0 / scale_factor)
     tok_out = []
@@ -973,30 +992,14 @@
     def token_grad(block):
         rows = slice(block * ROWS, (block + 1) * ROWS)
         last_part = jnp.transpose(dot_nn(kept_last[...], flip[:, rows]))
-        total[rows, :] += last_part + dot_nt(slope[rows, :], kept[...])
+        first_part = dot_nt(slope[rows, :], kept[0][...])
+        rest = dot_nt(slope[count + rows.start : count + rows.stop, :], kept[1][...])
+        total[rows, :] += last_part + first_part + rest
         tok_out.append(pltpu.make_async_copy(total.at[rows], g_tok_out.at[rows], io_sem.at[4 + block]))
         tok_out[-1].start()
 
     if comm:
-        g_small[...] = jnp.zeros_like(g_small)
         g_small[:, :HD] = g_w_box[...]
-        share_qkv, share_up, share = widths(width, ff)
-        for row, columns, share_of, order, source in (
-            (0, 3 * width, share_qkv, quad_order, g_b_qkv),
-            (1, ff, share_up, None, g_b_up),
-            (None, width, share, None, g_vectors),
-        ):
-            @pl.loop(0, columns // BLOCK)
-            def _(block):
-                pick, owned, row_of = owner_tables(block * BLOCK, share_of, 256, order)
-                keep = owned if row is None else owned & (row_of == row)
-                wide = 1 if row is not None else 8
-                full = source[:, aligned(block, BLOCK)].reshape(1, wide, BLOCK)
-                spread = jnp.broadcast_to(full, (16, 8, BLOCK)).reshape(128, BLOCK)
-                spread = jnp.where(keep, spread, 0.0)
-                upper = spread.astype(bf16)
-                g_small[:, 128:384] += dot_nt(upper, pick) + dot_nt((spread - upper.astype(f32)).astype(bf16), pick)
-
         sums.sum_cores(0)
         sum_tick(11, (1, 2, 3))
         sum_tick(11, (0,))
@@ -1011,16 +1014,20 @@
         sum_tick(13, (2,))
         sums.sum_column(0)
         token_grad(3)
+        blocks.results_in(0)
+        moves = [copy_in(final.at[PIECE:], final_out.at[PIECE:], 2)]
+        moves[0].start()
         sum_tick(14, (3,))
         sums.sum_end(0)
         for stream in range(STREAMS):
             blocks.summed(stream)
         sums.summed(0)
-        blocks.results_in()
-        sums.results_in()
-        moves = [copy_in(final, final_out, 2), copy_in(small_final, small_out, 3)]
-        for copy in moves:
-            copy.start()
+        blocks.results_in(1)
+        moves.append(copy_in(final.at[:PIECE], final_out.at[:PIECE], 3))
+        moves[1].start()
+        sums.results_in(1)
+        moves.append(copy_in(small_final, small_out, 8))
+        moves[2].start()
         for copy in moves:
             copy.wait()
     else:
@@ -1113,9 +1120,9 @@
             vmem((8, SMALL), f32),
             pltpu.SemaphoreType.REGULAR((2,)),
             *[vmem(value.shape, f32) for value in little],
-            dma((STREAMS, 4)), dma((STREAMS, 2)), dma((STREAMS, 4)), dma((STREAMS,)), dma((2,)),
+            dma((STREAMS, 4)), dma((STREAMS, 2)), dma((STREAMS, 4)), dma((STREAMS,)), dma((2, 2)),
             dma((1, 4)), dma((1, 2)), dma((1, 4)), dma((1,)),
-            dma((2,)),
+            dma((2, 2)),
         ]
         extra = dict(collective_id=0, has_side_effects=True)
     else:

time: 187 us -> 185 us (0.989)
  Pallas kernels: 186 us -> 184 us
where the time goes in v7:
time: 185 us
  Pallas kernels  184 us (99%)
    pallas_call x1, Pallas kernels, run_layer(): pl.pallas_call(functools.partial(layer_kernel, comm), out_shape=out_shape...  179 us
    pallas_call x1, Pallas kernels, run_finish(): pl.pallas_call(finish_kernel, out_shape=shapes, in_specs=in_hbm(4), out_s...  5.21 us

profile of v7, /device:TPU:0, one launch (start us, length us, event | category | flops | bytes accessed | tf_op | source)
XLA Modules:
  0.0 184.8 jit_solution(11701133153635076076)
XLA Ops:
  0.7 178.8 %layer.1 = (bf16[1024,768]{1,0:T(8,128)(2,1)}, f32[1024,768]{1,0:T(8,128)}, bf16[24,512,512]{2,1,0:T(8,128)(2,1)}, f32[576,768]{1,0:T(8,128)}, f32[8,512]{1,0:T(8,128)}) custom-call(bf16[1024,768]{1,0:T(8,128)(2,1)} %refs_0_.1, bf16[1024,768]{1,0:T(8,128)(2,1)} %refs_1_.1, s32[4,1024]{1,0:T(4,128)} %refs_2_.1, s32[1,1024]{1,0:T(1,128)} %bitcast.17, ...), custom_call_target="tpu_custom_call" | custom-call | tf_op jit(solution)/shard_map/layer/pallas_call | solution.py:1130
  179.4 5.2 %finish.1 = (bf16[1024,768]{1,0:T(8,128)(2,1)}, f32[1024,768]{1,0:T(8,128)}, f32[48,2304]{1,0:T(8,128)}, f32[48,768]{1,0:T(8,128)}, f32[48,3072]{1,0:T(8,128)}, ...) custom-call(bf16[1024,768]{1,0:T(8,128)(2,1)} %get-tuple-element.34., ...), custom_call_target="tpu_custom_call" | custom-call | tf_op jit(solution)/shard_map/finish/pallas_call | solution.py:1197

commit v8 on v7

--- a/solution.py
+++ b/solution.py
@@ -86,7 +86,7 @@
 SMALL = 512
 STREAMS = 12
 VECTORS = 6
-LEVEL_FIRST = 7
+LEVEL_FIRST = 11
 
 
 def widths(width, ff):
@@ -760,6 +760,7 @@
         unit = center * invdev
         grad = cot[rows, :].astype(f32)
         cot[rows, :] = (unit * gain_two + shift_two).astype(bf16)
+        pltpu.make_async_copy(cot.at[rows], layer_out.at[rows], io_sem.at[0]).start()
         scaled = grad * gain_two
         g_pre = invdev * (scaled - row_mean(scaled) - unit * row_mean(scaled * unit))
         total[rows, :] = g_pre
@@ -770,7 +771,6 @@
         g_vectors[7:8, :] += column_sum(grad)
 
     out_copy = pltpu.make_async_copy(cot, layer_out, io_sem.at[0])
-    out_copy.start()
     if comm:
         for stream in range(STREAMS):
             blocks.gather_sent(stream)
@@ -796,15 +796,18 @@
             else:
                 pl.when((at >= 0) & (at < STREAMS))(functools.partial(acts[behind], last(at)))
 
-    def meet(sem):
+    def tell(sem):
         if comm:
             for peer, core in route.peers():
                 pl.semaphore_signal(sem, inc=1, device_id=(peer, core), device_id_type=pl.DeviceIdType.MESH)
+
+    def told(sem):
+        if comm:
             pl.semaphore_wait(sem, 6)
 
     out_copy.wait()
     if comm:
-        meet(mid_sem.at[0])
+        tell(mid_sem.at[0])
 
     @pl.loop(0, up_blocks)
     def _(index):
@@ -825,6 +828,8 @@
         for part in range(2):
             at = pl.ds(pl.multiple_of(up_at + block * BLOCK + part * HALF, HALF), HALF)
             held[at, :] = dot_nn(flip[part * HALF : (part + 1) * HALF, :], g_up).astype(bf16)
+        if comm:
+            pl.when(index == 0)(lambda: told(mid_sem.at[0]))
         sum_start(index)
         for part in range(2):
             at = pl.ds(pl.multiple_of(down_at + block * BLOCK + part * HALF, HALF), HALF)
@@ -832,10 +837,14 @@
             held[at, :] = grads.astype(bf16)
 
     if comm:
-        meet(mid_sem.at[1])
+        tell(mid_sem.at[1])
     sum_tick(3)
+    if comm:
+        told(mid_sem.at[1])
     for step in range(up_blocks):
         sum_start(up_blocks + step)
+    for head in range(2):
+        e_copy(0, head, (quads - 1) * quad_steps * 2 + head, False).start()
 
     @pl.loop(0, row_blocks)
     def _(block):
@@ -888,7 +897,6 @@
         for head in range(2):
             e_copy(order % 2, head, e_step(order) * 2 + head, False).start()
 
-    fetch(0)
     ones = jnp.ones((16, count), bf16)
 
     def attend_back(order):

time: 185 us -> 183 us (0.989)
  Pallas kernels: 184 us -> 182 us
    pallas_call x1, Pallas kernels: 179 us -> 176 us  [run_layer(): pl.pallas_call(functools.partial(layer_kernel, comm), out_shape=out_shape...]
where the time goes in v8:
time: 183 us; the launch traced here: 182 us
  Pallas kernels  182 us (99%)
    pallas_call x1, Pallas kernels, run_layer(): pl.pallas_call(functools.partial(layer_kernel, comm), out_shape=out_shape...  176 us
    pallas_call x1, Pallas kernels, run_finish(): pl.pallas_call(finish_kernel, out_shape=shapes, in_specs=in_hbm(4), out_s...  5.21 us

profile of v8, /device:TPU:0, one launch (start us, length us, event | category | flops | bytes accessed | tf_op | source)
XLA Modules:
  0.0 182.4 jit_solution(16732251561851390713)
XLA Ops:
  0.7 176.3 %layer.1 = (bf16[1024,768]{1,0:T(8,128)(2,1)}, f32[1024,768]{1,0:T(8,128)}, bf16[24,512,512]{2,1,0:T(8,128)(2,1)}, f32[576,768]{1,0:T(8,128)}, f32[8,512]{1,0:T(8,128)}) custom-call(bf16[1024,768]{1,0:T(8,128)(2,1)} %refs_0_.1, bf16[1024,768]{1,0:T(8,128)(2,1)} %refs_1_.1, s32[4,1024]{1,0:T(4,128)} %refs_2_.1, s32[1,1024]{1,0:T(1,128)} %bitcast.17, ...), custom_call_target="tpu_custom_call" | custom-call | tf_op jit(solution)/shard_map/layer/pallas_call | solution.py:1138
  177.0 5.2 %finish.1 = (bf16[1024,768]{1,0:T(8,128)(2,1)}, f32[1024,768]{1,0:T(8,128)}, f32[48,2304]{1,0:T(8,128)}, f32[48,768]{1,0:T(8,128)}, f32[48,3072]{1,0:T(8,128)}, ...) custom-call(bf16[1024,768]{1,0:T(8,128)(2,1)} %get-tuple-element.34., ...), custom_call_target="tpu_custom_call" | custom-call | tf_op jit(solution)/shard_map/finish/pallas_call | solution.py:1205

commit v9 on v8

--- a/solution.py
+++ b/solution.py
@@ -708,8 +708,8 @@
     def column_sum(value):
         return jnp.sum(value, axis=0, keepdims=True)
 
+    gather_tick(6)
     need(3)
-    gather_tick(6)
 
     @pl.loop(0, row_blocks)
     def _(block):

time: 183 us -> 183 us (level)
  no operation moved by 1% of the time
where the time goes in v9:
time: 183 us; the launch traced here: 182 us
  Pallas kernels  182 us (99%)
    pallas_call x1, Pallas kernels, run_layer(): pl.pallas_call(functools.partial(layer_kernel, comm), out_shape=out_shape...  176 us
    pallas_call x1, Pallas kernels, run_finish(): pl.pallas_call(finish_kernel, out_shape=shapes, in_specs=in_hbm(4), out_s...  5.21 us

profile of v9, /device:TPU:0, one launch (start us, length us, event | category | flops | bytes accessed | tf_op | source)
XLA Modules:
  0.0 182.4 jit_solution(4422863330371301296)
XLA Ops:
  0.7 176.3 %layer.1 = (bf16[1024,768]{1,0:T(8,128)(2,1)}, f32[1024,768]{1,0:T(8,128)}, bf16[24,512,512]{2,1,0:T(8,128)(2,1)}, f32[576,768]{1,0:T(8,128)}, f32[8,512]{1,0:T(8,128)}) custom-call(bf16[1024,768]{1,0:T(8,128)(2,1)} %refs_0_.1, bf16[1024,768]{1,0:T(8,128)(2,1)} %refs_1_.1, s32[4,1024]{1,0:T(4,128)} %refs_2_.1, s32[1,1024]{1,0:T(1,128)} %bitcast.17, ...), custom_call_target="tpu_custom_call" | custom-call | tf_op jit(solution)/shard_map/layer/pallas_call | solution.py:1138
  177.0 5.2 %finish.1 = (bf16[1024,768]{1,0:T(8,128)(2,1)}, f32[1024,768]{1,0:T(8,128)}, f32[48,2304]{1,0:T(8,128)}, f32[48,768]{1,0:T(8,128)}, f32[48,3072]{1,0:T(8,128)}, ...) custom-call(bf16[1024,768]{1,0:T(8,128)(2,1)} %get-tuple-element.34., ...), custom_call_target="tpu_custom_call" | custom-call | tf_op jit(solution)/shard_map/finish/pallas_call | solution.py:1205
